TPU v7x, 512 devices: a whole 4x4x16 slice. The times are simulated.
512 devices in a mesh: row: 16 (over z), col: 16 (over y, x), rep: 2 (over core).
Axes of the slice: x: 4, y: 4, z: 16, core: 2. Of those that a mesh axis runs over, the one named last changes fastest.
Arguments:
- tokens: bfloat16 [512, 4096], P(('col', 'rep'), 'row'), may hold values from -6 to 6
- grad_out: bfloat16 [512, 4096], P(('col', 'rep'), 'row'), may hold values from -2.5 to 2.5
- gate_weight: bfloat16 [4096, 14336], P('row', 'col'), may hold values from -0.09375 to 0.09375
- up_weight: bfloat16 [4096, 14336], P('row', 'col'), may hold values from -0.09375 to 0.09375
- down_weight: bfloat16 [14336, 4096], P('col', 'row'), may hold values from -0.046875 to 0.046875
- gate_keep: int32 [32, 112], P('row', 'col'), may hold values from 0 to 1, as said below
- up_keep: int32 [32, 112], P('row', 'col'), may hold values from 0 to 1, as said below
- down_keep: int32 [112, 32], P('col', 'row'), may hold values from 0 to 1, as said below
Outputs:
- mixed: bfloat16 [512, 4096], P(('col', 'rep'), 'row')
- input_grad: bfloat16 [512, 4096], P(('col', 'rep'), 'row')
- gate_weight_grad: bfloat16 [4096, 14336], P('row', 'col')
- up_weight_grad: bfloat16 [4096, 14336], P('row', 'col')
- down_weight_grad: bfloat16 [14336, 4096], P('col', 'row')
Inputs may be any that keep to these rules, and one draw needn't show every extreme that they name: `gate_keep`: 1 keeps the 128 x 128 block of the gate projection, 0 prunes it; the kept share differs from one device's region to the next. `up_keep`: 1 keeps the 128 x 128 block of the up projection, 0 prunes it; the kept share differs from one device's region to the next. `down_keep`: 1 keeps the 128 x 128 block of the down projection, 0 prunes it; the kept share differs from one device's region to the next.
All inputs are finite; a program needn't handle non-finite values.
Results may differ from a plain program's by a relative error of at most 0.025.
Values may be sent and summed in bfloat16 or wider, within the bound.
No kernel may reach another device: no remote copies, remote signals or barrier semaphores. Data moves between devices by JAX's collectives and lax.ppermute only.
A program may use at most 64 MiB of HBM per device.

v0:
```python
import jax
import jax.numpy as jnp
from jax import lax
from jax.sharding import PartitionSpec as P

PLAIN = (((1,), (0,)), ((), ()))
FLIPPED = (((1,), (1,)), ((), ()))
OVER_ROWS = (((0,), (0,)), ((), ()))


def masked(weight, keep):
    rows, cols = keep.shape
    tiled = weight.reshape(rows, weight.shape[0] // rows, cols, weight.shape[1] // cols)
    return (tiled * keep[:, None, :, None].astype(weight.dtype)).reshape(weight.shape)


def product(left, weight, flipped):
    return lax.dot_general(
        left, weight, FLIPPED if flipped else PLAIN, preferred_element_type=jnp.float32
    )


def swiglu_grads(back, gate_value, gate_sig, up_value):
    gate_grad = (back * up_value * gate_sig * (1.0 + gate_value * (1.0 - gate_sig))).astype(
        jnp.bfloat16
    )
    up_grad = (back * gate_value * gate_sig).astype(jnp.bfloat16)
    return (gate_grad, up_grad)


def per_device(
    tokens, grad_out, gate_weight, up_weight, down_weight, gate_keep, up_keep, down_keep
):
    model_block = tokens.shape[1]
    gate_used = masked(gate_weight, gate_keep)
    up_used = masked(up_weight, up_keep)
    down_used = masked(down_weight, down_keep)
    token_panel, grad_panel = (
        lax.all_gather(tokens, "col", axis=0, tiled=True),
        lax.all_gather(grad_out, "col", axis=0, tiled=True),
    )
    gate_part = product(token_panel, gate_used, False)
    up_part = product(token_panel, up_used, False)
    gate_sum, up_sum = (
        lax.psum(gate_part.astype(jnp.bfloat16), "row").astype(jnp.float32),
        lax.psum(up_part.astype(jnp.bfloat16), "row").astype(jnp.float32),
    )
    gate_sig = jax.nn.sigmoid(gate_sum)
    hidden = (gate_sum * gate_sig * up_sum).astype(jnp.bfloat16)
    back_part = product(grad_panel, down_used, True)
    back_sum = lax.psum(back_part.astype(jnp.bfloat16), "row").astype(jnp.float32)
    gate_grad, up_grad = swiglu_grads(back_sum, gate_sum, gate_sig, up_sum)
    gate_term = masked(
        lax.dot_general(token_panel, gate_grad, OVER_ROWS, preferred_element_type=jnp.float32),
        gate_keep,
    )
    up_term = masked(
        lax.dot_general(token_panel, up_grad, OVER_ROWS, preferred_element_type=jnp.float32),
        up_keep,
    )
    down_term = masked(
        lax.dot_general(hidden, grad_panel, OVER_ROWS, preferred_element_type=jnp.float32),
        down_keep,
    )
    gate_total, up_total, down_total = (
        lax.psum(gate_term.astype(jnp.bfloat16), "rep").astype(jnp.float32),
        lax.psum(up_term.astype(jnp.bfloat16), "rep").astype(jnp.float32),
        lax.psum(down_term.astype(jnp.bfloat16), "rep").astype(jnp.float32),
    )
    forward = product(hidden, down_used, False)
    backward = product(gate_grad, gate_used, True) + product(up_grad, up_used, True)
    combined = lax.psum_scatter(
        jnp.concatenate([forward, backward], axis=1).astype(jnp.bfloat16),
        "col",
        scatter_dimension=0,
        tiled=True,
    ).astype(jnp.float32)
    mixed = combined[:, :model_block].astype(jnp.bfloat16)
    input_grad = combined[:, model_block:].astype(jnp.bfloat16)
    return (
        mixed,
        input_grad,
        gate_total.astype(jnp.bfloat16),
        up_total.astype(jnp.bfloat16),
        down_total.astype(jnp.bfloat16),
    )


def solution(mesh):
    return jax.shard_map(
        per_device,
        mesh=mesh,
        in_specs=(
            P(("col", "rep"), "row"),
            P(("col", "rep"), "row"),
            P("row", "col"),
            P("row", "col"),
            P("col", "row"),
            P("row", "col"),
            P("row", "col"),
            P("col", "row"),
        ),
        out_specs=(
            P(("col", "rep"), "row"),
            P(("col", "rep"), "row"),
            P("row", "col"),
            P("row", "col"),
            P("col", "row"),
        ),
        check_vma=False,
    )
```

profile of v0, /device:TPU:1, one launch (start us, length us, event | category | flops | bytes accessed | tf_op | source)
XLA Modules:
  0.0 352.1 jit_solution(348218787414217468)
XLA Ops:
  7.2 19.6 %all_gather.6 = bf16[256,256]{1,0:T(8,128)(2,1)S(1)} all-gather(bf16[16,256]{1,0:T(8,128)(2,1)} %param.8), channel_id=1, replica_groups=mesh['row'=16,'col'=16,'rep'=2] {'col'}, dimensions={0}, use_global_device_ids=true | all-gather | bytes 139264 | tf_op jit(solution)/shard_map/all_gather | solution.py:39
  26.9 1.3 copy.36
  28.3 17.7 %all_gather.7 = bf16[256,256]{1,0:T(8,128)(2,1)S(1)} all-gather(bf16[16,256]{1,0:T(8,128)(2,1)S(1)} %copy-done.8), channel_id=1, replica_groups=mesh['row'=16,'col'=16,'rep'=2] {'col'}, dimensions={0}, use_global_device_ids=true | all-gather | bytes 139264 | tf_op jit(solution)/shard_map/all_gather | solution.py:40
  46.1 0.2 copy.34
  46.4 0.5 copy-done.11
  46.8 0.1 copy.33
  46.9 0.3 mul.94
  47.2 1.1 fusion.6
  48.3 0.3 mul.90
  48.7 1.1 fusion.5
  49.7 0.3 mul.98
  50.0 0.7 copy-done.7
  50.8 1.1 fusion.7
  52.2 144.1 %all-reduce.5.cloned.1.call-done = (bf16[256,896]{0,1:T(8,128)(2,1)}, bf16[256,896]{0,1:T(8,128)(2,1)}, bf16[256,896]{0,1:T(8,128)(2,1)}) async-done(((bf16[256,896]{0,1:T(8,128)(2,1)}, bf16[256,896]{0,1:T(8,128)(2,1)}, bf16[256,896]{0,1:T(8,128)(2,1)}), (bf16[256,896]{0,1:T(8,128)(2,1)}, bf16[256,896]{0,1:T(8,128)(2,1)}, bf16[256,896]{0,1:T(8,128)(2,1)})) %all-reduce.5.cloned.1.call-update) | async-done | bytes 1376272 | tf_op jit(solution)/shard_map/psum | solution.py:46
  196.3 2.0 convolution_convert_fusion.3
  198.3 0.4 fusion.12
  198.8 0.4 fusion.19
  199.1 0.6 fusion.8
  199.8 0.8 copy.45
  200.7 0.3 mul.110
  201.0 0.7 copy-done.3
  201.6 1.2 fusion.3
  202.8 0.3 mul.107
  203.1 1.1 fusion.4
  204.2 0.3 mul.113
  204.5 1.2 fusion.2
  205.7 88.4 %reduce-scatter.4.cloned.1.call-done = bf16[16,512]{1,0:T(8,128)(2,1)} async-done(((bf16[256,512]{1,0:T(8,128)(2,1)}), bf16[16,512]{1,0:T(8,128)(2,1)}) %reduce-scatter.4.cloned.1.call-update) | async-done | bytes 16400
  294.1 1.3 fusion.24
  295.5 46.3 %all-reduce.7.cloned.1.call-done = (bf16[256,896]{0,1:T(8,128)(2,1)}, bf16[256,896]{0,1:T(8,128)(2,1)}, bf16[896,256]{1,0:T(8,128)(2,1)}) async-done(((bf16[256,896]{0,1:T(8,128)(2,1)}, bf16[256,896]{0,1:T(8,128)(2,1)}, bf16[896,256]{1,0:T(8,128)(2,1)}), (bf16[256,896]{0,1:T(8,128)(2,1)}, bf16[256,896]{0,1:T(8,128)(2,1)}, bf16[896,256]{1,0:T(8,128)(2,1)})) %all-reduce.7.cloned.1.call-update) | async-done | bytes 1376272 | tf_op jit(solution)/shard_map/psum | solution.py:66
  341.8 2.0 copy.43
  343.8 1.0 copy.44
  344.8 0.8 copy.73
  (36 shorter events, 0.8 us)
Async XLA Ops:
  7.2 189.1 %all-reduce.5.cloned.1.call-start = ((), (), s32[]{:S(2)}) async-start(), calls=%async_computation.2 | async-start | bytes 2752512 | tf_op jit(solution)/shard_map/psum | solution.py:46
  26.8 1.3 copy-start.9
  26.9 1.4 copy-start.8
  26.9 19.3 %copy-start.4 = (bf16[256,896]{1,0:T(8,128)(2,1)S(1)}, bf16[256,896]{1,0:T(8,128)(2,1)}, u32[]{:S(2)}) copy-start(bf16[256,896]{1,0:T(8,128)(2,1)} %param.10) | copy-start | bytes 1376260
  28.3 17.7 %copy-start.10 = (s32[7,2]{0,1:T(2,128)S(1)}, s32[7,2]{0,1:T(2,128)}, u32[]{:S(2)}) copy-start(s32[7,2]{0,1:T(2,128)} %param.15) | copy-start | bytes 172
  46.1 0.7 copy-start.11
  49.7 1.0 copy-start.7
  51.9 242.3 %reduce-scatter.4.cloned.1.call-start = ((), (), s32[]{:S(2)}) async-start(), calls=%async_computation.1 | async-start | bytes 278528
  196.3 2.0 copy-start
  196.3 2.0 copy-start.1
  196.3 2.0 copy-start.2
  200.6 1.0 copy-start.3
  200.6 141.1 %all-reduce.7.cloned.1.call-start = ((), (), s32[]{:S(2)}) async-start(), calls=%async_computation.3 | async-start | bytes 2752512 | tf_op jit(solution)/shard_map/psum | solution.py:66
  341.8 2.0 copy-start.6
  343.8 1.0 copy-start.5
Sparse Core Ops, SparseCore 0:
  52.0 144.2 all-reduce.4
  200.7 93.3 reduce-scatter.3
  297.8 43.9 all-reduce.6
where the time goes:
time: 353 us; the launch traced here: 352 us
  waiting for transfers between devices  279 us (79%)
  blocking collectives  37.4 us (11%)
  between operations  13.9 us (4%)
  local copies, waits for them, and re-layouts  11.7 us (3%)
  matrix products  9.67 us (3%)
    psum x1, waiting for transfers between devices, per_device(): lax.psum(up_part.astype(jnp.bfloat16), 'row').astype(jnp.float32)  144 us
    unnamed x4, waiting for transfers between devices  88.5 us
    psum x1, waiting for transfers between devices, per_device(): lax.psum(gate_term.astype(jnp.bfloat16), 'rep').astype(jnp.float32)  46.3 us
    all_gather x1, blocking collectives, per_device(): lax.all_gather(tokens, 'col', axis=0, tiled=True)  19.6 us
    all_gather x1, blocking collectives, per_device(): lax.all_gather(grad_out, 'col', axis=0, tiled=True)  17.7 us
    unnamed x30, local copies, waits for them, and re-layouts  8.01 us
  transfers between devices with their start and end apart: 3, of which 3 were waited for; matrix products, arithmetic and copies ran while one was open for 2% of the time, Pallas kernels for 0%

commit v1 on v0

v1 whole, which is shorter than its diff:
```python
import jax
import jax.numpy as jnp
from jax import lax
from jax.experimental import pallas as pl
from jax.experimental.pallas import tpu as pltpu
from jax.sharding import PartitionSpec as P

BF16 = jnp.bfloat16
F32 = jnp.float32
PLAIN = (((1,), (0,)), ((), ()))
FLIPPED = (((1,), (1,)), ((), ()))
OVER_ROWS = (((0,), (0,)), ((), ()))


def dot(left, right, dims):
    return lax.dot_general(left, right, dims, preferred_element_type=F32)


def prune(source, keep, target):
    rows, cols = keep.shape
    height, width = source.shape[0] // rows, source.shape[1] // cols
    for a in range(rows):
        for b in range(cols):
            block = (pl.ds(a * height, height), pl.ds(b * width, width))
            value = source[block]
            target[block] = jnp.where(keep[a, b] != 0, value, jnp.zeros_like(value))


def forward_body(panel, gate, up, down, gate_keep, up_keep, down_keep, part, gate_eff, up_eff, down_eff):
    model = gate.shape[0]
    hidden = gate.shape[1]
    prune(gate, gate_keep, gate_eff)
    prune(up, up_keep, up_eff)
    prune(down, down_keep, down_eff)
    tokens = panel[:, :model]
    grads = panel[:, model:]
    part[:, :hidden] = dot(tokens, gate_eff[...], PLAIN).astype(BF16)
    part[:, hidden : 2 * hidden] = dot(tokens, up_eff[...], PLAIN).astype(BF16)
    part[:, 2 * hidden :] = dot(grads, down_eff[...], FLIPPED).astype(BF16)


def pointwise_body(parts, out):
    width = parts.shape[2] // 3
    total = jnp.sum(parts[...].astype(F32), axis=0)
    gate = total[:, :width]
    up = total[:, width : 2 * width]
    back = total[:, 2 * width :]
    sig = jax.nn.sigmoid(gate)
    hidden = (gate * sig * up).astype(BF16)
    gate_grad = (back * up * sig * (1.0 + gate * (1.0 - sig))).astype(BF16)
    up_grad = (back * gate * sig).astype(BF16)
    for copy in range(out.shape[0]):
        out[copy, :, :width] = hidden
        out[copy, :, width : 2 * width] = gate_grad
        out[copy, :, 2 * width :] = up_grad


def outputs_body(mid, gate_eff, up_eff, down_eff, out):
    width = gate_eff.shape[1]
    model = gate_eff.shape[0]
    out[:, :model] = dot(mid[:, :width], down_eff[...], PLAIN).astype(BF16)
    out[:, model:] = (
        dot(mid[:, width : 2 * width], gate_eff[...], FLIPPED)
        + dot(mid[:, 2 * width :], up_eff[...], FLIPPED)
    ).astype(BF16)


def weights_body(panel, mid, gate_keep, up_keep, down_keep, gate_out, up_out, down_out, wide, tall):
    model = gate_out.shape[0]
    width = gate_out.shape[1]
    tokens = panel[:, :model]
    wide[...] = dot(tokens, mid[:, width : 2 * width], OVER_ROWS).astype(BF16)
    prune(wide, gate_keep, gate_out)
    wide[...] = dot(tokens, mid[:, 2 * width :], OVER_ROWS).astype(BF16)
    prune(wide, up_keep, up_out)
    tall[...] = dot(mid[:, :width], panel[:, model:], OVER_ROWS).astype(BF16)
    prune(tall, down_keep, down_out)


def reduce_body(parts, mixed, input_grad):
    model = mixed.shape[1]
    total = jnp.sum(parts[...].astype(F32), axis=0)
    mixed[...] = total[:, :model].astype(BF16)
    input_grad[...] = total[:, model:].astype(BF16)


VMEM = pl.BlockSpec(memory_space=pltpu.VMEM)
SMEM = pl.BlockSpec(memory_space=pltpu.SMEM)


def shape(*dims):
    return jax.ShapeDtypeStruct(dims, BF16)


def call(body, ins, outs, scratch=()):
    return pl.pallas_call(
        body,
        in_specs=ins,
        out_specs=[VMEM] * len(outs),
        out_shape=list(outs),
        scratch_shapes=list(scratch),
    )


def per_device(tokens, grad_out, gate_weight, up_weight, down_weight, gate_keep, up_keep, down_keep):
    rows = lax.axis_size("row")
    cols = lax.axis_size("col")
    block, model = tokens.shape
    width = gate_weight.shape[1]
    held = cols * block
    joined = jnp.concatenate([tokens, grad_out], axis=1)
    panel = lax.all_to_all(
        jnp.broadcast_to(joined[None], (cols, block, 2 * model)), "col", 0, 0
    ).reshape(held, 2 * model)
    part, gate_eff, up_eff, down_eff = call(
        forward_body,
        [VMEM] * 4 + [SMEM] * 3,
        [shape(held, 3 * width), shape(model, width), shape(model, width), shape(width, model)],
    )(panel, gate_weight, up_weight, down_weight, gate_keep, up_keep, down_keep)
    share = held // rows
    parts = lax.all_to_all(part.reshape(rows, share, 3 * width), "row", 0, 0)
    (spread,) = call(pointwise_body, [VMEM], [shape(rows, share, 3 * width)])(parts)
    mid = lax.all_to_all(spread, "row", 0, 0).reshape(held, 3 * width)
    own = call(
        weights_body,
        [VMEM] * 2 + [SMEM] * 3,
        [shape(model, width), shape(model, width), shape(width, model)],
        [pltpu.VMEM((model, width), BF16), pltpu.VMEM((width, model), BF16)],
    )(panel, mid, gate_keep, up_keep, down_keep)
    swap = [(0, 1), (1, 0)]
    other = [lax.ppermute(term, "rep", swap) for term in own]
    (out,) = call(outputs_body, [VMEM] * 4, [shape(held, 2 * model)])(
        mid, gate_eff, up_eff, down_eff
    )
    pieces = lax.all_to_all(out.reshape(cols, block, 2 * model), "col", 0, 0)
    mixed, input_grad = call(reduce_body, [VMEM], [shape(block, model)] * 2)(pieces)
    totals = [
        (mine.astype(F32) + theirs.astype(F32)).astype(BF16) for mine, theirs in zip(own, other)
    ]
    return (mixed, input_grad, *totals)


def solution(mesh):
    return jax.shard_map(
        per_device,
        mesh=mesh,
        in_specs=(
            P(("col", "rep"), "row"),
            P(("col", "rep"), "row"),
            P("row", "col"),
            P("row", "col"),
            P("col", "row"),
            P("row", "col"),
            P("row", "col"),
            P("col", "row"),
        ),
        out_specs=(
            P(("col", "rep"), "row"),
            P(("col", "rep"), "row"),
            P("row", "col"),
            P("row", "col"),
            P("col", "row"),
        ),
        check_vma=False,
    )
```

time: 353 us -> 203 us (0.58)
  waiting for transfers between devices: 279 us -> 10.5 us
  blocking collectives: 37.4 us -> 146 us
  starting transfers between devices: 0.12 us -> 24.6 us
  Pallas kernels: 0 us -> 14 us
  between operations: 13.9 us -> 0.72 us
  matrix products: 9.67 us -> 0 us
  local copies, waits for them, and re-layouts: 11.7 us -> 3.52 us
    psum x2 -> x0, waiting for transfers between devices: 190 us -> none  [the longest x1 144 us: per_device(): lax.psum(up_part.astype(jnp.bfloat16), 'row').astype(jnp.float32)]
    all_to_all x0 -> x2, blocking collectives: none -> 146 us  [the longest x1 74.3 us: per_device(): parts = lax.all_to_all(part.reshape(rows, share, 3 * width), 'row', 0, 0)]
    unnamed x4 -> x0, waiting for transfers between devices: 88.5 us -> none
    all_gather x2 -> x0, blocking collectives: 37.4 us -> none  [the longest x1 19.6 us: per_device(): lax.all_gather(tokens, 'col', axis=0, tiled=True)]
    pallas_call x0 -> x5, Pallas kernels: none -> 14 us  [the longest x1 3.42 us: per_device(): call(forward_body, [VMEM] * 4 + [SMEM] * 3, [shape(held, 3 * width), shap...]
    ppermute x0 -> x3, starting transfers between devices: none -> 13.1 us  [per_device(): other = [lax.ppermute(term, 'rep', swap) for term in own]]
    all_to_all x0 -> x2, starting transfers between devices: none -> 11.5 us  [the longest x1 7.57 us: per_device(): lax.all_to_all(jnp.broadcast_to(joined[None], (cols, block, 2 * model)),...]
    all_to_all x0 -> x2, waiting for transfers between devices: none -> 10.5 us  [the longest x1 6.34 us: per_device(): lax.all_to_all(jnp.broadcast_to(joined[None], (cols, block, 2 * model)),...]
  transfers between devices with their start and end apart: 3 -> 5, of which waited for: 3 -> 2; matrix products, arithmetic and copies ran while one was open for 2% -> 2% of each run, Pallas kernels for 0% -> 2%
where the time goes in v1:
time: 203 us
  blocking collectives  146 us (72%)
  starting transfers between devices  24.6 us (12%)
  Pallas kernels  14 us (7%)
  waiting for transfers between devices  10.5 us (5%)
  local copies, waits for them, and re-layouts  3.52 us (2%)
  other arithmetic  3.35 us (2%)
    all_to_all x1, blocking collectives, per_device(): parts = lax.all_to_all(part.reshape(rows, share, 3 * width), 'row', 0, 0)  74.3 us
    all_to_all x1, blocking collectives, per_device(): mid = lax.all_to_all(spread, 'row', 0, 0).reshape(held, 3 * width)  71.6 us
    ppermute x3, starting transfers between devices, per_device(): other = [lax.ppermute(term, 'rep', swap) for term in own]  13.1 us
    all_to_all x1, starting transfers between devices, per_device(): lax.all_to_all(jnp.broadcast_to(joined[None], (cols, block, 2 * model)),...  7.57 us
    all_to_all x1, waiting for transfers between devices, per_device(): lax.all_to_all(jnp.broadcast_to(joined[None], (cols, block, 2 * model)),...  6.34 us
    all_to_all x1, waiting for transfers between devices, per_device(): pieces = lax.all_to_all(out.reshape(cols, block, 2 * model), 'col', 0, 0)  4.12 us
  transfers between devices with their start and end apart: 5, of which 2 were waited for; matrix products, arithmetic and copies ran while one was open for 2% of the time, Pallas kernels for 2%

profile of v1, /device:TPU:1, one launch (start us, length us, event | category | flops | bytes accessed | tf_op | source)
XLA Modules:
  0.0 202.6 jit_solution(18371691230186174886)
XLA Ops:
  0.6 0.7 pad_maximum_fusion
  1.3 0.7 broadcast_in_dim.2
  2.1 7.6 %all-to-all-start = ((bf16[16,16,512]{2,1,0:T(8,128)(2,1)}), bf16[16,16,512]{2,1,0:T(8,128)(2,1)S(1)}, u32[]{:S(2)}, u32[]{:S(2)}) async-start(bf16[16,16,512]{2,1,0:T(8,128)(2,1)} %broadcast_in_dim.2), calls=%async_computation | async-start | bytes 524288 | tf_op jit(solution)/shard_map/all_to_all | solution.py:112
  9.7 1.4 copy.13.down_keep
  11.0 6.3 %all-to-all-done = bf16[16,16,512]{2,1,0:T(8,128)(2,1)S(1)} async-done(((bf16[16,16,512]{2,1,0:T(8,128)(2,1)}), bf16[16,16,512]{2,1,0:T(8,128)(2,1)S(1)}, u32[]{:S(2)}, u32[]{:S(2)}) %all-to-all-start) | async-done | bytes 262176 | tf_op jit(solution)/shard_map/all_to_all | solution.py:112
  17.4 0.0 copy-start
  17.4 0.7 copy-done
  18.1 3.4 %shard_map.119 = (bf16[256,2688]{1,0:T(8,128)(2,1)}, bf16[256,896]{1,0:T(8,128)(2,1)}, bf16[256,896]{1,0:T(8,128)(2,1)}, bf16[896,256]{1,0:T(8,128)(2,1)}) custom-call(bf16[256,512]{1,0:T(8,128)(2,1)} %bitcast.6, bf16[256,896]{1,0:T(8,128)(2,1)} %gate.1, bf16[256,896]{1,0:T(8,128)(2,1)} %up.1, bf16[896,256]{1,0:T(8,128)(2,1)} %down.1, s32[2,7]{1,0:T(2,128)} %gate_keep.3, ...), custom_call_target="tpu_custom_call" | custom-call | tf_op jit(solution)/shard_map/pallas_call | solution.py:115
  21.5 74.3 %all_to_all.20.parts = bf16[16,16,2688]{2,1,0:T(8,128)(2,1)} all-to-all(bf16[16,16,2688]{2,1,0:T(8,128)(2,1)} %bitcast.8), channel_id=1, replica_groups=mesh['row'=16,'col'=16,'rep'=2] {'row'}, dimensions={0} | all-to-all | bytes 2752512 | tf_op jit(solution)/shard_map/all_to_all | solution.py:121
  95.8 2.7 %shard_map.120 = bf16[16,16,2688]{2,1,0:T(8,128)(2,1)} custom-call(bf16[16,16,2688]{2,1,0:T(8,128)(2,1)} %all_to_all.20.parts), custom_call_target="tpu_custom_call" | custom-call | tf_op jit(solution)/shard_map/pallas_call | solution.py:122
  98.5 71.6 %all_to_all.21 = bf16[16,16,2688]{2,1,0:T(8,128)(2,1)} all-to-all(bf16[16,16,2688]{2,1,0:T(8,128)(2,1)} %shard_map.120), channel_id=1, replica_groups=mesh['row'=16,'col'=16,'rep'=2] {'row'}, dimensions={0} | all-to-all | bytes 2752512 | tf_op jit(solution)/shard_map/all_to_all | solution.py:123
  170.1 3.2 %shard_map.123 = (bf16[256,896]{1,0:T(8,128)(2,1)}, bf16[256,896]{1,0:T(8,128)(2,1)}, bf16[896,256]{1,0:T(8,128)(2,1)}) custom-call(bf16[256,512]{1,0:T(8,128)(2,1)} %bitcast.7, bf16[256,2688]{1,0:T(8,128)(2,1)} %bitcast.4, s32[2,7]{1,0:T(2,128)} %gate_keep.3, s32[2,7]{1,0:T(2,128)} %up_keep.3, s32[7,2]{1,0:T(8,128)} %copy.13.down_keep), custom_call_target="tpu_custom_call" | custom-call | tf_op jit(solution)/shard_map/pallas_call | solution.py:124
  173.3 8.8 %collective-permute-start = (bf16[256,896]{1,0:T(8,128)(2,1)}, bf16[256,896]{1,0:T(8,128)(2,1)S(1)}, u32[]{:S(2)}, u32[]{:S(2)}) collective-permute-start(bf16[256,896]{1,0:T(8,128)(2,1)} %get-tuple-element.20), channel_id=1, source_target_pairs={{0,1},{1,0},{2,3},{3,2},{4,5},{5,4},{6,7},{7,6},{8,9},{9,8},{10,11... | collective-permute-start | bytes 1376264 | tf_op jit(solution)/shard_map/ppermute | solution.py:131
  182.1 0.0 copy-start.3
  182.1 0.0 copy-start.2
  182.1 0.0 copy-start.4
  182.1 3.1 %shard_map.121 = bf16[256,512]{1,0:T(8,128)(2,1)} custom-call(bf16[256,2688]{1,0:T(8,128)(2,1)} %bitcast.5, bf16[256,896]{1,0:T(8,128)(2,1)} %get-tuple-element.15.gate_eff, bf16[256,896]{1,0:T(8,128)(2,1)} %get-tuple-element.16.up_eff, bf16[896,256]{1,0:T(8,128)(2,1)} %get-tuple-element.17.down_eff), custom_call_target="tpu_custom_call" | custom-call | tf_op jit(solution)/shard_map/pallas_call | solution.py:132
  185.2 4.0 %all-to-all-start.3 = ((bf16[16,16,512]{2,1,0:T(8,128)(2,1)}), bf16[16,16,512]{2,1,0:T(8,128)(2,1)S(1)}, u32[]{:S(2)}, u32[]{:S(2)}) async-start(bf16[16,16,512]{2,1,0:T(8,128)(2,1)} %bitcast.9), calls=%async_computation.3 | async-start | bytes 524288 | tf_op jit(solution)/shard_map/all_to_all | solution.py:135
  189.2 0.0 copy-done.3
  189.2 2.2 %collective-permute-start.1 = (bf16[256,896]{1,0:T(8,128)(2,1)S(1)}, bf16[256,896]{1,0:T(8,128)(2,1)S(1)}, u32[]{:S(2)}, u32[]{:S(2)}) collective-permute-start(bf16[256,896]{1,0:T(8,128)(2,1)S(1)} %copy-done.3), channel_id=1, source_target_pairs={{0,1},{1,0},{2,3},{3,2},{4,5},{5,4},{6,7},{7,6},{8,9},{9,8},{10,11... | collective-permute-start | bytes 1376264 | tf_op jit(solution)/shard_map/ppermute | solution.py:131
  191.4 0.0 copy-done.2
  191.4 2.1 %collective-permute-start.2 = (bf16[896,256]{1,0:T(8,128)(2,1)S(1)}, bf16[896,256]{1,0:T(8,128)(2,1)S(1)}, u32[]{:S(2)}, u32[]{:S(2)}) collective-permute-start(bf16[896,256]{1,0:T(8,128)(2,1)S(1)} %copy-done.2), channel_id=1, source_target_pairs={{0,1},{1,0},{2,3},{3,2},{4,5},{5,4},{6,7},{7,6},{8,9},{9,8},{10,11... | collective-permute-start | bytes 1376264 | tf_op jit(solution)/shard_map/ppermute | solution.py:131
  193.5 4.1 %all-to-all-done.3.parts = bf16[16,16,512]{2,1,0:T(8,128)(2,1)S(1)} async-done(((bf16[16,16,512]{2,1,0:T(8,128)(2,1)}), bf16[16,16,512]{2,1,0:T(8,128)(2,1)S(1)}, u32[]{:S(2)}, u32[]{:S(2)}) %all-to-all-start.3) | async-done | bytes 262176 | tf_op jit(solution)/shard_map/all_to_all | solution.py:135
  197.7 0.7 copy-done.1
  198.4 1.6 shard_map.122
  200.0 0.0 collective-permute-done
  200.0 0.0 copy-done.4
  200.0 0.9 add_convert_fusion.2
  200.8 0.0 collective-permute-done.1
  200.8 0.9 add_convert_fusion.1
  201.7 0.0 collective-permute-done.2
  201.7 0.9 add_convert_fusion
  (1 shorter events, 0.0 us)
Async XLA Ops:
  2.1 15.3 %all-to-all-start = ((bf16[16,16,512]{2,1,0:T(8,128)(2,1)}), bf16[16,16,512]{2,1,0:T(8,128)(2,1)S(1)}, u32[]{:S(2)}, u32[]{:S(2)}) async-start(bf16[16,16,512]{2,1,0:T(8,128)(2,1)} %broadcast_in_dim.2), calls=%async_computation | async-start | bytes 524288 | tf_op jit(solution)/shard_map/all_to_all | solution.py:112
  17.4 0.7 copy-start
  173.3 26.7 %collective-permute-start = (bf16[256,896]{1,0:T(8,128)(2,1)}, bf16[256,896]{1,0:T(8,128)(2,1)S(1)}, u32[]{:S(2)}, u32[]{:S(2)}) collective-permute-start(bf16[256,896]{1,0:T(8,128)(2,1)} %get-tuple-element.20), channel_id=1, source_target_pairs={{0,1},{1,0},{2,3},{3,2},{4,5},{5,4},{6,7},{7,6},{8,9},{9,8},{10,11... | collective-permute-start | bytes 1376264 | tf_op jit(solution)/shard_map/ppermute | solution.py:131
  182.1 7.1 %copy-start.3 = (bf16[256,896]{1,0:T(8,128)(2,1)S(1)}, bf16[256,896]{1,0:T(8,128)(2,1)}, u32[]{:S(2)}) copy-start(bf16[256,896]{1,0:T(8,128)(2,1)} %get-tuple-element.21) | copy-start | bytes 1376260
  182.1 9.3 %copy-start.2 = (bf16[896,256]{1,0:T(8,128)(2,1)S(1)}, bf16[896,256]{1,0:T(8,128)(2,1)}, u32[]{:S(2)}) copy-start(bf16[896,256]{1,0:T(8,128)(2,1)} %get-tuple-element.22) | copy-start | bytes 1376260
  182.1 17.9 %copy-start.4 = (bf16[256,896]{1,0:T(8,128)(2,1)S(1)}, bf16[256,896]{1,0:T(8,128)(2,1)}, u32[]{:S(2)}) copy-start(bf16[256,896]{1,0:T(8,128)(2,1)} %get-tuple-element.20) | copy-start | bytes 1376260
  185.2 12.4 %all-to-all-start.3 = ((bf16[16,16,512]{2,1,0:T(8,128)(2,1)}), bf16[16,16,512]{2,1,0:T(8,128)(2,1)S(1)}, u32[]{:S(2)}, u32[]{:S(2)}) async-start(bf16[16,16,512]{2,1,0:T(8,128)(2,1)} %bitcast.9), calls=%async_computation.3 | async-start | bytes 524288 | tf_op jit(solution)/shard_map/all_to_all | solution.py:135
  189.2 11.7 %collective-permute-start.1 = (bf16[256,896]{1,0:T(8,128)(2,1)S(1)}, bf16[256,896]{1,0:T(8,128)(2,1)S(1)}, u32[]{:S(2)}, u32[]{:S(2)}) collective-permute-start(bf16[256,896]{1,0:T(8,128)(2,1)S(1)} %copy-done.3), channel_id=1, source_target_pairs={{0,1},{1,0},{2,3},{3,2},{4,5},{5,4},{6,7},{7,6},{8,9},{9,8},{10,11... | collective-permute-start | bytes 1376264 | tf_op jit(solution)/shard_map/ppermute | solution.py:131
  191.4 10.3 %collective-permute-start.2 = (bf16[896,256]{1,0:T(8,128)(2,1)S(1)}, bf16[896,256]{1,0:T(8,128)(2,1)S(1)}, u32[]{:S(2)}, u32[]{:S(2)}) collective-permute-start(bf16[896,256]{1,0:T(8,128)(2,1)S(1)} %copy-done.2), channel_id=1, source_target_pairs={{0,1},{1,0},{2,3},{3,2},{4,5},{5,4},{6,7},{7,6},{8,9},{9,8},{10,11... | collective-permute-start | bytes 1376264 | tf_op jit(solution)/shard_map/ppermute | solution.py:131
  197.7 0.7 copy-start.1

commit v2 on v0

v2 whole, which is shorter than its diff:
```python
import jax
import jax.numpy as jnp
from jax import lax
from jax.experimental import pallas as pl
from jax.experimental.pallas import tpu as pltpu
from jax.sharding import Mesh, PartitionSpec as P


BF16 = jnp.bfloat16
F32 = jnp.float32
PLAIN = (((1,), (0,)), ((), ()))
FLIPPED = (((1,), (1,)), ((), ()))
NEAR = 4
LIMIT = 24 * 1024 * 1024
HALVES = 2
SWAP = [(0, 1), (1, 0)]
VMEM = pl.BlockSpec(memory_space=pltpu.VMEM)
SMEM = pl.BlockSpec(memory_space=pltpu.SMEM)


def dot(left, right, dims):
    return lax.dot_general(left, right, dims, preferred_element_type=F32)


def shape(*dims):
    return jax.ShapeDtypeStruct(dims, BF16)


def call(body, ins, outs, scratch=()):
    return pl.pallas_call(
        body,
        in_specs=ins,
        out_specs=[VMEM] * len(outs),
        out_shape=list(outs),
        scratch_shapes=list(scratch),
        compiler_params=pltpu.CompilerParams(vmem_limit_bytes=LIMIT),
    )


def near(value):
    return pltpu.with_memory_space_constraint(value, pltpu.VMEM)


def local(*dims):
    return pltpu.VMEM(dims, BF16)


def mark_body(rep, out):
    out[0] = rep[0]
    out[1] = rep[1]


def mark(rep):
    return pl.pallas_call(
        mark_body,
        in_specs=[SMEM],
        out_specs=SMEM,
        out_shape=jax.ShapeDtypeStruct((2,), jnp.int32),
    )(rep)


def half_of(index, size):
    return pl.ds(pl.multiple_of(index * size, size), size)


def pick(keep, value):
    return jnp.where(keep != 0, value, jnp.zeros_like(value))


def prepare_body(place_of, gate, up, down, gate_keep, up_keep, down_keep, *refs):
    *outs, full, rows, tall = refs
    out = full
    part, own = place_of[0], place_of[1]
    size = rows.shape[0]
    blocks = gate_keep.shape[1]
    span = rows.shape[1] // blocks
    units = out.shape[1] // 3
    for place, source, keep in ((0, gate, gate_keep), (1, up, up_keep)):
        value = source[half_of(part, size), :]
        for b in range(blocks):
            rows[:, b * span : (b + 1) * span] = pick(keep[part, b], value[:, b * span : (b + 1) * span])
        turned = rows[...].T
        for b in range(out.shape[0]):
            out[b, place * units : (place + 1) * units, :] = turned[b * units : (b + 1) * units]
    value = down[:, half_of(part, size)]
    for b in range(blocks):
        tall[b * span : (b + 1) * span, :] = pick(down_keep[b, part], value[b * span : (b + 1) * span])
    for b in range(out.shape[0]):
        out[b, 2 * units : 3 * units, :] = tall[b * units : (b + 1) * units, :]
    for k, target in enumerate(outs):
        target[...] = full[own ^ k]


def pack_body(place_of, *refs):
    *pieces, out = refs
    own = place_of[1]
    for k, piece in enumerate(pieces):
        out[own ^ k] = piece[...]


def panel_of(panel, b):
    cols, _, block, width = panel.shape
    return panel[:, b].reshape(cols * block, width)


def partial_body(rep, panel, mine, theirs, weights, part):
    own = rep[0]
    size = mine.shape[2]
    weights[:, :, half_of(own, size)] = mine[...]
    weights[:, :, half_of(1 - own, size)] = theirs[...]
    units = weights.shape[1] // 3
    model = weights.shape[2]
    far, _, piece, _ = part.shape
    both = [None] * 2
    for b in range(weights.shape[0]):
        rows = panel_of(panel, b)
        first = dot(weights[b, : 2 * units, :], rows[:, :model], FLIPPED)
        last = dot(weights[b, 2 * units :, :], rows[:, model:], FLIPPED)
        both = [first, last] if b == 0 else [both[0] + first, both[1] + last]
    for a in range(far):
        part[a, 0] = both[0][a * piece : (a + 1) * piece].astype(BF16)
        part[a, 1] = both[0][units + a * piece : units + (a + 1) * piece].astype(BF16)
        part[a, 2] = both[1][a * piece : (a + 1) * piece].astype(BF16)


def pointwise_body(parts, out):
    total = parts[0].astype(F32)
    for a in range(1, parts.shape[0]):
        total = total + parts[a].astype(F32)
    gate, up, back = total[0], total[1], total[2]
    sig = jax.nn.sigmoid(gate)
    out[0] = (gate * sig * up).astype(BF16)
    out[1] = (back * up * sig * (1.0 + gate * (1.0 - sig))).astype(BF16)
    out[2] = (back * gate * sig).astype(BF16)


def assemble(mid, place):
    return jnp.concatenate([mid[a, place].astype(F32) for a in range(mid.shape[0])], axis=0)


def outputs_body(mid, weights, out):
    units = weights.shape[1] // 3
    model = weights.shape[2]
    cols, near, block, _ = out.shape
    hidden, gate, up = (assemble(mid, m).T.astype(BF16) for m in range(3))
    for b in range(near):
        ahead = dot(hidden, weights[b, 2 * units :, :], PLAIN)
        behind = dot(gate, weights[b, :units, :], PLAIN) + dot(up, weights[b, units : 2 * units, :], PLAIN)
        out[:, b, :, :model] = ahead.astype(BF16).reshape(cols, block, model)
        out[:, b, :, model:] = behind.astype(BF16).reshape(cols, block, model)


def terms_body(rep, panel, mid, keep, give, full):
    own = rep[0]
    size = keep.shape[2]
    near, stacked, model = full.shape
    units = stacked // 3
    hidden, gate, up = (assemble(mid, m).astype(BF16) for m in range(3))
    for b in range(near):
        rows = panel_of(panel, b)
        full[b, :units, :] = dot(gate, rows[:, :model], PLAIN).astype(BF16)
        full[b, units : 2 * units, :] = dot(up, rows[:, :model], PLAIN).astype(BF16)
        full[b, 2 * units :, :] = dot(hidden, rows[:, model:], PLAIN).astype(BF16)
    keep[...] = full[:, :, half_of(own, size)]
    give[...] = full[:, :, half_of(1 - own, size)]


def add_body(place_of, left, right, *outs):
    own = place_of[1]
    for k, out in enumerate(outs):
        member = own ^ k
        out[...] = (left[member].astype(F32) + right[member].astype(F32)).astype(BF16)


def fold_body(pieces, out):
    total = pieces[0].astype(F32)
    for c in range(1, pieces.shape[0]):
        total = total + pieces[c].astype(F32)
    out[...] = total.astype(BF16)


def finish_body(pieces, mixed, input_grad):
    model = mixed.shape[1]
    total = pieces[0].astype(F32)
    for b in range(1, pieces.shape[0]):
        total = total + pieces[b].astype(F32)
    mixed[...] = total[:, :model].astype(BF16)
    input_grad[...] = total[:, model:].astype(BF16)


def unpack_body(rep, mine, theirs, gate_keep, up_keep, down_keep, gate_out, up_out, down_out, tall):
    own = rep[0]
    near, stacked, size = mine.shape
    units = stacked // 3
    blocks = gate_keep.shape[1]
    span = gate_out.shape[1] // blocks
    for source, part in ((mine, own), (theirs, 1 - own)):
        for place, keep, out in ((0, gate_keep, gate_out), (1, up_keep, up_out), (2, down_keep, down_out)):
            for b in range(near):
                tall[b * units : (b + 1) * units, :] = source[b, place * units : (place + 1) * units, :]
            if place < 2:
                turned = tall[...].T
                for b in range(blocks):
                    out[half_of(part, size), b * span : (b + 1) * span] = pick(
                        keep[part, b], turned[:, b * span : (b + 1) * span]
                    )
            else:
                for b in range(blocks):
                    out[b * span : (b + 1) * span, half_of(part, size)] = pick(
                        keep[b, part], tall[b * span : (b + 1) * span, :]
                    )


def spread(value, axis):
    count = lax.axis_size(axis)
    return lax.all_to_all(jnp.broadcast_to(value[None], (count,) + value.shape), axis, 0, 0)


def exchange(pieces, count):
    own, *others = pieces
    moved = [
        lax.ppermute(piece, "b", [(i, i ^ k) for i in range(count)])
        for k, piece in enumerate(others, 1)
    ]
    return [own, *moved]


def per_device(tokens, grad_out, gate_weight, up_weight, down_weight, gate_keep, up_keep, down_keep):
    far = lax.axis_size("a")
    group = lax.axis_size("b")
    cols = lax.axis_size("col")
    block, model = tokens.shape
    width = gate_weight.shape[1]
    units = width // group
    piece = units // far
    held = cols * block
    size = model // HALVES
    place = jnp.stack([lax.axis_index("rep"), lax.axis_index("b")]).astype(jnp.int32)
    joined = jnp.concatenate([tokens, grad_out], axis=1)
    panel = spread(joined, "b")
    sent = call(
        prepare_body,
        [SMEM] + [VMEM] * 3 + [SMEM] * 3,
        [local(3 * units, size)] * group,
        [pltpu.VMEM((group, 3 * units, size), BF16), pltpu.VMEM((size, width), BF16), pltpu.VMEM((width, size), BF16)],
    )(place, gate_weight, up_weight, down_weight, gate_keep, up_keep, down_keep)
    got = exchange(sent, group)
    panel = spread(panel, "col")
    (mine,) = call(pack_body, [SMEM] + [VMEM] * group, [local(group, 3 * units, size)])(
        place, *map(near, got)
    )
    theirs = lax.ppermute(mine, "rep", SWAP)
    first_mark = mark(place)
    weights, part = call(
        partial_body,
        [SMEM] + [VMEM] * 3,
        [local(group, 3 * units, model), local(far, 3, piece, held)],
    )(first_mark, near(panel), near(mine), near(theirs))
    parts = lax.all_to_all(part, "a", 0, 0)
    (own,) = call(pointwise_body, [VMEM], [local(3, piece, held)])(near(parts))
    mid = lax.all_gather(own.reshape(3 * piece, held), "a", axis=0, tiled=True)
    mid = near(mid.reshape(far, 3, piece, held))
    keep, give = call(
        terms_body,
        [SMEM] + [VMEM] * 2,
        [local(group, 3 * units, size)] * 2,
        [pltpu.VMEM((group, 3 * units, model), BF16)],
    )(place, near(panel), mid)
    taken = lax.ppermute(give, "rep", SWAP)
    (out,) = call(outputs_body, [VMEM] * 2, [local(cols, group, block, 2 * model)])(
        mid, weights
    )
    pieces = lax.all_to_all(out, "col", 0, 0)
    terms = call(add_body, [SMEM] + [VMEM] * 2, [local(3 * units, size)] * group)(
        place, keep, near(taken)
    )
    terms = exchange(terms, group)
    second_mark = mark(first_mark)
    (folded,) = call(fold_body, [VMEM], [local(group, block, 2 * model)])(near(pieces))
    last = lax.all_to_all(folded, "b", 0, 0)
    (terms,) = call(pack_body, [SMEM] + [VMEM] * group, [local(group, 3 * units, size)])(second_mark, *map(near, terms))
    others = lax.ppermute(terms, "rep", SWAP)
    mixed, input_grad = call(finish_body, [VMEM], [shape(block, model)] * 2)(near(last))
    gate_grad, up_grad, down_grad = call(
        unpack_body,
        [SMEM] + [VMEM] * 2 + [SMEM] * 3,
        [shape(model, width), shape(model, width), shape(width, model)],
        [pltpu.VMEM((width, size), BF16)],
    )(place, near(terms), near(others), gate_keep, up_keep, down_keep)
    return (mixed, input_grad, gate_grad, up_grad, down_grad)


def solution(mesh):
    rows = mesh.shape["row"]
    grid = Mesh(
        mesh.devices.reshape(rows // NEAR, NEAR, mesh.shape["col"], mesh.shape["rep"]),
        ("a", "b", "col", "rep"),
    )
    row = ("a", "b")
    return jax.shard_map(
        per_device,
        mesh=grid,
        in_specs=(
            P(("col", "rep"), row),
            P(("col", "rep"), row),
            P(row, "col"),
            P(row, "col"),
            P("col", row),
            P(row, "col"),
            P(row, "col"),
            P("col", row),
        ),
        out_specs=(
            P(("col", "rep"), row),
            P(("col", "rep"), row),
            P(row, "col"),
            P(row, "col"),
            P("col", row),
        ),
        check_vma=False,
    )
```

time: 353 us -> 156 us (0.44)
  waiting for transfers between devices: 279 us -> 17.4 us
  starting transfers between devices: 0.12 us -> 54 us
  blocking collectives: 37.4 us -> 66.8 us
  between operations: 13.9 us -> 0.9 us
  Pallas kernels: 0 us -> 12.4 us
  matrix products: 9.67 us -> 0 us
  local copies, waits for them, and re-layouts: 11.7 us -> 2.59 us
    psum x2 -> x0, waiting for transfers between devices: 190 us -> none  [the longest x1 144 us: per_device(): lax.psum(up_part.astype(jnp.bfloat16), 'row').astype(jnp.float32)]
    unnamed x4 -> x0, waiting for transfers between devices: 88.5 us -> none
    all_to_all x0 -> x3, blocking collectives: none -> 48.2 us  [the longest x1 27.7 us: per_device(): parts = lax.all_to_all(part, 'a', 0, 0)]
    ppermute x0 -> x9, starting transfers between devices: none -> 39.6 us  [the longest x6 20 us: exchange(): lax.ppermute(piece, 'b', [(i, i ^ k) for i in range(count)])]
    all_gather x2 -> x1, blocking collectives: 37.4 us -> 18.5 us  [per_device(): mid = lax.all_gather(own.reshape(3 * piece, held), 'a', axis=0, tiled=True)]
    ppermute x0 -> x9, waiting for transfers between devices: none -> 17.4 us  [the longest x6 16.9 us: exchange(): lax.ppermute(piece, 'b', [(i, i ^ k) for i in range(count)])]
    all_to_all x0 -> x2, starting transfers between devices: none -> 14.4 us  [the longest x1 7.65 us: per_device(): pieces = lax.all_to_all(out, 'col', 0, 0)]
    pallas_call x0 -> x13, Pallas kernels: none -> 12.4 us  [the longest x2 2.37 us: mark(): pl.pallas_call(mark_body, in_specs=[SMEM], out_specs=SMEM, out_shape=jax....]
  transfers between devices with their start and end apart: 3 -> 11, of which waited for: 3 -> 3; matrix products, arithmetic and copies ran while one was open for 2% -> 0% of each run, Pallas kernels for 0% -> 5%
where the time goes in v2:
time: 156 us; the launch traced here: 155 us
  blocking collectives  66.8 us (43%)
  starting transfers between devices  54 us (35%)
  waiting for transfers between devices  17.4 us (11%)
  Pallas kernels  12.4 us (8%)
  local copies, waits for them, and re-layouts  2.59 us (2%)
    all_to_all x1, blocking collectives, per_device(): parts = lax.all_to_all(part, 'a', 0, 0)  27.7 us
    ppermute x6, starting transfers between devices, exchange(): lax.ppermute(piece, 'b', [(i, i ^ k) for i in range(count)])  20 us
    all_gather x1, blocking collectives, per_device(): mid = lax.all_gather(own.reshape(3 * piece, held), 'a', axis=0, tiled=True)  18.5 us
    ppermute x6, waiting for transfers between devices, exchange(): lax.ppermute(piece, 'b', [(i, i ^ k) for i in range(count)])  16.9 us
    all_to_all x1, blocking collectives, spread(): lax.all_to_all(jnp.broadcast_to(value[None], (count,) + value.shape), axi...  10.8 us
    ppermute x1, starting transfers between devices, per_device(): taken = lax.ppermute(give, 'rep', SWAP)  10.2 us
    all_to_all x1, blocking collectives, per_device(): last = lax.all_to_all(folded, 'b', 0, 0)  9.67 us
    all_to_all x1, starting transfers between devices, per_device(): pieces = lax.all_to_all(out, 'col', 0, 0)  7.65 us
  transfers between devices with their start and end apart: 11, of which 3 were waited for; matrix products, arithmetic and copies ran while one was open for 0% of the time, Pallas kernels for 5%

profile of v2, /device:TPU:1, one launch (start us, length us, event | category | flops | bytes accessed | tf_op | source)
XLA Modules:
  0.0 154.8 jit_solution(9479528531997220838)
XLA Ops:
  0.6 0.7 pad_maximum_fusion
  1.4 10.8 %all_to_all.25 = bf16[4,16,512]{2,1,0:T(8,128)(2,1)S(1)} all-to-all(bf16[4,16,512]{2,1,0:T(8,128)(2,1)S(1)} %broadcast_in_dim.4), channel_id=1, replica_groups=mesh['a'=4,'b'=4,'col'=16,'rep'=2] {'b'}, dimensions={0} | all-to-all | bytes 131072 | tf_op jit(solution)/shard_map/all_to_all | solution.py:216
  12.2 1.1 broadcast_in_dim.5
  13.3 6.8 %all-to-all-start.1 = ((bf16[16,4,16,512]{3,2,1,0:T(8,128)(2,1)}), bf16[16,4,16,512]{3,2,1,0:T(8,128)(2,1)S(1)}, u32[]{:S(2)}, u32[]{:S(2)}) async-start(bf16[16,4,16,512]{3,2,1,0:T(8,128)(2,1)} %broadcast_in_dim.5), calls=%async_computation.1 | async-start | bytes 2097152 | tf_op jit(solution)/shard_map/all_to_all | solution.py:216
  20.3 1.0 shard_map.120
  21.3 2.5 %collective-permute-start = (bf16[672,128]{1,0:T(8,128)(2,1)S(1)}, bf16[672,128]{1,0:T(8,128)(2,1)S(1)}, u32[]{:S(2)}, u32[]{:S(2)}) collective-permute-start(bf16[672,128]{1,0:T(8,128)(2,1)S(1)} %get-tuple-element.23), channel_id=1, source_target_pairs={{0,32},{32,0},{64,96},{96,64},{1,33},{33,1},{65,97},{97,65},{2,34}... | collective-permute-start | bytes 516104 | tf_op jit(solution)/shard_map/ppermute | solution.py:222
  23.9 2.3 %collective-permute-start.1 = (bf16[672,128]{1,0:T(8,128)(2,1)S(1)}, bf16[672,128]{1,0:T(8,128)(2,1)S(1)}, u32[]{:S(2)}, u32[]{:S(2)}) collective-permute-start(bf16[672,128]{1,0:T(8,128)(2,1)S(1)} %get-tuple-element.24), channel_id=1, source_target_pairs={{0,64},{32,96},{64,0},{96,32},{1,65},{33,97},{65,1},{97,33},{2,66}... | collective-permute-start | bytes 516104 | tf_op jit(solution)/shard_map/ppermute | solution.py:222
  26.1 4.5 %collective-permute-start.2 = (bf16[672,128]{1,0:T(8,128)(2,1)S(1)}, bf16[672,128]{1,0:T(8,128)(2,1)S(1)}, u32[]{:S(2)}, u32[]{:S(2)}) collective-permute-start(bf16[672,128]{1,0:T(8,128)(2,1)S(1)} %get-tuple-element.25), channel_id=1, source_target_pairs={{0,96},{32,64},{64,32},{96,0},{1,97},{33,65},{65,33},{97,1},{2,98}... | collective-permute-start | bytes 516104 | tf_op jit(solution)/shard_map/ppermute | solution.py:222
  30.6 8.3 %collective-permute-done.1.refs_2_ = bf16[672,128]{1,0:T(8,128)(2,1)S(1)} collective-permute-done((bf16[672,128]{1,0:T(8,128)(2,1)S(1)}, bf16[672,128]{1,0:T(8,128)(2,1)S(1)}, u32[]{:S(2)}, u32[]{:S(2)}) %collective-permute-start.1) | collective-permute-done | bytes 172064 | tf_op jit(solution)/shard_map/ppermute | solution.py:222
  38.9 0.6 shard_map.121.mine
  39.5 5.3 %collective-permute-start.3 = (bf16[4,672,128]{2,1,0:T(8,128)(2,1)S(1)}, bf16[4,672,128]{2,1,0:T(8,128)(2,1)S(1)}, u32[]{:S(2)}, u32[]{:S(2)}) collective-permute-start(bf16[4,672,128]{2,1,0:T(8,128)(2,1)S(1)} %shard_map.121.mine), channel_id=1, source_target_pairs={{0,1},{1,0},{2,3},{3,2},{4,5},{5,4},{6,7},{7,6},{8,9},{9,8},{10,11... | collective-permute-start | bytes 2064392 | tf_op jit(solution)/shard_map/ppermute | solution.py:252
  44.9 1.2 shard_map.119.rep
  46.6 0.7 copy-done.8
  47.3 1.3 shard_map.122
  48.6 27.7 %all_to_all.26.parts = bf16[4,3,56,256]{3,2,1,0:T(8,128)(2,1)S(1)} all-to-all(bf16[4,3,56,256]{3,2,1,0:T(8,128)(2,1)S(1)} %get-tuple-element.26), channel_id=1, replica_groups=mesh['a'=4,'b'=4,'col'=16,'rep'=2] {'a'}, dimensions={0} | all-to-all | bytes 688128 | tf_op jit(solution)/shard_map/all_to_all | solution.py:259
  76.4 18.5 %all_gather.3 = bf16[672,256]{1,0:T(8,128)(2,1)S(1)} all-gather(bf16[168,256]{1,0:T(8,128)(2,1)S(1)} %bitcast.6), channel_id=1, replica_groups=mesh['a'=4,'b'=4,'col'=16,'rep'=2] {'a'}, dimensions={0}, use_global_device_ids=true | all-gather | bytes 430080 | tf_op jit(solution)/shard_map/all_gather | solution.py:261
  95.0 1.3 shard_map.128
  96.3 10.2 %collective-permute-start.4 = (bf16[4,672,128]{2,1,0:T(8,128)(2,1)S(1)}, bf16[4,672,128]{2,1,0:T(8,128)(2,1)S(1)}, u32[]{:S(2)}, u32[]{:S(2)}) collective-permute-start(bf16[4,672,128]{2,1,0:T(8,128)(2,1)S(1)} %get-tuple-element.31), channel_id=1, source_target_pairs={{0,1},{1,0},{2,3},{3,2},{4,5},{5,4},{6,7},{7,6},{8,9},{9,8},{10,11... | collective-permute-start | bytes 2064392 | tf_op jit(solution)/shard_map/ppermute | solution.py:269
  106.5 1.6 %shard_map.124 = bf16[16,4,16,512]{3,2,1,0:T(8,128)(2,1)} custom-call(bf16[4,3,56,256]{3,2,1,0:T(8,128)(2,1)S(1)} %bitcast.5, bf16[4,672,256]{2,1,0:T(8,128)(2,1)S(1)} %get-tuple-element.27.weights), custom_call_target="tpu_custom_call" | custom-call | tf_op jit(solution)/shard_map/pallas_call | solution.py:270
  108.2 7.6 %all-to-all-start.3 = ((bf16[16,4,16,512]{3,2,1,0:T(8,128)(2,1)}), bf16[16,4,16,512]{3,2,1,0:T(8,128)(2,1)S(1)}, u32[]{:S(2)}, u32[]{:S(2)}) async-start(bf16[16,4,16,512]{3,2,1,0:T(8,128)(2,1)} %shard_map.124), calls=%async_computation.3 | async-start | bytes 2097152 | tf_op jit(solution)/shard_map/all_to_all | solution.py:273
  115.8 0.7 shard_map.129
  116.5 4.8 %collective-permute-start.5 = (bf16[672,128]{1,0:T(8,128)(2,1)S(1)}, bf16[672,128]{1,0:T(8,128)(2,1)S(1)}, u32[]{:S(2)}, u32[]{:S(2)}) collective-permute-start(bf16[672,128]{1,0:T(8,128)(2,1)S(1)} %get-tuple-element.33), channel_id=1, source_target_pairs={{0,32},{32,0},{64,96},{96,64},{1,33},{33,1},{65,97},{97,65},{2,34}... | collective-permute-start | bytes 516104 | tf_op jit(solution)/shard_map/ppermute | solution.py:222
  121.4 2.8 %collective-permute-start.6 = (bf16[672,128]{1,0:T(8,128)(2,1)S(1)}, bf16[672,128]{1,0:T(8,128)(2,1)S(1)}, u32[]{:S(2)}, u32[]{:S(2)}) collective-permute-start(bf16[672,128]{1,0:T(8,128)(2,1)S(1)} %get-tuple-element.34), channel_id=1, source_target_pairs={{0,64},{32,96},{64,0},{96,32},{1,65},{33,97},{65,1},{97,33},{2,66}... | collective-permute-start | bytes 516104 | tf_op jit(solution)/shard_map/ppermute | solution.py:222
  124.2 3.1 %collective-permute-start.7 = (bf16[672,128]{1,0:T(8,128)(2,1)S(1)}, bf16[672,128]{1,0:T(8,128)(2,1)S(1)}, u32[]{:S(2)}, u32[]{:S(2)}) collective-permute-start(bf16[672,128]{1,0:T(8,128)(2,1)S(1)} %get-tuple-element.35), channel_id=1, source_target_pairs={{0,96},{32,64},{64,32},{96,0},{1,97},{33,65},{65,33},{97,1},{2,98}... | collective-permute-start | bytes 516104 | tf_op jit(solution)/shard_map/ppermute | solution.py:222
  127.3 1.2 shard_map.127.place_of
  128.5 8.6 %collective-permute-done.6.refs_2_ = bf16[672,128]{1,0:T(8,128)(2,1)S(1)} collective-permute-done((bf16[672,128]{1,0:T(8,128)(2,1)S(1)}, bf16[672,128]{1,0:T(8,128)(2,1)S(1)}, u32[]{:S(2)}, u32[]{:S(2)}) %collective-permute-start.6) | collective-permute-done | bytes 172064 | tf_op jit(solution)/shard_map/ppermute | solution.py:222
  137.0 0.7 copy-done.7
  137.7 0.6 shard_map.130.mine
  138.3 4.1 %collective-permute-start.8 = (bf16[4,672,128]{2,1,0:T(8,128)(2,1)S(1)}, bf16[4,672,128]{2,1,0:T(8,128)(2,1)S(1)}, u32[]{:S(2)}, u32[]{:S(2)}) collective-permute-start(bf16[4,672,128]{2,1,0:T(8,128)(2,1)S(1)} %shard_map.130.mine), channel_id=1, source_target_pairs={{0,1},{1,0},{2,3},{3,2},{4,5},{5,4},{6,7},{7,6},{8,9},{9,8},{10,11... | collective-permute-start | bytes 2064392 | tf_op jit(solution)/shard_map/ppermute | solution.py:282
  142.5 9.7 %all_to_all.27.pieces = bf16[4,16,512]{2,1,0:T(8,128)(2,1)S(1)} all-to-all(bf16[4,16,512]{2,1,0:T(8,128)(2,1)S(1)} %shard_map.125), channel_id=1, replica_groups=mesh['a'=4,'b'=4,'col'=16,'rep'=2] {'b'}, dimensions={0} | all-to-all | bytes 131072 | tf_op jit(solution)/shard_map/all_to_all | solution.py:280
  152.2 0.6 shard_map.126
  152.8 2.0 %shard_map.131 = (bf16[256,896]{1,0:T(8,128)(2,1)}, bf16[256,896]{1,0:T(8,128)(2,1)}, bf16[896,256]{1,0:T(8,128)(2,1)}) custom-call(s32[2]{0:T(128)S(1)} %copy-done.4, bf16[4,672,128]{2,1,0:T(8,128)(2,1)S(1)} %shard_map.130.mine, bf16[4,672,128]{2,1,0:T(8,128)(2,1)S(1)} %collective-permute-done.8.theirs, s32[2,7]{1,0:T(2,128)S(1)} %copy-done.5, ...), custom_call_target="tpu_custom_call" | custom-call | tf_op jit(solution)/shard_map/pallas_call | solution.py:284
  (32 shorter events, 1.0 us)
Async XLA Ops:
  12.2 7.9 %copy-start.9 = (s32[7,2]{0,1:T(2,128)S(1)}, s32[7,2]{0,1:T(2,128)}, u32[]{:S(2)}) copy-start(s32[7,2]{0,1:T(2,128)} %param.15) | copy-start | bytes 172
  12.2 8.1 %copy-start = (bf16[256,896]{1,0:T(8,128)(2,1)S(1)}, bf16[256,896]{1,0:T(8,128)(2,1)}, u32[]{:S(2)}) copy-start(bf16[256,896]{1,0:T(8,128)(2,1)} %gate.1) | copy-start | bytes 1376260
  12.2 8.1 %copy-start.1 = (bf16[256,896]{1,0:T(8,128)(2,1)S(1)}, bf16[256,896]{1,0:T(8,128)(2,1)}, u32[]{:S(2)}) copy-start(bf16[256,896]{1,0:T(8,128)(2,1)} %up.1) | copy-start | bytes 1376260
  12.2 8.1 %copy-start.2 = (bf16[896,256]{1,0:T(8,128)(2,1)S(1)}, bf16[896,256]{1,0:T(8,128)(2,1)}, u32[]{:S(2)}) copy-start(bf16[896,256]{1,0:T(8,128)(2,1)} %down.1) | copy-start | bytes 1376260
  12.2 8.1 %copy-start.5 = (s32[2,7]{1,0:T(2,128)S(1)}, s32[2,7]{1,0:T(2,128)}, u32[]{:S(2)}) copy-start(s32[2,7]{1,0:T(2,128)} %gate_keep.3) | copy-start | bytes 172
  12.2 8.1 %copy-start.6 = (s32[2,7]{1,0:T(2,128)S(1)}, s32[2,7]{1,0:T(2,128)}, u32[]{:S(2)}) copy-start(s32[2,7]{1,0:T(2,128)} %up_keep.3) | copy-start | bytes 172
  13.3 33.3 %all-to-all-start.1 = ((bf16[16,4,16,512]{3,2,1,0:T(8,128)(2,1)}), bf16[16,4,16,512]{3,2,1,0:T(8,128)(2,1)S(1)}, u32[]{:S(2)}, u32[]{:S(2)}) async-start(bf16[16,4,16,512]{3,2,1,0:T(8,128)(2,1)} %broadcast_in_dim.5), calls=%async_computation.1 | async-start | bytes 2097152 | tf_op jit(solution)/shard_map/all_to_all | solution.py:216
  20.3 19.2 %copy-start.3 = (s32[2]{0:T(128)}, s32[2]{0:T(128)S(1)}, u32[]{:S(2)}) copy-start(s32[2]{0:T(128)S(1)} %pad_add_fusion.rep.place_of) | copy-start | bytes 28
  21.3 9.3 %collective-permute-start = (bf16[672,128]{1,0:T(8,128)(2,1)S(1)}, bf16[672,128]{1,0:T(8,128)(2,1)S(1)}, u32[]{:S(2)}, u32[]{:S(2)}) collective-permute-start(bf16[672,128]{1,0:T(8,128)(2,1)S(1)} %get-tuple-element.23), channel_id=1, source_target_pairs={{0,32},{32,0},{64,96},{96,64},{1,33},{33,1},{65,97},{97,65},{2,34}... | collective-permute-start | bytes 516104 | tf_op jit(solution)/shard_map/ppermute | solution.py:222
  23.9 15.0 %collective-permute-start.1 = (bf16[672,128]{1,0:T(8,128)(2,1)S(1)}, bf16[672,128]{1,0:T(8,128)(2,1)S(1)}, u32[]{:S(2)}, u32[]{:S(2)}) collective-permute-start(bf16[672,128]{1,0:T(8,128)(2,1)S(1)} %get-tuple-element.24), channel_id=1, source_target_pairs={{0,64},{32,96},{64,0},{96,32},{1,65},{33,97},{65,1},{97,33},{2,66}... | collective-permute-start | bytes 516104 | tf_op jit(solution)/shard_map/ppermute | solution.py:222
  26.1 12.8 %collective-permute-start.2 = (bf16[672,128]{1,0:T(8,128)(2,1)S(1)}, bf16[672,128]{1,0:T(8,128)(2,1)S(1)}, u32[]{:S(2)}, u32[]{:S(2)}) collective-permute-start(bf16[672,128]{1,0:T(8,128)(2,1)S(1)} %get-tuple-element.25), channel_id=1, source_target_pairs={{0,96},{32,64},{64,32},{96,0},{1,97},{33,65},{65,33},{97,1},{2,98}... | collective-permute-start | bytes 516104 | tf_op jit(solution)/shard_map/ppermute | solution.py:222
  39.5 7.1 %collective-permute-start.3 = (bf16[4,672,128]{2,1,0:T(8,128)(2,1)S(1)}, bf16[4,672,128]{2,1,0:T(8,128)(2,1)S(1)}, u32[]{:S(2)}, u32[]{:S(2)}) collective-permute-start(bf16[4,672,128]{2,1,0:T(8,128)(2,1)S(1)} %shard_map.121.mine), channel_id=1, source_target_pairs={{0,1},{1,0},{2,3},{3,2},{4,5},{5,4},{6,7},{7,6},{8,9},{9,8},{10,11... | collective-permute-start | bytes 2064392 | tf_op jit(solution)/shard_map/ppermute | solution.py:252
  46.6 0.7 copy-start.8
  48.6 46.4 %copy-start.4 = (s32[2]{0:T(128)S(1)}, s32[2]{0:T(128)}, u32[]{:S(2)}) copy-start(s32[2]{0:T(128)} %copy-done.3) | copy-start | bytes 28
  96.3 19.5 %collective-permute-start.4 = (bf16[4,672,128]{2,1,0:T(8,128)(2,1)S(1)}, bf16[4,672,128]{2,1,0:T(8,128)(2,1)S(1)}, u32[]{:S(2)}, u32[]{:S(2)}) collective-permute-start(bf16[4,672,128]{2,1,0:T(8,128)(2,1)S(1)} %get-tuple-element.31), channel_id=1, source_target_pairs={{0,1},{1,0},{2,3},{3,2},{4,5},{5,4},{6,7},{7,6},{8,9},{9,8},{10,11... | collective-permute-start | bytes 2064392 | tf_op jit(solution)/shard_map/ppermute | solution.py:269
  108.2 34.2 %all-to-all-start.3 = ((bf16[16,4,16,512]{3,2,1,0:T(8,128)(2,1)}), bf16[16,4,16,512]{3,2,1,0:T(8,128)(2,1)S(1)}, u32[]{:S(2)}, u32[]{:S(2)}) async-start(bf16[16,4,16,512]{3,2,1,0:T(8,128)(2,1)} %shard_map.124), calls=%async_computation.3 | async-start | bytes 2097152 | tf_op jit(solution)/shard_map/all_to_all | solution.py:273
  116.5 11.9 %collective-permute-start.5 = (bf16[672,128]{1,0:T(8,128)(2,1)S(1)}, bf16[672,128]{1,0:T(8,128)(2,1)S(1)}, u32[]{:S(2)}, u32[]{:S(2)}) collective-permute-start(bf16[672,128]{1,0:T(8,128)(2,1)S(1)} %get-tuple-element.33), channel_id=1, source_target_pairs={{0,32},{32,0},{64,96},{96,64},{1,33},{33,1},{65,97},{97,65},{2,34}... | collective-permute-start | bytes 516104 | tf_op jit(solution)/shard_map/ppermute | solution.py:222
  121.4 15.7 %collective-permute-start.6 = (bf16[672,128]{1,0:T(8,128)(2,1)S(1)}, bf16[672,128]{1,0:T(8,128)(2,1)S(1)}, u32[]{:S(2)}, u32[]{:S(2)}) collective-permute-start(bf16[672,128]{1,0:T(8,128)(2,1)S(1)} %get-tuple-element.34), channel_id=1, source_target_pairs={{0,64},{32,96},{64,0},{96,32},{1,65},{33,97},{65,1},{97,33},{2,66}... | collective-permute-start | bytes 516104 | tf_op jit(solution)/shard_map/ppermute | solution.py:222
  124.2 12.9 %collective-permute-start.7 = (bf16[672,128]{1,0:T(8,128)(2,1)S(1)}, bf16[672,128]{1,0:T(8,128)(2,1)S(1)}, u32[]{:S(2)}, u32[]{:S(2)}) collective-permute-start(bf16[672,128]{1,0:T(8,128)(2,1)S(1)} %get-tuple-element.35), channel_id=1, source_target_pairs={{0,96},{32,64},{64,32},{96,0},{1,97},{33,65},{65,33},{97,1},{2,98}... | collective-permute-start | bytes 516104 | tf_op jit(solution)/shard_map/ppermute | solution.py:222
  137.0 0.7 copy-start.7
  138.3 14.5 %collective-permute-start.8 = (bf16[4,672,128]{2,1,0:T(8,128)(2,1)S(1)}, bf16[4,672,128]{2,1,0:T(8,128)(2,1)S(1)}, u32[]{:S(2)}, u32[]{:S(2)}) collective-permute-start(bf16[4,672,128]{2,1,0:T(8,128)(2,1)S(1)} %shard_map.130.mine), channel_id=1, source_target_pairs={{0,1},{1,0},{2,3},{3,2},{4,5},{5,4},{6,7},{7,6},{8,9},{9,8},{10,11... | collective-permute-start | bytes 2064392 | tf_op jit(solution)/shard_map/ppermute | solution.py:282

commit v3 on v2

--- a/solution.py
+++ b/solution.py
@@ -45,18 +45,16 @@
     return pltpu.VMEM(dims, BF16)
 
 
-def mark_body(rep, out):
-    out[0] = rep[0]
-    out[1] = rep[1]
-
-
-def mark(rep):
-    return pl.pallas_call(
-        mark_body,
-        in_specs=[SMEM],
-        out_specs=SMEM,
-        out_shape=jax.ShapeDtypeStruct((2,), jnp.int32),
-    )(rep)
+def mark_body(out):
+    out[...] = jnp.zeros_like(out)
+
+
+def next_mark_body(before, out):
+    out[...] = before[...]
+
+
+def distant(value):
+    return pltpu.with_memory_space_constraint(value, pltpu.HBM)
 
 
 def half_of(index, size):
@@ -67,10 +65,10 @@
     return jnp.where(keep != 0, value, jnp.zeros_like(value))
 
 
-def prepare_body(place_of, gate, up, down, gate_keep, up_keep, down_keep, *refs):
+def prepare_body(gate, up, down, gate_keep, up_keep, down_keep, *refs):
     *outs, full, rows, tall = refs
     out = full
-    part, own = place_of[0], place_of[1]
+    part, own = lax.axis_index("rep"), lax.axis_index("b")
     size = rows.shape[0]
     blocks = gate_keep.shape[1]
     span = rows.shape[1] // blocks
@@ -84,16 +82,16 @@
             out[b, place * units : (place + 1) * units, :] = turned[b * units : (b + 1) * units]
     value = down[:, half_of(part, size)]
     for b in range(blocks):
-        tall[b * span : (b + 1) * span, :] = pick(down_keep[b, part], value[b * span : (b + 1) * span])
+        tall[b * span : (b + 1) * span, :] = pick(down_keep[part, b], value[b * span : (b + 1) * span])
     for b in range(out.shape[0]):
         out[b, 2 * units : 3 * units, :] = tall[b * units : (b + 1) * units, :]
     for k, target in enumerate(outs):
         target[...] = full[own ^ k]
 
 
-def pack_body(place_of, *refs):
+def pack_body(*refs):
     *pieces, out = refs
-    own = place_of[1]
+    own = lax.axis_index("b")
     for k, piece in enumerate(pieces):
         out[own ^ k] = piece[...]
 
@@ -103,8 +101,8 @@
     return panel[:, b].reshape(cols * block, width)
 
 
-def partial_body(rep, panel, mine, theirs, weights, part):
-    own = rep[0]
+def partial_body(marked, panel, mine, theirs, weights, part):
+    own = lax.axis_index("rep")
     size = mine.shape[2]
     weights[:, :, half_of(own, size)] = mine[...]
     weights[:, :, half_of(1 - own, size)] = theirs[...]
@@ -150,8 +148,8 @@
         out[:, b, :, model:] = behind.astype(BF16).reshape(cols, block, model)
 
 
-def terms_body(rep, panel, mid, keep, give, full):
-    own = rep[0]
+def terms_body(panel, mid, keep, give, full):
+    own = lax.axis_index("rep")
     size = keep.shape[2]
     near, stacked, model = full.shape
     units = stacked // 3
@@ -165,8 +163,8 @@
     give[...] = full[:, :, half_of(1 - own, size)]
 
 
-def add_body(place_of, left, right, *outs):
-    own = place_of[1]
+def add_body(left, right, *outs):
+    own = lax.axis_index("b")
     for k, out in enumerate(outs):
         member = own ^ k
         out[...] = (left[member].astype(F32) + right[member].astype(F32)).astype(BF16)
@@ -188,8 +186,8 @@
     input_grad[...] = total[:, model:].astype(BF16)
 
 
-def unpack_body(rep, mine, theirs, gate_keep, up_keep, down_keep, gate_out, up_out, down_out, tall):
-    own = rep[0]
+def unpack_body(marked, mine, theirs, gate_keep, up_keep, down_keep, gate_out, up_out, down_out, tall):
+    own = lax.axis_index("rep")
     near, stacked, size = mine.shape
     units = stacked // 3
     blocks = gate_keep.shape[1]
@@ -207,7 +205,7 @@
             else:
                 for b in range(blocks):
                     out[b * span : (b + 1) * span, half_of(part, size)] = pick(
-                        keep[b, part], tall[b * span : (b + 1) * span, :]
+                        keep[part, b], tall[b * span : (b + 1) * span, :]
                     )
 
 
@@ -235,58 +233,60 @@
     piece = units // far
     held = cols * block
     size = model // HALVES
-    place = jnp.stack([lax.axis_index("rep"), lax.axis_index("b")]).astype(jnp.int32)
     joined = jnp.concatenate([tokens, grad_out], axis=1)
+    down_keep = down_keep.T
     panel = spread(joined, "b")
     sent = call(
         prepare_body,
-        [SMEM] + [VMEM] * 3 + [SMEM] * 3,
+        [VMEM] * 3 + [SMEM] * 3,
         [local(3 * units, size)] * group,
         [pltpu.VMEM((group, 3 * units, size), BF16), pltpu.VMEM((size, width), BF16), pltpu.VMEM((width, size), BF16)],
-    )(place, gate_weight, up_weight, down_weight, gate_keep, up_keep, down_keep)
+    )(*map(distant, (gate_weight, up_weight, down_weight, gate_keep, up_keep, down_keep)))
     got = exchange(sent, group)
     panel = spread(panel, "col")
-    (mine,) = call(pack_body, [SMEM] + [VMEM] * group, [local(group, 3 * units, size)])(
-        place, *map(near, got)
+    (mine,) = call(pack_body, [VMEM] * group, [local(group, 3 * units, size)])(
+        *map(near, got)
     )
     theirs = lax.ppermute(mine, "rep", SWAP)
-    first_mark = mark(place)
+    (first_mark,) = call(mark_body, [], [local(16, 128)])()
     weights, part = call(
         partial_body,
-        [SMEM] + [VMEM] * 3,
+        [VMEM] * 4,
         [local(group, 3 * units, model), local(far, 3, piece, held)],
     )(first_mark, near(panel), near(mine), near(theirs))
     parts = lax.all_to_all(part, "a", 0, 0)
     (own,) = call(pointwise_body, [VMEM], [local(3, piece, held)])(near(parts))
     mid = lax.all_gather(own.reshape(3 * piece, held), "a", axis=0, tiled=True)
     mid = near(mid.reshape(far, 3, piece, held))
+    (out,) = call(outputs_body, [VMEM] * 2, [local(cols, group, block, 2 * model)])(
+        mid, weights
+    )
+    pieces = lax.all_to_all(out, "col", 0, 0)
     keep, give = call(
         terms_body,
-        [SMEM] + [VMEM] * 2,
+        [VMEM] * 2,
         [local(group, 3 * units, size)] * 2,
         [pltpu.VMEM((group, 3 * units, model), BF16)],
-    )(place, near(panel), mid)
+    )(near(panel), mid)
     taken = lax.ppermute(give, "rep", SWAP)
-    (out,) = call(outputs_body, [VMEM] * 2, [local(cols, group, block, 2 * model)])(
-        mid, weights
-    )
-    pieces = lax.all_to_all(out, "col", 0, 0)
-    terms = call(add_body, [SMEM] + [VMEM] * 2, [local(3 * units, size)] * group)(
-        place, keep, near(taken)
+    terms = call(add_body, [VMEM] * 2, [local(3 * units, size)] * group)(
+        keep, near(taken)
     )
     terms = exchange(terms, group)
-    second_mark = mark(first_mark)
+    (second_mark,) = call(next_mark_body, [VMEM], [local(16, 128)])(first_mark)
     (folded,) = call(fold_body, [VMEM], [local(group, block, 2 * model)])(near(pieces))
     last = lax.all_to_all(folded, "b", 0, 0)
-    (terms,) = call(pack_body, [SMEM] + [VMEM] * group, [local(group, 3 * units, size)])(second_mark, *map(near, terms))
+    (terms,) = call(pack_body, [VMEM] * group, [local(group, 3 * units, size)])(
+        *map(near, terms)
+    )
     others = lax.ppermute(terms, "rep", SWAP)
     mixed, input_grad = call(finish_body, [VMEM], [shape(block, model)] * 2)(near(last))
     gate_grad, up_grad, down_grad = call(
         unpack_body,
-        [SMEM] + [VMEM] * 2 + [SMEM] * 3,
+        [VMEM] * 3 + [SMEM] * 3,
         [shape(model, width), shape(model, width), shape(width, model)],
         [pltpu.VMEM((width, size), BF16)],
-    )(place, near(terms), near(others), gate_keep, up_keep, down_keep)
+    )(second_mark, near(terms), near(others), *map(distant, (gate_keep, up_keep, down_keep)))
     return (mixed, input_grad, gate_grad, up_grad, down_grad)
 
 

time: 156 us -> 153 us (0.981)
  blocking collectives: 66.8 us -> 57.1 us
  waiting for transfers between devices: 17.4 us -> 24.6 us
  starting transfers between devices: 54 us -> 59.2 us
  Pallas kernels: 12.4 us -> 8.93 us
    all_to_all x1 -> x0, blocking collectives: 9.67 us -> none  [per_device(): last = lax.all_to_all(folded, 'b', 0, 0)]
    all_to_all x0 -> x1, starting transfers between devices: none -> 5.16 us  [per_device(): last = lax.all_to_all(folded, 'b', 0, 0)]
    all_to_all x0 -> x1, waiting for transfers between devices: none -> 4.69 us  [per_device(): last = lax.all_to_all(folded, 'b', 0, 0)]
    pallas_call x9, Pallas kernels: 9.91 us -> 5.85 us  [the longest x1 2.14 us: per_device(): call(unpack_body, [VMEM] * 3 + [SMEM] * 3, [shape(model, width), shape(mo...]
  transfers between devices with their start and end apart: 11 -> 12, of which waited for: 3 -> 4; matrix products, arithmetic and copies ran while one was open for 0% -> 0% of each run, Pallas kernels for 5% -> 3%
where the time goes in v3:
time: 153 us; the launch traced here: 152 us
  starting transfers between devices  59.2 us (39%)
  blocking collectives  57.1 us (37%)
  waiting for transfers between devices  24.6 us (16%)
  Pallas kernels  8.93 us (6%)
    all_to_all x1, blocking collectives, per_device(): parts = lax.all_to_all(part, 'a', 0, 0)  27.7 us
    ppermute x6, starting transfers between devices, exchange(): lax.ppermute(piece, 'b', [(i, i ^ k) for i in range(count)])  19.8 us
    all_gather x1, blocking collectives, per_device(): mid = lax.all_gather(own.reshape(3 * piece, held), 'a', axis=0, tiled=True)  18.5 us
    ppermute x6, waiting for transfers between devices, exchange(): lax.ppermute(piece, 'b', [(i, i ^ k) for i in range(count)])  18.1 us
    all_to_all x1, blocking collectives, spread(): lax.all_to_all(jnp.broadcast_to(value[None], (count,) + value.shape), axi...  10.8 us
    ppermute x1, starting transfers between devices, per_device(): taken = lax.ppermute(give, 'rep', SWAP)  10 us
    all_to_all x1, starting transfers between devices, per_device(): pieces = lax.all_to_all(out, 'col', 0, 0)  8.19 us
    all_to_all x1, starting transfers between devices, spread(): lax.all_to_all(jnp.broadcast_to(value[None], (count,) + value.shape), axi...  6.75 us
  transfers between devices with their start and end apart: 12, of which 4 were waited for; matrix products, arithmetic and copies ran while one was open for 0% of the time, Pallas kernels for 3%

profile of v3, /device:TPU:1, one launch (start us, length us, event | category | flops | bytes accessed | tf_op | source)
XLA Modules:
  0.0 152.4 jit_solution(8945444691288927799)
XLA Ops:
  0.6 0.7 pad_maximum_fusion
  1.4 10.8 %all_to_all.25 = bf16[4,16,512]{2,1,0:T(8,128)(2,1)S(1)} all-to-all(bf16[4,16,512]{2,1,0:T(8,128)(2,1)S(1)} %broadcast_in_dim.4), channel_id=1, replica_groups=mesh['a'=4,'b'=4,'col'=16,'rep'=2] {'b'}, dimensions={0} | all-to-all | bytes 131072 | tf_op jit(solution)/shard_map/all_to_all | solution.py:214
  12.2 1.1 broadcast_in_dim.5
  13.3 6.8 %all-to-all-start.1 = ((bf16[16,4,16,512]{3,2,1,0:T(8,128)(2,1)}), bf16[16,4,16,512]{3,2,1,0:T(8,128)(2,1)S(1)}, u32[]{:S(2)}, u32[]{:S(2)}) async-start(bf16[16,4,16,512]{3,2,1,0:T(8,128)(2,1)} %broadcast_in_dim.5), calls=%async_computation.1 | async-start | bytes 2097152 | tf_op jit(solution)/shard_map/all_to_all | solution.py:214
  20.1 1.7 %shard_map.120 = (bf16[672,128]{1,0:T(8,128)(2,1)S(1)}, bf16[672,128]{1,0:T(8,128)(2,1)S(1)}, bf16[672,128]{1,0:T(8,128)(2,1)S(1)}, bf16[672,128]{1,0:T(8,128)(2,1)S(1)}) custom-call(bf16[256,896]{1,0:T(8,128)(2,1)} %gate.1, bf16[256,896]{1,0:T(8,128)(2,1)} %up.1, bf16[896,256]{1,0:T(8,128)(2,1)} %down.1, s32[2,7]{1,0:T(2,128)} %gate_keep.3, ...), custom_call_target="tpu_custom_call" | custom-call | tf_op jit(solution)/shard_map/pallas_call | solution.py:239
  21.7 2.5 %collective-permute-start = (bf16[672,128]{1,0:T(8,128)(2,1)S(1)}, bf16[672,128]{1,0:T(8,128)(2,1)S(1)}, u32[]{:S(2)}, u32[]{:S(2)}) collective-permute-start(bf16[672,128]{1,0:T(8,128)(2,1)S(1)} %get-tuple-element.23), channel_id=1, source_target_pairs={{0,32},{32,0},{64,96},{96,64},{1,33},{33,1},{65,97},{97,65},{2,34}... | collective-permute-start | bytes 516104 | tf_op jit(solution)/shard_map/ppermute | solution.py:220
  24.3 2.3 %collective-permute-start.1 = (bf16[672,128]{1,0:T(8,128)(2,1)S(1)}, bf16[672,128]{1,0:T(8,128)(2,1)S(1)}, u32[]{:S(2)}, u32[]{:S(2)}) collective-permute-start(bf16[672,128]{1,0:T(8,128)(2,1)S(1)} %get-tuple-element.24), channel_id=1, source_target_pairs={{0,64},{32,96},{64,0},{96,32},{1,65},{33,97},{65,1},{97,33},{2,66}... | collective-permute-start | bytes 516104 | tf_op jit(solution)/shard_map/ppermute | solution.py:220
  26.6 4.5 %collective-permute-start.2 = (bf16[672,128]{1,0:T(8,128)(2,1)S(1)}, bf16[672,128]{1,0:T(8,128)(2,1)S(1)}, u32[]{:S(2)}, u32[]{:S(2)}) collective-permute-start(bf16[672,128]{1,0:T(8,128)(2,1)S(1)} %get-tuple-element.25), channel_id=1, source_target_pairs={{0,96},{32,64},{64,32},{96,0},{1,97},{33,65},{65,33},{97,1},{2,98}... | collective-permute-start | bytes 516104 | tf_op jit(solution)/shard_map/ppermute | solution.py:220
  31.0 8.3 %collective-permute-done.1.refs_2_ = bf16[672,128]{1,0:T(8,128)(2,1)S(1)} collective-permute-done((bf16[672,128]{1,0:T(8,128)(2,1)S(1)}, bf16[672,128]{1,0:T(8,128)(2,1)S(1)}, u32[]{:S(2)}, u32[]{:S(2)}) %collective-permute-start.1) | collective-permute-done | bytes 172064 | tf_op jit(solution)/shard_map/ppermute | solution.py:220
  39.3 0.1 shard_map.121.mine
  39.4 5.3 %collective-permute-start.3 = (bf16[4,672,128]{2,1,0:T(8,128)(2,1)S(1)}, bf16[4,672,128]{2,1,0:T(8,128)(2,1)S(1)}, u32[]{:S(2)}, u32[]{:S(2)}) collective-permute-start(bf16[4,672,128]{2,1,0:T(8,128)(2,1)S(1)} %shard_map.121.mine), channel_id=1, source_target_pairs={{0,1},{1,0},{2,3},{3,2},{4,5},{5,4},{6,7},{7,6},{8,9},{9,8},{10,11... | collective-permute-start | bytes 2064392 | tf_op jit(solution)/shard_map/ppermute | solution.py:250
  44.7 1.7 %collective-permute-done.3.theirs = bf16[4,672,128]{2,1,0:T(8,128)(2,1)S(1)} collective-permute-done((bf16[4,672,128]{2,1,0:T(8,128)(2,1)S(1)}, bf16[4,672,128]{2,1,0:T(8,128)(2,1)S(1)}, u32[]{:S(2)}, u32[]{:S(2)}) %collective-permute-start.3) | collective-permute-done | bytes 688160 | tf_op jit(solution)/shard_map/ppermute | solution.py:250
  46.5 0.9 shard_map.122
  47.3 27.7 %all_to_all.26.parts = bf16[4,3,56,256]{3,2,1,0:T(8,128)(2,1)S(1)} all-to-all(bf16[4,3,56,256]{3,2,1,0:T(8,128)(2,1)S(1)} %get-tuple-element.26), channel_id=1, replica_groups=mesh['a'=4,'b'=4,'col'=16,'rep'=2] {'a'}, dimensions={0} | all-to-all | bytes 688128 | tf_op jit(solution)/shard_map/all_to_all | solution.py:257
  75.1 0.1 shard_map.123
  75.2 18.5 %all_gather.3 = bf16[672,256]{1,0:T(8,128)(2,1)S(1)} all-gather(bf16[168,256]{1,0:T(8,128)(2,1)S(1)} %bitcast.5), channel_id=1, replica_groups=mesh['a'=4,'b'=4,'col'=16,'rep'=2] {'a'}, dimensions={0}, use_global_device_ids=true | all-gather | bytes 430080 | tf_op jit(solution)/shard_map/all_gather | solution.py:259
  93.7 0.9 shard_map.128
  94.6 10.0 %collective-permute-start.4 = (bf16[4,672,128]{2,1,0:T(8,128)(2,1)S(1)}, bf16[4,672,128]{2,1,0:T(8,128)(2,1)S(1)}, u32[]{:S(2)}, u32[]{:S(2)}) collective-permute-start(bf16[4,672,128]{2,1,0:T(8,128)(2,1)S(1)} %get-tuple-element.31), channel_id=1, source_target_pairs={{0,1},{1,0},{2,3},{3,2},{4,5},{5,4},{6,7},{7,6},{8,9},{9,8},{10,11... | collective-permute-start | bytes 2064392 | tf_op jit(solution)/shard_map/ppermute | solution.py:271
  104.6 1.6 %shard_map.124 = bf16[16,4,16,512]{3,2,1,0:T(8,128)(2,1)} custom-call(bf16[4,3,56,256]{3,2,1,0:T(8,128)(2,1)S(1)} %bitcast.4, bf16[4,672,256]{2,1,0:T(8,128)(2,1)S(1)} %get-tuple-element.27.weights), custom_call_target="tpu_custom_call" | custom-call | tf_op jit(solution)/shard_map/pallas_call | solution.py:261
  106.2 8.2 %all-to-all-start.3 = ((bf16[16,4,16,512]{3,2,1,0:T(8,128)(2,1)}), bf16[16,4,16,512]{3,2,1,0:T(8,128)(2,1)S(1)}, u32[]{:S(2)}, u32[]{:S(2)}) async-start(bf16[16,4,16,512]{3,2,1,0:T(8,128)(2,1)} %shard_map.124), calls=%async_computation.3 | async-start | bytes 2097152 | tf_op jit(solution)/shard_map/all_to_all | solution.py:264
  114.4 0.2 shard_map.129
  114.6 4.7 %collective-permute-start.5 = (bf16[672,128]{1,0:T(8,128)(2,1)S(1)}, bf16[672,128]{1,0:T(8,128)(2,1)S(1)}, u32[]{:S(2)}, u32[]{:S(2)}) collective-permute-start(bf16[672,128]{1,0:T(8,128)(2,1)S(1)} %get-tuple-element.33), channel_id=1, source_target_pairs={{0,32},{32,0},{64,96},{96,64},{1,33},{33,1},{65,97},{97,65},{2,34}... | collective-permute-start | bytes 516104 | tf_op jit(solution)/shard_map/ppermute | solution.py:220
  119.3 2.6 %collective-permute-start.6 = (bf16[672,128]{1,0:T(8,128)(2,1)S(1)}, bf16[672,128]{1,0:T(8,128)(2,1)S(1)}, u32[]{:S(2)}, u32[]{:S(2)}) collective-permute-start(bf16[672,128]{1,0:T(8,128)(2,1)S(1)} %get-tuple-element.34), channel_id=1, source_target_pairs={{0,64},{32,96},{64,0},{96,32},{1,65},{33,97},{65,1},{97,33},{2,66}... | collective-permute-start | bytes 516104 | tf_op jit(solution)/shard_map/ppermute | solution.py:220
  121.9 3.3 %collective-permute-start.7 = (bf16[672,128]{1,0:T(8,128)(2,1)S(1)}, bf16[672,128]{1,0:T(8,128)(2,1)S(1)}, u32[]{:S(2)}, u32[]{:S(2)}) collective-permute-start(bf16[672,128]{1,0:T(8,128)(2,1)S(1)} %get-tuple-element.35), channel_id=1, source_target_pairs={{0,96},{32,64},{64,32},{96,0},{1,97},{33,65},{65,33},{97,1},{2,98}... | collective-permute-start | bytes 516104 | tf_op jit(solution)/shard_map/ppermute | solution.py:220
  125.2 9.8 %collective-permute-done.6.refs_2_ = bf16[672,128]{1,0:T(8,128)(2,1)S(1)} collective-permute-done((bf16[672,128]{1,0:T(8,128)(2,1)S(1)}, bf16[672,128]{1,0:T(8,128)(2,1)S(1)}, u32[]{:S(2)}, u32[]{:S(2)}) %collective-permute-start.6) | collective-permute-done | bytes 172064 | tf_op jit(solution)/shard_map/ppermute | solution.py:220
  135.1 0.1 shard_map.130.mine
  135.1 3.9 %collective-permute-start.8 = (bf16[4,672,128]{2,1,0:T(8,128)(2,1)S(1)}, bf16[4,672,128]{2,1,0:T(8,128)(2,1)S(1)}, u32[]{:S(2)}, u32[]{:S(2)}) collective-permute-start(bf16[4,672,128]{2,1,0:T(8,128)(2,1)S(1)} %shard_map.130.mine), channel_id=1, source_target_pairs={{0,1},{1,0},{2,3},{3,2},{4,5},{5,4},{6,7},{7,6},{8,9},{9,8},{10,11... | collective-permute-start | bytes 2064392 | tf_op jit(solution)/shard_map/ppermute | solution.py:282
  139.0 0.8 shard_map.125
  139.8 5.2 %all-to-all-start.4 = ((bf16[4,16,512]{2,1,0:T(8,128)(2,1)}), bf16[4,16,512]{2,1,0:T(8,128)(2,1)S(1)}, u32[]{:S(2)}, u32[]{:S(2)}) async-start(bf16[4,16,512]{2,1,0:T(8,128)(2,1)} %shard_map.125), calls=%async_computation.4 | async-start | bytes 131072 | tf_op jit(solution)/shard_map/all_to_all | solution.py:278
  145.0 4.7 %all-to-all-done.4.pieces = bf16[4,16,512]{2,1,0:T(8,128)(2,1)S(1)} async-done(((bf16[4,16,512]{2,1,0:T(8,128)(2,1)}), bf16[4,16,512]{2,1,0:T(8,128)(2,1)S(1)}, u32[]{:S(2)}, u32[]{:S(2)}) %all-to-all-start.4) | async-done | bytes 65568 | tf_op jit(solution)/shard_map/all_to_all | solution.py:278
  149.7 0.6 shard_map.126
  150.3 2.1 %shard_map.131 = (bf16[256,896]{1,0:T(8,128)(2,1)}, bf16[256,896]{1,0:T(8,128)(2,1)}, bf16[896,256]{1,0:T(8,128)(2,1)}) custom-call(bf16[16,128]{1,0:T(8,128)(2,1)S(1)} %shard_map.127.marked, bf16[4,672,128]{2,1,0:T(8,128)(2,1)S(1)} %shard_map.130.mine, bf16[4,672,128]{2,1,0:T(8,128)(2,1)S(1)} %collective-permute-done.8.theirs, s32[2,7]{1,0:T(2,128)} %gate_keep.3, ...), custom_call_target="tpu_custom_call" | custom-call | tf_op jit(solution)/shard_map/pallas_call | solution.py:284
  (11 shorter events, 0.0 us)
Async XLA Ops:
  13.3 33.2 %all-to-all-start.1 = ((bf16[16,4,16,512]{3,2,1,0:T(8,128)(2,1)}), bf16[16,4,16,512]{3,2,1,0:T(8,128)(2,1)S(1)}, u32[]{:S(2)}, u32[]{:S(2)}) async-start(bf16[16,4,16,512]{3,2,1,0:T(8,128)(2,1)} %broadcast_in_dim.5), calls=%async_computation.1 | async-start | bytes 2097152 | tf_op jit(solution)/shard_map/all_to_all | solution.py:214
  21.7 9.3 %collective-permute-start = (bf16[672,128]{1,0:T(8,128)(2,1)S(1)}, bf16[672,128]{1,0:T(8,128)(2,1)S(1)}, u32[]{:S(2)}, u32[]{:S(2)}) collective-permute-start(bf16[672,128]{1,0:T(8,128)(2,1)S(1)} %get-tuple-element.23), channel_id=1, source_target_pairs={{0,32},{32,0},{64,96},{96,64},{1,33},{33,1},{65,97},{97,65},{2,34}... | collective-permute-start | bytes 516104 | tf_op jit(solution)/shard_map/ppermute | solution.py:220
  24.3 15.0 %collective-permute-start.1 = (bf16[672,128]{1,0:T(8,128)(2,1)S(1)}, bf16[672,128]{1,0:T(8,128)(2,1)S(1)}, u32[]{:S(2)}, u32[]{:S(2)}) collective-permute-start(bf16[672,128]{1,0:T(8,128)(2,1)S(1)} %get-tuple-element.24), channel_id=1, source_target_pairs={{0,64},{32,96},{64,0},{96,32},{1,65},{33,97},{65,1},{97,33},{2,66}... | collective-permute-start | bytes 516104 | tf_op jit(solution)/shard_map/ppermute | solution.py:220
  26.6 12.8 %collective-permute-start.2 = (bf16[672,128]{1,0:T(8,128)(2,1)S(1)}, bf16[672,128]{1,0:T(8,128)(2,1)S(1)}, u32[]{:S(2)}, u32[]{:S(2)}) collective-permute-start(bf16[672,128]{1,0:T(8,128)(2,1)S(1)} %get-tuple-element.25), channel_id=1, source_target_pairs={{0,96},{32,64},{64,32},{96,0},{1,97},{33,65},{65,33},{97,1},{2,98}... | collective-permute-start | bytes 516104 | tf_op jit(solution)/shard_map/ppermute | solution.py:220
  39.4 7.1 %collective-permute-start.3 = (bf16[4,672,128]{2,1,0:T(8,128)(2,1)S(1)}, bf16[4,672,128]{2,1,0:T(8,128)(2,1)S(1)}, u32[]{:S(2)}, u32[]{:S(2)}) collective-permute-start(bf16[4,672,128]{2,1,0:T(8,128)(2,1)S(1)} %shard_map.121.mine), channel_id=1, source_target_pairs={{0,1},{1,0},{2,3},{3,2},{4,5},{5,4},{6,7},{7,6},{8,9},{9,8},{10,11... | collective-permute-start | bytes 2064392 | tf_op jit(solution)/shard_map/ppermute | solution.py:250
  94.6 19.8 %collective-permute-start.4 = (bf16[4,672,128]{2,1,0:T(8,128)(2,1)S(1)}, bf16[4,672,128]{2,1,0:T(8,128)(2,1)S(1)}, u32[]{:S(2)}, u32[]{:S(2)}) collective-permute-start(bf16[4,672,128]{2,1,0:T(8,128)(2,1)S(1)} %get-tuple-element.31), channel_id=1, source_target_pairs={{0,1},{1,0},{2,3},{3,2},{4,5},{5,4},{6,7},{7,6},{8,9},{9,8},{10,11... | collective-permute-start | bytes 2064392 | tf_op jit(solution)/shard_map/ppermute | solution.py:271
  106.2 32.8 %all-to-all-start.3 = ((bf16[16,4,16,512]{3,2,1,0:T(8,128)(2,1)}), bf16[16,4,16,512]{3,2,1,0:T(8,128)(2,1)S(1)}, u32[]{:S(2)}, u32[]{:S(2)}) async-start(bf16[16,4,16,512]{3,2,1,0:T(8,128)(2,1)} %shard_map.124), calls=%async_computation.3 | async-start | bytes 2097152 | tf_op jit(solution)/shard_map/all_to_all | solution.py:264
  114.6 10.6 %collective-permute-start.5 = (bf16[672,128]{1,0:T(8,128)(2,1)S(1)}, bf16[672,128]{1,0:T(8,128)(2,1)S(1)}, u32[]{:S(2)}, u32[]{:S(2)}) collective-permute-start(bf16[672,128]{1,0:T(8,128)(2,1)S(1)} %get-tuple-element.33), channel_id=1, source_target_pairs={{0,32},{32,0},{64,96},{96,64},{1,33},{33,1},{65,97},{97,65},{2,34}... | collective-permute-start | bytes 516104 | tf_op jit(solution)/shard_map/ppermute | solution.py:220
  119.3 15.8 %collective-permute-start.6 = (bf16[672,128]{1,0:T(8,128)(2,1)S(1)}, bf16[672,128]{1,0:T(8,128)(2,1)S(1)}, u32[]{:S(2)}, u32[]{:S(2)}) collective-permute-start(bf16[672,128]{1,0:T(8,128)(2,1)S(1)} %get-tuple-element.34), channel_id=1, source_target_pairs={{0,64},{32,96},{64,0},{96,32},{1,65},{33,97},{65,1},{97,33},{2,66}... | collective-permute-start | bytes 516104 | tf_op jit(solution)/shard_map/ppermute | solution.py:220
  121.9 13.1 %collective-permute-start.7 = (bf16[672,128]{1,0:T(8,128)(2,1)S(1)}, bf16[672,128]{1,0:T(8,128)(2,1)S(1)}, u32[]{:S(2)}, u32[]{:S(2)}) collective-permute-start(bf16[672,128]{1,0:T(8,128)(2,1)S(1)} %get-tuple-element.35), channel_id=1, source_target_pairs={{0,96},{32,64},{64,32},{96,0},{1,97},{33,65},{65,33},{97,1},{2,98}... | collective-permute-start | bytes 516104 | tf_op jit(solution)/shard_map/ppermute | solution.py:220
  135.1 15.2 %collective-permute-start.8 = (bf16[4,672,128]{2,1,0:T(8,128)(2,1)S(1)}, bf16[4,672,128]{2,1,0:T(8,128)(2,1)S(1)}, u32[]{:S(2)}, u32[]{:S(2)}) collective-permute-start(bf16[4,672,128]{2,1,0:T(8,128)(2,1)S(1)} %shard_map.130.mine), channel_id=1, source_target_pairs={{0,1},{1,0},{2,3},{3,2},{4,5},{5,4},{6,7},{7,6},{8,9},{9,8},{10,11... | collective-permute-start | bytes 2064392 | tf_op jit(solution)/shard_map/ppermute | solution.py:282
  139.8 9.9 %all-to-all-start.4 = ((bf16[4,16,512]{2,1,0:T(8,128)(2,1)}), bf16[4,16,512]{2,1,0:T(8,128)(2,1)S(1)}, u32[]{:S(2)}, u32[]{:S(2)}) async-start(bf16[4,16,512]{2,1,0:T(8,128)(2,1)} %shard_map.125), calls=%async_computation.4 | async-start | bytes 131072 | tf_op jit(solution)/shard_map/all_to_all | solution.py:278

commit v4 on v3

v4 whole, which is shorter than its diff:
```python
import jax
import jax.numpy as jnp
from jax import lax
from jax.experimental import pallas as pl
from jax.experimental.pallas import tpu as pltpu
from jax.sharding import Mesh, PartitionSpec as P


BF16 = jnp.bfloat16
F32 = jnp.float32
PLAIN = (((1,), (0,)), ((), ()))
FLIPPED = (((1,), (1,)), ((), ()))
NEAR = 4
LIMIT = 16 * 1024 * 1024
HALVES = 2
SWAP = [(0, 1), (1, 0)]
VMEM = pl.BlockSpec(memory_space=pltpu.VMEM)
SMEM = pl.BlockSpec(memory_space=pltpu.SMEM)


def dot(left, right, dims):
    return lax.dot_general(left, right, dims, preferred_element_type=F32)


def shape(*dims):
    return jax.ShapeDtypeStruct(dims, BF16)


def call(body, ins, outs, scratch=()):
    return pl.pallas_call(
        body,
        in_specs=ins,
        out_specs=[VMEM] * len(outs),
        out_shape=list(outs),
        scratch_shapes=list(scratch),
        compiler_params=pltpu.CompilerParams(vmem_limit_bytes=LIMIT),
    )


def near(value):
    return pltpu.with_memory_space_constraint(value, pltpu.VMEM)


def local(*dims):
    return pltpu.VMEM(dims, BF16)


def outside(*dims):
    return pltpu.HBM(dims, BF16)


def mark_body(out):
    out[...] = jnp.zeros_like(out)


def next_mark_body(before, out):
    out[...] = before[...]


def distant(value):
    return pltpu.with_memory_space_constraint(value, pltpu.HBM)


def half_of(index, size):
    return pl.ds(pl.multiple_of(index * size, size), size)


def pick(keep, value):
    return jnp.where(keep != 0, value, jnp.zeros_like(value))


def members(own):
    rep = lax.axis_index("rep")
    return own ^ (1 + rep), own ^ (2 - rep), own ^ 3


def prepare_body(gate, up, down, gate_keep, up_keep, down_keep, stay, whole, part, full, rows, tall):
    own, rep = lax.axis_index("b"), lax.axis_index("rep")
    blocks = gate_keep.shape[1]
    span = gate.shape[1] // blocks
    size = part.shape[1]
    units = stay.shape[0] // 3
    for place, source, keep in ((0, gate, gate_keep), (1, up, up_keep)):
        for h in range(HALVES):
            for b in range(blocks):
                cut = (slice(h * size, (h + 1) * size), slice(b * span, (b + 1) * span))
                rows[cut] = pick(keep[h, b], source[cut])
        turned = rows[...].T
        for b in range(full.shape[0]):
            full[b, place * units : (place + 1) * units, :] = turned[b * units : (b + 1) * units]
    for h in range(HALVES):
        for b in range(blocks):
            cut = (slice(b * span, (b + 1) * span), slice(h * size, (h + 1) * size))
            tall[cut] = pick(down_keep[h, b], down[cut])
    for b in range(full.shape[0]):
        full[b, 2 * units : 3 * units, :] = tall[b * units : (b + 1) * units, :]
    first, _, last = members(own)
    stay[...] = full[own]
    whole[...] = full[first]
    part[...] = full[last, :, half_of(rep, size)]


def pack_body(whole, part, out):
    width = whole.shape[1]
    out[:, :width] = whole[...]
    out[:, width:] = part[...]


def panel_of(panel, b):
    cols, _, block, width = panel.shape
    return panel[:, b].reshape(cols * block, width)


def partial_body(marked, panel, stay, whole, part_in, theirs, weights, part):
    own, rep = lax.axis_index("b"), lax.axis_index("rep")
    size = part_in.shape[1]
    width = weights.shape[2]
    first, second, last = members(own)
    weights[own] = stay[...]
    weights[first] = whole[...]
    weights[second] = theirs[:, :width]
    weights[last, :, half_of(rep, size)] = part_in[...]
    weights[last, :, half_of(1 - rep, size)] = theirs[:, width:]
    units = weights.shape[1] // 3
    model = weights.shape[2]
    far, _, piece, _ = part.shape
    both = [None] * 2
    for b in range(weights.shape[0]):
        rows = panel_of(panel, b)
        first = dot(weights[b, : 2 * units, :], rows[:, :model], FLIPPED)
        last = dot(weights[b, 2 * units :, :], rows[:, model:], FLIPPED)
        both = [first, last] if b == 0 else [both[0] + first, both[1] + last]
    for a in range(far):
        part[a, 0] = both[0][a * piece : (a + 1) * piece].astype(BF16)
        part[a, 1] = both[0][units + a * piece : units + (a + 1) * piece].astype(BF16)
        part[a, 2] = both[1][a * piece : (a + 1) * piece].astype(BF16)


def pointwise_body(parts, out):
    total = parts[0].astype(F32)
    for a in range(1, parts.shape[0]):
        total = total + parts[a].astype(F32)
    gate, up, back = total[0], total[1], total[2]
    sig = jax.nn.sigmoid(gate)
    out[0] = (gate * sig * up).astype(BF16)
    out[1] = (back * up * sig * (1.0 + gate * (1.0 - sig))).astype(BF16)
    out[2] = (back * gate * sig).astype(BF16)


def assemble(mid, place):
    return jnp.concatenate([mid[a, place].astype(F32) for a in range(mid.shape[0])], axis=0)


def outputs_body(mid, weights, out):
    units = weights.shape[1] // 3
    model = weights.shape[2]
    cols, near, block, _ = out.shape
    hidden, gate, up = (assemble(mid, m).T.astype(BF16) for m in range(3))
    for b in range(near):
        ahead = dot(hidden, weights[b, 2 * units :, :], PLAIN)
        behind = dot(gate, weights[b, :units, :], PLAIN) + dot(up, weights[b, units : 2 * units, :], PLAIN)
        out[:, b, :, :model] = ahead.astype(BF16).reshape(cols, block, model)
        out[:, b, :, model:] = behind.astype(BF16).reshape(cols, block, model)


def terms_body(marked, panel, other_panel, mid, other_mid, stay, whole, part, full):
    own, rep = lax.axis_index("b"), lax.axis_index("rep")
    first, _, last = members(own)
    cols, _, block, double = panel.shape
    model = double // 2
    size = part.shape[1]
    units = stay.shape[0] // 3
    sources = [
        (rows, *(assemble(values, m).astype(BF16) for m in range(3)))
        for rows, values in ((panel, mid), (other_panel, other_mid))
    ]

    for member, out in ((own, stay), (first, whole), (last, full)):
        total = [0.0, 0.0, 0.0]
        for rows, hidden, gate, up in sources:
            block_rows = rows[:, member].reshape(cols * block, double)
            total[0] = total[0] + dot(gate, block_rows[:, :model], PLAIN)
            total[1] = total[1] + dot(up, block_rows[:, :model], PLAIN)
            total[2] = total[2] + dot(hidden, block_rows[:, model:], PLAIN)
        for place in range(3):
            out[place * units : (place + 1) * units, :] = total[place].astype(BF16)
    part[...] = full[:, half_of(rep, size)]


def fold_body(pieces, out):
    total = pieces[0].astype(F32)
    for c in range(1, pieces.shape[0]):
        total = total + pieces[c].astype(F32)
    out[...] = total.astype(BF16)


def finish_body(pieces, mixed, input_grad):
    model = mixed.shape[1]
    total = pieces[0].astype(F32)
    for b in range(1, pieces.shape[0]):
        total = total + pieces[b].astype(F32)
    mixed[...] = total[:, :model].astype(BF16)
    input_grad[...] = total[:, model:].astype(BF16)


def unpack_body(
    marked,
    stay,
    whole,
    part,
    theirs,
    gate_keep,
    up_keep,
    down_keep,
    gate_out,
    up_out,
    down_out,
    pieces,
    tall,
):
    own, rep = lax.axis_index("b"), lax.axis_index("rep")
    first, second, last = members(own)
    size = part.shape[1]
    model = stay.shape[1]
    units = stay.shape[0] // 3
    blocks = gate_keep.shape[1]
    span = gate_out.shape[1] // blocks

    pieces[own] = stay[...]
    pieces[first] = whole[...]
    pieces[second] = theirs[:, :model]
    pieces[last, :, half_of(rep, size)] = part[...]
    pieces[last, :, half_of(1 - rep, size)] = theirs[:, model:]
    for place, keep, out in ((0, gate_keep, gate_out), (1, up_keep, up_out), (2, down_keep, down_out)):
        for member in range(pieces.shape[0]):
            tall[member * units : (member + 1) * units, :] = pieces[
                member, place * units : (place + 1) * units, :
            ]
        turned = tall[...].T if place < 2 else None
        for h in range(HALVES):
            for b in range(blocks):
                if place < 2:
                    at = (slice(h * size, (h + 1) * size), slice(b * span, (b + 1) * span))
                    out[at] = pick(keep[h, b], turned[at])
                else:
                    at = (slice(b * span, (b + 1) * span), slice(h * size, (h + 1) * size))
                    out[at] = pick(keep[h, b], tall[at])


def spread(value, axis):
    count = lax.axis_size(axis)
    return lax.all_to_all(jnp.broadcast_to(value[None], (count,) + value.shape), axis, 0, 0)


def exchange(whole, part, group):
    whole_moves = [
        (HALVES * b + r, HALVES * (b ^ (1 + r)) + r) for b in range(group) for r in range(HALVES)
    ]
    return (
        lax.ppermute(whole, ("b", "rep"), whole_moves),
        lax.ppermute(part, "b", [(b, b ^ 3) for b in range(group)]),
    )


def per_device(tokens, grad_out, gate_weight, up_weight, down_weight, gate_keep, up_keep, down_keep):
    far = lax.axis_size("a")
    group = lax.axis_size("b")
    cols = lax.axis_size("col")
    block, model = tokens.shape
    width = gate_weight.shape[1]
    units = width // group
    piece = units // far
    held = cols * block
    size = model // HALVES
    joined = jnp.concatenate([tokens, grad_out], axis=1)
    down_keep = down_keep.T
    panel = spread(joined, "b")
    stay, whole, part = call(
        prepare_body,
        [VMEM] * 3 + [SMEM] * 3,
        [local(3 * units, model)] * 2 + [local(3 * units, size)],
        [
            pltpu.VMEM((group, 3 * units, model), BF16),
            pltpu.VMEM((model, width), BF16),
            pltpu.VMEM((width, model), BF16),
        ],
    )(*map(distant, (gate_weight, up_weight, down_weight, gate_keep, up_keep, down_keep)))
    whole, part = exchange(whole, part, group)
    panel = near(spread(panel, "col"))
    (packed,) = call(pack_body, [VMEM] * 2, [local(3 * units, model + size)])(
        near(whole), near(part)
    )
    theirs = lax.ppermute(packed, "rep", SWAP)
    (first_mark,) = call(mark_body, [], [local(16, 128)])()
    weights, partial = call(
        partial_body,
        [VMEM] * 6,
        [outside(group, 3 * units, model), local(far, 3, piece, held)],
    )(first_mark, panel, stay, near(whole), near(part), near(theirs))
    parts = lax.all_to_all(partial, "a", 0, 0)
    other_panel = lax.ppermute(panel, "rep", SWAP)
    (second_mark,) = call(next_mark_body, [VMEM], [local(16, 128)])(first_mark)
    (own,) = call(pointwise_body, [VMEM], [local(3, piece, held)])(near(parts))
    mid = lax.all_gather(own.reshape(3 * piece, held), "a", axis=0, tiled=True)
    mid = near(mid.reshape(far, 3, piece, held))
    (out,) = call(outputs_body, [VMEM] * 2, [local(cols, group, block, 2 * model)])(
        mid, distant(weights)
    )
    pieces = lax.all_to_all(out, "col", 0, 0)
    other_mid = lax.ppermute(mid, "rep", SWAP)
    stay, whole, part = call(
        terms_body,
        [VMEM] * 5,
        [outside(3 * units, model), local(3 * units, model), local(3 * units, size)],
        [pltpu.VMEM((3 * units, model), BF16)],
    )(second_mark, panel, near(other_panel), mid, near(other_mid))
    whole, part = exchange(whole, part, group)
    (third_mark,) = call(next_mark_body, [VMEM], [local(16, 128)])(second_mark)
    (folded,) = call(fold_body, [VMEM], [local(group, block, 2 * model)])(near(pieces))
    last = lax.all_to_all(folded, "b", 0, 0)
    (packed,) = call(pack_body, [VMEM] * 2, [local(3 * units, model + size)])(
        near(whole), near(part)
    )
    theirs = lax.ppermute(packed, "rep", SWAP)
    mixed, input_grad = call(finish_body, [VMEM], [shape(block, model)] * 2)(near(last))
    gate_grad, up_grad, down_grad = call(
        unpack_body,
        [VMEM] * 5 + [SMEM] * 3,
        [shape(model, width), shape(model, width), shape(width, model)],
        [pltpu.VMEM((group, 3 * units, model), BF16), pltpu.VMEM((width, model), BF16)],
    )(
        third_mark,
        distant(stay),
        near(whole),
        near(part),
        near(theirs),
        *map(distant, (gate_keep, up_keep, down_keep)),
    )
    return (mixed, input_grad, gate_grad, up_grad, down_grad)


def solution(mesh):
    rows = mesh.shape["row"]
    grid = Mesh(
        mesh.devices.reshape(rows // NEAR, NEAR, mesh.shape["col"], mesh.shape["rep"]),
        ("a", "b", "col", "rep"),
    )
    row = ("a", "b")
    return jax.shard_map(
        per_device,
        mesh=grid,
        in_specs=(
            P(("col", "rep"), row),
            P(("col", "rep"), row),
            P(row, "col"),
            P(row, "col"),
            P("col", row),
            P(row, "col"),
            P(row, "col"),
            P("col", row),
        ),
        out_specs=(
            P(("col", "rep"), row),
            P(("col", "rep"), row),
            P(row, "col"),
            P(row, "col"),
            P("col", row),
        ),
        check_vma=False,
    )
```

time: 153 us -> 150 us (0.980)
  blocking collectives: 57.1 us -> 28.1 us
  waiting for transfers between devices: 24.6 us -> 40 us
  starting transfers between devices: 59.2 us -> 65.7 us
  Pallas kernels: 8.93 us -> 12.5 us
    all_to_all x1 -> x0, blocking collectives: 27.7 us -> none  [per_device(): parts = lax.all_to_all(part, 'a', 0, 0)]
    all_to_all x0 -> x1, waiting for transfers between devices: none -> 12.7 us  [per_device(): parts = lax.all_to_all(partial, 'a', 0, 0)]
    all_to_all x0 -> x1, starting transfers between devices: none -> 12.1 us  [per_device(): parts = lax.all_to_all(partial, 'a', 0, 0)]
    ppermute x9 -> x8, waiting for transfers between devices: 19.9 us -> 22.7 us  [the longest x2 16.9 us: exchange(): lax.ppermute(part, 'b', [(b, b ^ 3) for b in range(group)])]
    all_to_all x1, starting transfers between devices: 8.19 us -> 5.48 us  [per_device(): pieces = lax.all_to_all(out, 'col', 0, 0)]
    ppermute x9 -> x8, starting transfers between devices: 39.1 us -> 36.5 us  [the longest x1 13 us: per_device(): other_mid = lax.ppermute(mid, 'rep', SWAP)]
    pallas_call x7, Pallas kernels: 5.85 us -> 8.14 us  [the longest x1 2.47 us: per_device(): call(unpack_body, [VMEM] * 5 + [SMEM] * 3, [shape(model, width), shape(mo...]
  transfers between devices with their start and end apart: 12 -> 12, of which waited for: 4 -> 7; matrix products, arithmetic and copies ran while one was open for 0% -> 0% of each run, Pallas kernels for 3% -> 6%
where the time goes in v4:
time: 150 us; the launch traced here: 149 us
  starting transfers between devices  65.7 us (44%)
  waiting for transfers between devices  40 us (27%)
  blocking collectives  28.1 us (19%)
  Pallas kernels  12.5 us (8%)
    all_gather x1, blocking collectives, per_device(): mid = lax.all_gather(own.reshape(3 * piece, held), 'a', axis=0, tiled=True)  17.3 us
    ppermute x2, waiting for transfers between devices, exchange(): lax.ppermute(part, 'b', [(b, b ^ 3) for b in range(group)])  16.9 us
    ppermute x1, starting transfers between devices, per_device(): other_mid = lax.ppermute(mid, 'rep', SWAP)  13 us
    all_to_all x1, waiting for transfers between devices, per_device(): parts = lax.all_to_all(partial, 'a', 0, 0)  12.7 us
    all_to_all x1, starting transfers between devices, per_device(): parts = lax.all_to_all(partial, 'a', 0, 0)  12.1 us
    ppermute x2, starting transfers between devices, exchange(): lax.ppermute(whole, ('b', 'rep'), whole_moves)  11.2 us
    all_to_all x1, blocking collectives, spread(): lax.all_to_all(jnp.broadcast_to(value[None], (count,) + value.shape), axi...  10.8 us
    all_to_all x1, starting transfers between devices, spread(): lax.all_to_all(jnp.broadcast_to(value[None], (count,) + value.shape), axi...  6.75 us
  transfers between devices with their start and end apart: 12, of which 7 were waited for; matrix products, arithmetic and copies ran while one was open for 0% of the time, Pallas kernels for 6%

profile of v4, /device:TPU:1, one launch (start us, length us, event | category | flops | bytes accessed | tf_op | source)
XLA Modules:
  0.0 148.9 jit_solution(15511300800258635136)
XLA Ops:
  0.6 0.7 pad_maximum_fusion
  1.4 10.8 %all_to_all.25 = bf16[4,16,512]{2,1,0:T(8,128)(2,1)S(1)} all-to-all(bf16[4,16,512]{2,1,0:T(8,128)(2,1)S(1)} %broadcast_in_dim.4), channel_id=1, replica_groups=mesh['a'=4,'b'=4,'col'=16,'rep'=2] {'b'}, dimensions={0} | all-to-all | bytes 131072 | tf_op jit(solution)/shard_map/all_to_all | solution.py:252
  12.2 1.1 broadcast_in_dim.5
  13.3 6.8 %all-to-all-start.1 = ((bf16[16,4,16,512]{3,2,1,0:T(8,128)(2,1)}), bf16[16,4,16,512]{3,2,1,0:T(8,128)(2,1)S(1)}, u32[]{:S(2)}, u32[]{:S(2)}) async-start(bf16[16,4,16,512]{3,2,1,0:T(8,128)(2,1)} %broadcast_in_dim.5), calls=%async_computation.1 | async-start | bytes 2097152 | tf_op jit(solution)/shard_map/all_to_all | solution.py:252
  20.1 1.9 %shard_map.120 = (bf16[672,256]{1,0:T(8,128)(2,1)S(1)}, bf16[672,256]{1,0:T(8,128)(2,1)S(1)}, bf16[672,128]{1,0:T(8,128)(2,1)S(1)}) custom-call(bf16[256,896]{1,0:T(8,128)(2,1)} %gate.1, bf16[256,896]{1,0:T(8,128)(2,1)} %up.1, bf16[896,256]{1,0:T(8,128)(2,1)} %down.1, s32[2,7]{1,0:T(2,128)} %gate_keep.3, s32[2,7]{1,0:T(2,128)} %up_keep.3, s32[2,7]{1,0:T(2,128)} %bitcast.7), custom_call_target="tpu_custom_call" | custom-call | tf_op jit(solution)/shard_map/pallas_call | solution.py:278
  22.0 2.7 %collective-permute-start = (bf16[672,256]{1,0:T(8,128)(2,1)S(1)}, bf16[672,256]{1,0:T(8,128)(2,1)S(1)}, u32[]{:S(2)}, u32[]{:S(2)}) collective-permute-start(bf16[672,256]{1,0:T(8,128)(2,1)S(1)} %get-tuple-element.19), channel_id=1, source_target_pairs={{0,32},{1,65},{32,0},{33,97},{64,96},{65,1},{96,64},{97,33},{2,34}... | collective-permute-start | bytes 1032200 | tf_op jit(solution)/shard_map/ppermute | solution.py:260
  24.6 3.9 %collective-permute-start.1 = (bf16[672,128]{1,0:T(8,128)(2,1)S(1)}, bf16[672,128]{1,0:T(8,128)(2,1)S(1)}, u32[]{:S(2)}, u32[]{:S(2)}) collective-permute-start(bf16[672,128]{1,0:T(8,128)(2,1)S(1)} %get-tuple-element.20), channel_id=1, source_target_pairs={{0,96},{32,64},{64,32},{96,0},{1,97},{33,65},{65,33},{97,1},{2,98}... | collective-permute-start | bytes 516104 | tf_op jit(solution)/shard_map/ppermute | solution.py:261
  28.5 8.7 %collective-permute-done.1.part.part_in = bf16[672,128]{1,0:T(8,128)(2,1)S(1)} collective-permute-done((bf16[672,128]{1,0:T(8,128)(2,1)S(1)}, bf16[672,128]{1,0:T(8,128)(2,1)S(1)}, u32[]{:S(2)}, u32[]{:S(2)}) %collective-permute-start.1) | collective-permute-done | bytes 172064 | tf_op jit(solution)/shard_map/ppermute | solution.py:261
  37.2 2.7 %collective-permute-done.whole = bf16[672,256]{1,0:T(8,128)(2,1)S(1)} collective-permute-done((bf16[672,256]{1,0:T(8,128)(2,1)S(1)}, bf16[672,256]{1,0:T(8,128)(2,1)S(1)}, u32[]{:S(2)}, u32[]{:S(2)}) %collective-permute-start) | collective-permute-done | bytes 344096 | tf_op jit(solution)/shard_map/ppermute | solution.py:260
  40.0 2.2 %collective-permute-start.2 = (bf16[672,384]{1,0:T(8,128)(2,1)S(1)}, bf16[672,384]{1,0:T(8,128)(2,1)S(1)}, u32[]{:S(2)}, u32[]{:S(2)}) collective-permute-start(bf16[672,384]{1,0:T(8,128)(2,1)S(1)} %shard_map.121), channel_id=1, source_target_pairs={{0,1},{1,0},{2,3},{3,2},{4,5},{5,4},{6,7},{7,6},{8,9},{9,8},{10,11... | collective-permute-start | bytes 1548296 | tf_op jit(solution)/shard_map/ppermute | solution.py:293
  42.2 1.6 %collective-permute-done.2.theirs = bf16[672,384]{1,0:T(8,128)(2,1)S(1)} collective-permute-done((bf16[672,384]{1,0:T(8,128)(2,1)S(1)}, bf16[672,384]{1,0:T(8,128)(2,1)S(1)}, u32[]{:S(2)}, u32[]{:S(2)}) %collective-permute-start.2) | collective-permute-done | bytes 516128 | tf_op jit(solution)/shard_map/ppermute | solution.py:293
  43.8 1.6 %shard_map.122 = (bf16[4,672,256]{2,1,0:T(8,128)(2,1)}, bf16[4,3,56,256]{3,2,1,0:T(8,128)(2,1)}) custom-call(bf16[16,128]{1,0:T(8,128)(2,1)S(1)} %shard_map.119.marked.before, bf16[16,4,16,512]{3,2,1,0:T(8,128)(2,1)S(1)} %all-to-all-done.1.panel, bf16[672,256]{1,0:T(8,128)(2,1)S(1)} %get-tuple-element.18.stay, ...), custom_call_target="tpu_custom_call" | custom-call | tf_op jit(solution)/shard_map/pallas_call | solution.py:295
  45.4 12.1 %all-to-all-start.2 = ((bf16[4,3,56,256]{3,2,1,0:T(8,128)(2,1)}), bf16[4,3,56,256]{3,2,1,0:T(8,128)(2,1)S(1)}, u32[]{:S(2)}, u32[]{:S(2)}) async-start(bf16[4,3,56,256]{3,2,1,0:T(8,128)(2,1)} %get-tuple-element.21), calls=%async_computation.2 | async-start | bytes 688128 | tf_op jit(solution)/shard_map/all_to_all | solution.py:300
  57.5 2.5 %collective-permute-start.3 = (bf16[16,4,16,512]{3,2,1,0:T(8,128)(2,1)S(1)}, bf16[16,4,16,512]{3,2,1,0:T(8,128)(2,1)S(1)}, u32[]{:S(2)}, u32[]{:S(2)}) collective-permute-start(bf16[16,4,16,512]{3,2,1,0:T(8,128)(2,1)S(1)} %all-to-all-done.1.panel), channel_id=1, source_target_pairs={{0,1},{1,0},{2,3},{3,2},{4,5},{5,4},{6,7},{7,6},{8,9},{9,8},{10,11... | collective-permute-start | bytes 3145736 | tf_op jit(solution)/shard_map/ppermute | solution.py:301
  60.0 12.7 %all-to-all-done.2.parts = bf16[4,3,56,256]{3,2,1,0:T(8,128)(2,1)S(1)} async-done(((bf16[4,3,56,256]{3,2,1,0:T(8,128)(2,1)}), bf16[4,3,56,256]{3,2,1,0:T(8,128)(2,1)S(1)}, u32[]{:S(2)}, u32[]{:S(2)}) %all-to-all-start.2) | async-done | bytes 344096 | tf_op jit(solution)/shard_map/all_to_all | solution.py:300
  72.6 0.1 shard_map.123
  72.7 17.3 %all_gather.3 = bf16[672,256]{1,0:T(8,128)(2,1)S(1)} all-gather(bf16[168,256]{1,0:T(8,128)(2,1)S(1)} %bitcast.6), channel_id=1, replica_groups=mesh['a'=4,'b'=4,'col'=16,'rep'=2] {'a'}, dimensions={0}, use_global_device_ids=true | all-gather | bytes 430080 | tf_op jit(solution)/shard_map/all_gather | solution.py:304
  89.9 13.0 %collective-permute-start.4 = (bf16[4,3,56,256]{3,2,1,0:T(8,128)(2,1)S(1)}, bf16[4,3,56,256]{3,2,1,0:T(8,128)(2,1)}, u32[]{:S(2)}, u32[]{:S(2)}) collective-permute-start(bf16[4,3,56,256]{3,2,1,0:T(8,128)(2,1)S(1)} %bitcast.3), channel_id=1, source_target_pairs={{0,1},{1,0},{2,3},{3,2},{4,5},{5,4},{6,7},{7,6},{8,9},{9,8},{10,11... | collective-permute-start | bytes 1032200 | tf_op jit(solution)/shard_map/ppermute | solution.py:310
  102.9 2.9 %shard_map.124 = bf16[16,4,16,512]{3,2,1,0:T(8,128)(2,1)} custom-call(bf16[4,3,56,256]{3,2,1,0:T(8,128)(2,1)S(1)} %bitcast.4, bf16[4,672,256]{2,1,0:T(8,128)(2,1)} %get-tuple-element.22.weights), custom_call_target="tpu_custom_call" | custom-call | tf_op jit(solution)/shard_map/pallas_call | solution.py:306
  105.8 5.5 %all-to-all-start.3 = ((bf16[16,4,16,512]{3,2,1,0:T(8,128)(2,1)}), bf16[16,4,16,512]{3,2,1,0:T(8,128)(2,1)S(1)}, u32[]{:S(2)}, u32[]{:S(2)}) async-start(bf16[16,4,16,512]{3,2,1,0:T(8,128)(2,1)} %shard_map.124), calls=%async_computation.3 | async-start | bytes 2097152 | tf_op jit(solution)/shard_map/all_to_all | solution.py:309
  111.4 2.1 %shard_map.129 = (bf16[672,256]{1,0:T(8,128)(2,1)}, bf16[672,256]{1,0:T(8,128)(2,1)S(1)}, bf16[672,128]{1,0:T(8,128)(2,1)S(1)}) custom-call(bf16[16,128]{1,0:T(8,128)(2,1)S(1)} %shard_map.127.before.marked, bf16[16,4,16,512]{3,2,1,0:T(8,128)(2,1)S(1)} %all-to-all-done.1.panel, bf16[16,4,16,512]{3,2,1,0:T(8,128)(2,1)S(1)} %collective-permute-done.3.other_panel, ...), custom_call_target="tpu_custom_call" | custom-call | tf_op jit(solution)/shard_map/pallas_call | solution.py:311
  113.4 8.5 %collective-permute-start.5 = (bf16[672,256]{1,0:T(8,128)(2,1)S(1)}, bf16[672,256]{1,0:T(8,128)(2,1)S(1)}, u32[]{:S(2)}, u32[]{:S(2)}) collective-permute-start(bf16[672,256]{1,0:T(8,128)(2,1)S(1)} %get-tuple-element.26), channel_id=1, source_target_pairs={{0,32},{1,65},{32,0},{33,97},{64,96},{65,1},{96,64},{97,33},{2,34}... | collective-permute-start | bytes 1032200 | tf_op jit(solution)/shard_map/ppermute | solution.py:260
  122.0 1.9 %collective-permute-start.6 = (bf16[672,128]{1,0:T(8,128)(2,1)S(1)}, bf16[672,128]{1,0:T(8,128)(2,1)S(1)}, u32[]{:S(2)}, u32[]{:S(2)}) collective-permute-start(bf16[672,128]{1,0:T(8,128)(2,1)S(1)} %get-tuple-element.27), channel_id=1, source_target_pairs={{0,96},{32,64},{64,32},{96,0},{1,97},{33,65},{65,33},{97,1},{2,98}... | collective-permute-start | bytes 516104 | tf_op jit(solution)/shard_map/ppermute | solution.py:261
  123.9 8.2 %collective-permute-done.6.part = bf16[672,128]{1,0:T(8,128)(2,1)S(1)} collective-permute-done((bf16[672,128]{1,0:T(8,128)(2,1)S(1)}, bf16[672,128]{1,0:T(8,128)(2,1)S(1)}, u32[]{:S(2)}, u32[]{:S(2)}) %collective-permute-start.6) | collective-permute-done | bytes 172064 | tf_op jit(solution)/shard_map/ppermute | solution.py:261
  132.1 1.5 collective-permute-done.5.whole
  133.6 0.1 shard_map.130
  133.6 1.9 %collective-permute-start.7 = (bf16[672,384]{1,0:T(8,128)(2,1)S(1)}, bf16[672,384]{1,0:T(8,128)(2,1)S(1)}, u32[]{:S(2)}, u32[]{:S(2)}) collective-permute-start(bf16[672,384]{1,0:T(8,128)(2,1)S(1)} %shard_map.130), channel_id=1, source_target_pairs={{0,1},{1,0},{2,3},{3,2},{4,5},{5,4},{6,7},{7,6},{8,9},{9,8},{10,11... | collective-permute-start | bytes 1548296 | tf_op jit(solution)/shard_map/ppermute | solution.py:324
  135.5 0.8 shard_map.125
  136.3 4.8 %all-to-all-start.4 = ((bf16[4,16,512]{2,1,0:T(8,128)(2,1)}), bf16[4,16,512]{2,1,0:T(8,128)(2,1)S(1)}, u32[]{:S(2)}, u32[]{:S(2)}) async-start(bf16[4,16,512]{2,1,0:T(8,128)(2,1)} %shard_map.125), calls=%async_computation.4 | async-start | bytes 131072 | tf_op jit(solution)/shard_map/all_to_all | solution.py:320
  141.2 4.7 %all-to-all-done.4.pieces = bf16[4,16,512]{2,1,0:T(8,128)(2,1)S(1)} async-done(((bf16[4,16,512]{2,1,0:T(8,128)(2,1)}), bf16[4,16,512]{2,1,0:T(8,128)(2,1)S(1)}, u32[]{:S(2)}, u32[]{:S(2)}) %all-to-all-start.4) | async-done | bytes 65568 | tf_op jit(solution)/shard_map/all_to_all | solution.py:320
  145.8 0.6 shard_map.126
  146.5 2.5 %shard_map.131 = (bf16[256,896]{1,0:T(8,128)(2,1)}, bf16[256,896]{1,0:T(8,128)(2,1)}, bf16[896,256]{1,0:T(8,128)(2,1)}) custom-call(bf16[16,128]{1,0:T(8,128)(2,1)S(1)} %shard_map.128.marked, bf16[672,256]{1,0:T(8,128)(2,1)} %get-tuple-element.25.stay, bf16[672,256]{1,0:T(8,128)(2,1)S(1)} %collective-permute-done.5.whole, ...), custom_call_target="tpu_custom_call" | custom-call | tf_op jit(solution)/shard_map/pallas_call | solution.py:326
  (10 shorter events, 0.1 us)
Async XLA Ops:
  13.3 30.5 %all-to-all-start.1 = ((bf16[16,4,16,512]{3,2,1,0:T(8,128)(2,1)}), bf16[16,4,16,512]{3,2,1,0:T(8,128)(2,1)S(1)}, u32[]{:S(2)}, u32[]{:S(2)}) async-start(bf16[16,4,16,512]{3,2,1,0:T(8,128)(2,1)} %broadcast_in_dim.5), calls=%async_computation.1 | async-start | bytes 2097152 | tf_op jit(solution)/shard_map/all_to_all | solution.py:252
  22.0 18.0 %collective-permute-start = (bf16[672,256]{1,0:T(8,128)(2,1)S(1)}, bf16[672,256]{1,0:T(8,128)(2,1)S(1)}, u32[]{:S(2)}, u32[]{:S(2)}) collective-permute-start(bf16[672,256]{1,0:T(8,128)(2,1)S(1)} %get-tuple-element.19), channel_id=1, source_target_pairs={{0,32},{1,65},{32,0},{33,97},{64,96},{65,1},{96,64},{97,33},{2,34}... | collective-permute-start | bytes 1032200 | tf_op jit(solution)/shard_map/ppermute | solution.py:260
  24.6 12.6 %collective-permute-start.1 = (bf16[672,128]{1,0:T(8,128)(2,1)S(1)}, bf16[672,128]{1,0:T(8,128)(2,1)S(1)}, u32[]{:S(2)}, u32[]{:S(2)}) collective-permute-start(bf16[672,128]{1,0:T(8,128)(2,1)S(1)} %get-tuple-element.20), channel_id=1, source_target_pairs={{0,96},{32,64},{64,32},{96,0},{1,97},{33,65},{65,33},{97,1},{2,98}... | collective-permute-start | bytes 516104 | tf_op jit(solution)/shard_map/ppermute | solution.py:261
  40.0 3.8 %collective-permute-start.2 = (bf16[672,384]{1,0:T(8,128)(2,1)S(1)}, bf16[672,384]{1,0:T(8,128)(2,1)S(1)}, u32[]{:S(2)}, u32[]{:S(2)}) collective-permute-start(bf16[672,384]{1,0:T(8,128)(2,1)S(1)} %shard_map.121), channel_id=1, source_target_pairs={{0,1},{1,0},{2,3},{3,2},{4,5},{5,4},{6,7},{7,6},{8,9},{9,8},{10,11... | collective-permute-start | bytes 1548296 | tf_op jit(solution)/shard_map/ppermute | solution.py:293
  45.4 27.2 %all-to-all-start.2 = ((bf16[4,3,56,256]{3,2,1,0:T(8,128)(2,1)}), bf16[4,3,56,256]{3,2,1,0:T(8,128)(2,1)S(1)}, u32[]{:S(2)}, u32[]{:S(2)}) async-start(bf16[4,3,56,256]{3,2,1,0:T(8,128)(2,1)} %get-tuple-element.21), calls=%async_computation.2 | async-start | bytes 688128 | tf_op jit(solution)/shard_map/all_to_all | solution.py:300
  57.5 53.9 %collective-permute-start.3 = (bf16[16,4,16,512]{3,2,1,0:T(8,128)(2,1)S(1)}, bf16[16,4,16,512]{3,2,1,0:T(8,128)(2,1)S(1)}, u32[]{:S(2)}, u32[]{:S(2)}) collective-permute-start(bf16[16,4,16,512]{3,2,1,0:T(8,128)(2,1)S(1)} %all-to-all-done.1.panel), channel_id=1, source_target_pairs={{0,1},{1,0},{2,3},{3,2},{4,5},{5,4},{6,7},{7,6},{8,9},{9,8},{10,11... | collective-permute-start | bytes 3145736 | tf_op jit(solution)/shard_map/ppermute | solution.py:301
  89.9 21.4 %collective-permute-start.4 = (bf16[4,3,56,256]{3,2,1,0:T(8,128)(2,1)S(1)}, bf16[4,3,56,256]{3,2,1,0:T(8,128)(2,1)}, u32[]{:S(2)}, u32[]{:S(2)}) collective-permute-start(bf16[4,3,56,256]{3,2,1,0:T(8,128)(2,1)S(1)} %bitcast.3), channel_id=1, source_target_pairs={{0,1},{1,0},{2,3},{3,2},{4,5},{5,4},{6,7},{7,6},{8,9},{9,8},{10,11... | collective-permute-start | bytes 1032200 | tf_op jit(solution)/shard_map/ppermute | solution.py:310
  105.8 29.7 %all-to-all-start.3 = ((bf16[16,4,16,512]{3,2,1,0:T(8,128)(2,1)}), bf16[16,4,16,512]{3,2,1,0:T(8,128)(2,1)S(1)}, u32[]{:S(2)}, u32[]{:S(2)}) async-start(bf16[16,4,16,512]{3,2,1,0:T(8,128)(2,1)} %shard_map.124), calls=%async_computation.3 | async-start | bytes 2097152 | tf_op jit(solution)/shard_map/all_to_all | solution.py:309
  113.4 20.1 %collective-permute-start.5 = (bf16[672,256]{1,0:T(8,128)(2,1)S(1)}, bf16[672,256]{1,0:T(8,128)(2,1)S(1)}, u32[]{:S(2)}, u32[]{:S(2)}) collective-permute-start(bf16[672,256]{1,0:T(8,128)(2,1)S(1)} %get-tuple-element.26), channel_id=1, source_target_pairs={{0,32},{1,65},{32,0},{33,97},{64,96},{65,1},{96,64},{97,33},{2,34}... | collective-permute-start | bytes 1032200 | tf_op jit(solution)/shard_map/ppermute | solution.py:260
  122.0 10.1 %collective-permute-start.6 = (bf16[672,128]{1,0:T(8,128)(2,1)S(1)}, bf16[672,128]{1,0:T(8,128)(2,1)S(1)}, u32[]{:S(2)}, u32[]{:S(2)}) collective-permute-start(bf16[672,128]{1,0:T(8,128)(2,1)S(1)} %get-tuple-element.27), channel_id=1, source_target_pairs={{0,96},{32,64},{64,32},{96,0},{1,97},{33,65},{65,33},{97,1},{2,98}... | collective-permute-start | bytes 516104 | tf_op jit(solution)/shard_map/ppermute | solution.py:261
  133.6 12.9 %collective-permute-start.7 = (bf16[672,384]{1,0:T(8,128)(2,1)S(1)}, bf16[672,384]{1,0:T(8,128)(2,1)S(1)}, u32[]{:S(2)}, u32[]{:S(2)}) collective-permute-start(bf16[672,384]{1,0:T(8,128)(2,1)S(1)} %shard_map.130), channel_id=1, source_target_pairs={{0,1},{1,0},{2,3},{3,2},{4,5},{5,4},{6,7},{7,6},{8,9},{9,8},{10,11... | collective-permute-start | bytes 1548296 | tf_op jit(solution)/shard_map/ppermute | solution.py:324
  136.3 9.5 %all-to-all-start.4 = ((bf16[4,16,512]{2,1,0:T(8,128)(2,1)}), bf16[4,16,512]{2,1,0:T(8,128)(2,1)S(1)}, u32[]{:S(2)}, u32[]{:S(2)}) async-start(bf16[4,16,512]{2,1,0:T(8,128)(2,1)} %shard_map.125), calls=%async_computation.4 | async-start | bytes 131072 | tf_op jit(solution)/shard_map/all_to_all | solution.py:320

commit v5 on v4

--- a/solution.py
+++ b/solution.py
@@ -256,10 +256,9 @@
     whole_moves = [
         (HALVES * b + r, HALVES * (b ^ (1 + r)) + r) for b in range(group) for r in range(HALVES)
     ]
-    return (
-        lax.ppermute(whole, ("b", "rep"), whole_moves),
-        lax.ppermute(part, "b", [(b, b ^ 3) for b in range(group)]),
-    )
+    whole = lax.ppermute(whole, ("b", "rep"), whole_moves)
+    part = lax.ppermute(part, "b", [(b, b ^ 3) for b in range(group)])
+    return whole, part
 
 
 def per_device(tokens, grad_out, gate_weight, up_weight, down_weight, gate_keep, up_keep, down_keep):
@@ -272,9 +271,8 @@
     piece = units // far
     held = cols * block
     size = model // HALVES
-    joined = jnp.concatenate([tokens, grad_out], axis=1)
     down_keep = down_keep.T
-    panel = spread(joined, "b")
+    panel = spread(jnp.concatenate([tokens, grad_out], axis=1), "b")
     stay, whole, part = call(
         prepare_body,
         [VMEM] * 3 + [SMEM] * 3,

time: 150 us -> 150 us (level)
  no operation moved by 1% of the time
where the time goes in v5:
time: 150 us; the launch traced here: 149 us
  starting transfers between devices  65.7 us (44%)
  waiting for transfers between devices  40 us (27%)
  blocking collectives  28.1 us (19%)
  Pallas kernels  12.5 us (8%)
    all_gather x1, blocking collectives, per_device(): mid = lax.all_gather(own.reshape(3 * piece, held), 'a', axis=0, tiled=True)  17.3 us
    ppermute x2, waiting for transfers between devices, exchange(): part = lax.ppermute(part, 'b', [(b, b ^ 3) for b in range(group)])  16.9 us
    ppermute x1, starting transfers between devices, per_device(): other_mid = lax.ppermute(mid, 'rep', SWAP)  13 us
    all_to_all x1, waiting for transfers between devices, per_device(): parts = lax.all_to_all(partial, 'a', 0, 0)  12.7 us
    all_to_all x1, starting transfers between devices, per_device(): parts = lax.all_to_all(partial, 'a', 0, 0)  12.1 us
    ppermute x2, starting transfers between devices, exchange(): whole = lax.ppermute(whole, ('b', 'rep'), whole_moves)  11.2 us
    all_to_all x1, blocking collectives, spread(): lax.all_to_all(jnp.broadcast_to(value[None], (count,) + value.shape), axi...  10.8 us
    all_to_all x1, starting transfers between devices, spread(): lax.all_to_all(jnp.broadcast_to(value[None], (count,) + value.shape), axi...  6.75 us
  transfers between devices with their start and end apart: 12, of which 7 were waited for; matrix products, arithmetic and copies ran while one was open for 0% of the time, Pallas kernels for 6%

profile of v5, /device:TPU:1, one launch (start us, length us, event | category | flops | bytes accessed | tf_op | source)
XLA Modules:
  0.0 148.9 jit_solution(15511300800258635136)
XLA Ops:
  0.6 0.7 pad_maximum_fusion
  1.4 10.8 %all_to_all.25 = bf16[4,16,512]{2,1,0:T(8,128)(2,1)S(1)} all-to-all(bf16[4,16,512]{2,1,0:T(8,128)(2,1)S(1)} %broadcast_in_dim.4), channel_id=1, replica_groups=mesh['a'=4,'b'=4,'col'=16,'rep'=2] {'b'}, dimensions={0} | all-to-all | bytes 131072 | tf_op jit(solution)/shard_map/all_to_all | solution.py:252
  12.2 1.1 broadcast_in_dim.5
  13.3 6.8 %all-to-all-start.1 = ((bf16[16,4,16,512]{3,2,1,0:T(8,128)(2,1)}), bf16[16,4,16,512]{3,2,1,0:T(8,128)(2,1)S(1)}, u32[]{:S(2)}, u32[]{:S(2)}) async-start(bf16[16,4,16,512]{3,2,1,0:T(8,128)(2,1)} %broadcast_in_dim.5), calls=%async_computation.1 | async-start | bytes 2097152 | tf_op jit(solution)/shard_map/all_to_all | solution.py:252
  20.1 1.9 %shard_map.120 = (bf16[672,256]{1,0:T(8,128)(2,1)S(1)}, bf16[672,256]{1,0:T(8,128)(2,1)S(1)}, bf16[672,128]{1,0:T(8,128)(2,1)S(1)}) custom-call(bf16[256,896]{1,0:T(8,128)(2,1)} %gate.1, bf16[256,896]{1,0:T(8,128)(2,1)} %up.1, bf16[896,256]{1,0:T(8,128)(2,1)} %down.1, s32[2,7]{1,0:T(2,128)} %gate_keep.3, s32[2,7]{1,0:T(2,128)} %up_keep.3, s32[2,7]{1,0:T(2,128)} %bitcast.7), custom_call_target="tpu_custom_call" | custom-call | tf_op jit(solution)/shard_map/pallas_call | solution.py:276
  22.0 2.7 %collective-permute-start = (bf16[672,256]{1,0:T(8,128)(2,1)S(1)}, bf16[672,256]{1,0:T(8,128)(2,1)S(1)}, u32[]{:S(2)}, u32[]{:S(2)}) collective-permute-start(bf16[672,256]{1,0:T(8,128)(2,1)S(1)} %get-tuple-element.19), channel_id=1, source_target_pairs={{0,32},{1,65},{32,0},{33,97},{64,96},{65,1},{96,64},{97,33},{2,34}... | collective-permute-start | bytes 1032200 | tf_op jit(solution)/shard_map/ppermute | solution.py:259
  24.6 3.9 %collective-permute-start.1 = (bf16[672,128]{1,0:T(8,128)(2,1)S(1)}, bf16[672,128]{1,0:T(8,128)(2,1)S(1)}, u32[]{:S(2)}, u32[]{:S(2)}) collective-permute-start(bf16[672,128]{1,0:T(8,128)(2,1)S(1)} %get-tuple-element.20), channel_id=1, source_target_pairs={{0,96},{32,64},{64,32},{96,0},{1,97},{33,65},{65,33},{97,1},{2,98}... | collective-permute-start | bytes 516104 | tf_op jit(solution)/shard_map/ppermute | solution.py:260
  28.5 8.7 %collective-permute-done.1.part.part_in = bf16[672,128]{1,0:T(8,128)(2,1)S(1)} collective-permute-done((bf16[672,128]{1,0:T(8,128)(2,1)S(1)}, bf16[672,128]{1,0:T(8,128)(2,1)S(1)}, u32[]{:S(2)}, u32[]{:S(2)}) %collective-permute-start.1) | collective-permute-done | bytes 172064 | tf_op jit(solution)/shard_map/ppermute | solution.py:260
  37.2 2.7 %collective-permute-done.whole = bf16[672,256]{1,0:T(8,128)(2,1)S(1)} collective-permute-done((bf16[672,256]{1,0:T(8,128)(2,1)S(1)}, bf16[672,256]{1,0:T(8,128)(2,1)S(1)}, u32[]{:S(2)}, u32[]{:S(2)}) %collective-permute-start) | collective-permute-done | bytes 344096 | tf_op jit(solution)/shard_map/ppermute | solution.py:259
  40.0 2.2 %collective-permute-start.2 = (bf16[672,384]{1,0:T(8,128)(2,1)S(1)}, bf16[672,384]{1,0:T(8,128)(2,1)S(1)}, u32[]{:S(2)}, u32[]{:S(2)}) collective-permute-start(bf16[672,384]{1,0:T(8,128)(2,1)S(1)} %shard_map.121), channel_id=1, source_target_pairs={{0,1},{1,0},{2,3},{3,2},{4,5},{5,4},{6,7},{7,6},{8,9},{9,8},{10,11... | collective-permute-start | bytes 1548296 | tf_op jit(solution)/shard_map/ppermute | solution.py:291
  42.2 1.6 %collective-permute-done.2.theirs = bf16[672,384]{1,0:T(8,128)(2,1)S(1)} collective-permute-done((bf16[672,384]{1,0:T(8,128)(2,1)S(1)}, bf16[672,384]{1,0:T(8,128)(2,1)S(1)}, u32[]{:S(2)}, u32[]{:S(2)}) %collective-permute-start.2) | collective-permute-done | bytes 516128 | tf_op jit(solution)/shard_map/ppermute | solution.py:291
  43.8 1.6 %shard_map.122 = (bf16[4,672,256]{2,1,0:T(8,128)(2,1)}, bf16[4,3,56,256]{3,2,1,0:T(8,128)(2,1)}) custom-call(bf16[16,128]{1,0:T(8,128)(2,1)S(1)} %shard_map.119.marked.before, bf16[16,4,16,512]{3,2,1,0:T(8,128)(2,1)S(1)} %all-to-all-done.1.panel, bf16[672,256]{1,0:T(8,128)(2,1)S(1)} %get-tuple-element.18.stay, ...), custom_call_target="tpu_custom_call" | custom-call | tf_op jit(solution)/shard_map/pallas_call | solution.py:293
  45.4 12.1 %all-to-all-start.2 = ((bf16[4,3,56,256]{3,2,1,0:T(8,128)(2,1)}), bf16[4,3,56,256]{3,2,1,0:T(8,128)(2,1)S(1)}, u32[]{:S(2)}, u32[]{:S(2)}) async-start(bf16[4,3,56,256]{3,2,1,0:T(8,128)(2,1)} %get-tuple-element.21), calls=%async_computation.2 | async-start | bytes 688128 | tf_op jit(solution)/shard_map/all_to_all | solution.py:298
  57.5 2.5 %collective-permute-start.3 = (bf16[16,4,16,512]{3,2,1,0:T(8,128)(2,1)S(1)}, bf16[16,4,16,512]{3,2,1,0:T(8,128)(2,1)S(1)}, u32[]{:S(2)}, u32[]{:S(2)}) collective-permute-start(bf16[16,4,16,512]{3,2,1,0:T(8,128)(2,1)S(1)} %all-to-all-done.1.panel), channel_id=1, source_target_pairs={{0,1},{1,0},{2,3},{3,2},{4,5},{5,4},{6,7},{7,6},{8,9},{9,8},{10,11... | collective-permute-start | bytes 3145736 | tf_op jit(solution)/shard_map/ppermute | solution.py:299
  60.0 12.7 %all-to-all-done.2.parts = bf16[4,3,56,256]{3,2,1,0:T(8,128)(2,1)S(1)} async-done(((bf16[4,3,56,256]{3,2,1,0:T(8,128)(2,1)}), bf16[4,3,56,256]{3,2,1,0:T(8,128)(2,1)S(1)}, u32[]{:S(2)}, u32[]{:S(2)}) %all-to-all-start.2) | async-done | bytes 344096 | tf_op jit(solution)/shard_map/all_to_all | solution.py:298
  72.6 0.1 shard_map.123
  72.7 17.3 %all_gather.3 = bf16[672,256]{1,0:T(8,128)(2,1)S(1)} all-gather(bf16[168,256]{1,0:T(8,128)(2,1)S(1)} %bitcast.6), channel_id=1, replica_groups=mesh['a'=4,'b'=4,'col'=16,'rep'=2] {'a'}, dimensions={0}, use_global_device_ids=true | all-gather | bytes 430080 | tf_op jit(solution)/shard_map/all_gather | solution.py:302
  89.9 13.0 %collective-permute-start.4 = (bf16[4,3,56,256]{3,2,1,0:T(8,128)(2,1)S(1)}, bf16[4,3,56,256]{3,2,1,0:T(8,128)(2,1)}, u32[]{:S(2)}, u32[]{:S(2)}) collective-permute-start(bf16[4,3,56,256]{3,2,1,0:T(8,128)(2,1)S(1)} %bitcast.3), channel_id=1, source_target_pairs={{0,1},{1,0},{2,3},{3,2},{4,5},{5,4},{6,7},{7,6},{8,9},{9,8},{10,11... | collective-permute-start | bytes 1032200 | tf_op jit(solution)/shard_map/ppermute | solution.py:308
  102.9 2.9 %shard_map.124 = bf16[16,4,16,512]{3,2,1,0:T(8,128)(2,1)} custom-call(bf16[4,3,56,256]{3,2,1,0:T(8,128)(2,1)S(1)} %bitcast.4, bf16[4,672,256]{2,1,0:T(8,128)(2,1)} %get-tuple-element.22.weights), custom_call_target="tpu_custom_call" | custom-call | tf_op jit(solution)/shard_map/pallas_call | solution.py:304
  105.8 5.5 %all-to-all-start.3 = ((bf16[16,4,16,512]{3,2,1,0:T(8,128)(2,1)}), bf16[16,4,16,512]{3,2,1,0:T(8,128)(2,1)S(1)}, u32[]{:S(2)}, u32[]{:S(2)}) async-start(bf16[16,4,16,512]{3,2,1,0:T(8,128)(2,1)} %shard_map.124), calls=%async_computation.3 | async-start | bytes 2097152 | tf_op jit(solution)/shard_map/all_to_all | solution.py:307
  111.4 2.1 %shard_map.129 = (bf16[672,256]{1,0:T(8,128)(2,1)}, bf16[672,256]{1,0:T(8,128)(2,1)S(1)}, bf16[672,128]{1,0:T(8,128)(2,1)S(1)}) custom-call(bf16[16,128]{1,0:T(8,128)(2,1)S(1)} %shard_map.127.before.marked, bf16[16,4,16,512]{3,2,1,0:T(8,128)(2,1)S(1)} %all-to-all-done.1.panel, bf16[16,4,16,512]{3,2,1,0:T(8,128)(2,1)S(1)} %collective-permute-done.3.other_panel, ...), custom_call_target="tpu_custom_call" | custom-call | tf_op jit(solution)/shard_map/pallas_call | solution.py:309
  113.4 8.5 %collective-permute-start.5 = (bf16[672,256]{1,0:T(8,128)(2,1)S(1)}, bf16[672,256]{1,0:T(8,128)(2,1)S(1)}, u32[]{:S(2)}, u32[]{:S(2)}) collective-permute-start(bf16[672,256]{1,0:T(8,128)(2,1)S(1)} %get-tuple-element.26), channel_id=1, source_target_pairs={{0,32},{1,65},{32,0},{33,97},{64,96},{65,1},{96,64},{97,33},{2,34}... | collective-permute-start | bytes 1032200 | tf_op jit(solution)/shard_map/ppermute | solution.py:259
  122.0 1.9 %collective-permute-start.6 = (bf16[672,128]{1,0:T(8,128)(2,1)S(1)}, bf16[672,128]{1,0:T(8,128)(2,1)S(1)}, u32[]{:S(2)}, u32[]{:S(2)}) collective-permute-start(bf16[672,128]{1,0:T(8,128)(2,1)S(1)} %get-tuple-element.27), channel_id=1, source_target_pairs={{0,96},{32,64},{64,32},{96,0},{1,97},{33,65},{65,33},{97,1},{2,98}... | collective-permute-start | bytes 516104 | tf_op jit(solution)/shard_map/ppermute | solution.py:260
  123.9 8.2 %collective-permute-done.6.part = bf16[672,128]{1,0:T(8,128)(2,1)S(1)} collective-permute-done((bf16[672,128]{1,0:T(8,128)(2,1)S(1)}, bf16[672,128]{1,0:T(8,128)(2,1)S(1)}, u32[]{:S(2)}, u32[]{:S(2)}) %collective-permute-start.6) | collective-permute-done | bytes 172064 | tf_op jit(solution)/shard_map/ppermute | solution.py:260
  132.1 1.5 collective-permute-done.5.whole
  133.6 0.1 shard_map.130
  133.6 1.9 %collective-permute-start.7 = (bf16[672,384]{1,0:T(8,128)(2,1)S(1)}, bf16[672,384]{1,0:T(8,128)(2,1)S(1)}, u32[]{:S(2)}, u32[]{:S(2)}) collective-permute-start(bf16[672,384]{1,0:T(8,128)(2,1)S(1)} %shard_map.130), channel_id=1, source_target_pairs={{0,1},{1,0},{2,3},{3,2},{4,5},{5,4},{6,7},{7,6},{8,9},{9,8},{10,11... | collective-permute-start | bytes 1548296 | tf_op jit(solution)/shard_map/ppermute | solution.py:322
  135.5 0.8 shard_map.125
  136.3 4.8 %all-to-all-start.4 = ((bf16[4,16,512]{2,1,0:T(8,128)(2,1)}), bf16[4,16,512]{2,1,0:T(8,128)(2,1)S(1)}, u32[]{:S(2)}, u32[]{:S(2)}) async-start(bf16[4,16,512]{2,1,0:T(8,128)(2,1)} %shard_map.125), calls=%async_computation.4 | async-start | bytes 131072 | tf_op jit(solution)/shard_map/all_to_all | solution.py:318
  141.2 4.7 %all-to-all-done.4.pieces = bf16[4,16,512]{2,1,0:T(8,128)(2,1)S(1)} async-done(((bf16[4,16,512]{2,1,0:T(8,128)(2,1)}), bf16[4,16,512]{2,1,0:T(8,128)(2,1)S(1)}, u32[]{:S(2)}, u32[]{:S(2)}) %all-to-all-start.4) | async-done | bytes 65568 | tf_op jit(solution)/shard_map/all_to_all | solution.py:318
  145.8 0.6 shard_map.126
  146.5 2.5 %shard_map.131 = (bf16[256,896]{1,0:T(8,128)(2,1)}, bf16[256,896]{1,0:T(8,128)(2,1)}, bf16[896,256]{1,0:T(8,128)(2,1)}) custom-call(bf16[16,128]{1,0:T(8,128)(2,1)S(1)} %shard_map.128.marked, bf16[672,256]{1,0:T(8,128)(2,1)} %get-tuple-element.25.stay, bf16[672,256]{1,0:T(8,128)(2,1)S(1)} %collective-permute-done.5.whole, ...), custom_call_target="tpu_custom_call" | custom-call | tf_op jit(solution)/shard_map/pallas_call | solution.py:324
  (10 shorter events, 0.1 us)
Async XLA Ops:
  13.3 30.5 %all-to-all-start.1 = ((bf16[16,4,16,512]{3,2,1,0:T(8,128)(2,1)}), bf16[16,4,16,512]{3,2,1,0:T(8,128)(2,1)S(1)}, u32[]{:S(2)}, u32[]{:S(2)}) async-start(bf16[16,4,16,512]{3,2,1,0:T(8,128)(2,1)} %broadcast_in_dim.5), calls=%async_computation.1 | async-start | bytes 2097152 | tf_op jit(solution)/shard_map/all_to_all | solution.py:252
  22.0 18.0 %collective-permute-start = (bf16[672,256]{1,0:T(8,128)(2,1)S(1)}, bf16[672,256]{1,0:T(8,128)(2,1)S(1)}, u32[]{:S(2)}, u32[]{:S(2)}) collective-permute-start(bf16[672,256]{1,0:T(8,128)(2,1)S(1)} %get-tuple-element.19), channel_id=1, source_target_pairs={{0,32},{1,65},{32,0},{33,97},{64,96},{65,1},{96,64},{97,33},{2,34}... | collective-permute-start | bytes 1032200 | tf_op jit(solution)/shard_map/ppermute | solution.py:259
  24.6 12.6 %collective-permute-start.1 = (bf16[672,128]{1,0:T(8,128)(2,1)S(1)}, bf16[672,128]{1,0:T(8,128)(2,1)S(1)}, u32[]{:S(2)}, u32[]{:S(2)}) collective-permute-start(bf16[672,128]{1,0:T(8,128)(2,1)S(1)} %get-tuple-element.20), channel_id=1, source_target_pairs={{0,96},{32,64},{64,32},{96,0},{1,97},{33,65},{65,33},{97,1},{2,98}... | collective-permute-start | bytes 516104 | tf_op jit(solution)/shard_map/ppermute | solution.py:260
  40.0 3.8 %collective-permute-start.2 = (bf16[672,384]{1,0:T(8,128)(2,1)S(1)}, bf16[672,384]{1,0:T(8,128)(2,1)S(1)}, u32[]{:S(2)}, u32[]{:S(2)}) collective-permute-start(bf16[672,384]{1,0:T(8,128)(2,1)S(1)} %shard_map.121), channel_id=1, source_target_pairs={{0,1},{1,0},{2,3},{3,2},{4,5},{5,4},{6,7},{7,6},{8,9},{9,8},{10,11... | collective-permute-start | bytes 1548296 | tf_op jit(solution)/shard_map/ppermute | solution.py:291
  45.4 27.2 %all-to-all-start.2 = ((bf16[4,3,56,256]{3,2,1,0:T(8,128)(2,1)}), bf16[4,3,56,256]{3,2,1,0:T(8,128)(2,1)S(1)}, u32[]{:S(2)}, u32[]{:S(2)}) async-start(bf16[4,3,56,256]{3,2,1,0:T(8,128)(2,1)} %get-tuple-element.21), calls=%async_computation.2 | async-start | bytes 688128 | tf_op jit(solution)/shard_map/all_to_all | solution.py:298
  57.5 53.9 %collective-permute-start.3 = (bf16[16,4,16,512]{3,2,1,0:T(8,128)(2,1)S(1)}, bf16[16,4,16,512]{3,2,1,0:T(8,128)(2,1)S(1)}, u32[]{:S(2)}, u32[]{:S(2)}) collective-permute-start(bf16[16,4,16,512]{3,2,1,0:T(8,128)(2,1)S(1)} %all-to-all-done.1.panel), channel_id=1, source_target_pairs={{0,1},{1,0},{2,3},{3,2},{4,5},{5,4},{6,7},{7,6},{8,9},{9,8},{10,11... | collective-permute-start | bytes 3145736 | tf_op jit(solution)/shard_map/ppermute | solution.py:299
  89.9 21.4 %collective-permute-start.4 = (bf16[4,3,56,256]{3,2,1,0:T(8,128)(2,1)S(1)}, bf16[4,3,56,256]{3,2,1,0:T(8,128)(2,1)}, u32[]{:S(2)}, u32[]{:S(2)}) collective-permute-start(bf16[4,3,56,256]{3,2,1,0:T(8,128)(2,1)S(1)} %bitcast.3), channel_id=1, source_target_pairs={{0,1},{1,0},{2,3},{3,2},{4,5},{5,4},{6,7},{7,6},{8,9},{9,8},{10,11... | collective-permute-start | bytes 1032200 | tf_op jit(solution)/shard_map/ppermute | solution.py:308
  105.8 29.7 %all-to-all-start.3 = ((bf16[16,4,16,512]{3,2,1,0:T(8,128)(2,1)}), bf16[16,4,16,512]{3,2,1,0:T(8,128)(2,1)S(1)}, u32[]{:S(2)}, u32[]{:S(2)}) async-start(bf16[16,4,16,512]{3,2,1,0:T(8,128)(2,1)} %shard_map.124), calls=%async_computation.3 | async-start | bytes 2097152 | tf_op jit(solution)/shard_map/all_to_all | solution.py:307
  113.4 20.1 %collective-permute-start.5 = (bf16[672,256]{1,0:T(8,128)(2,1)S(1)}, bf16[672,256]{1,0:T(8,128)(2,1)S(1)}, u32[]{:S(2)}, u32[]{:S(2)}) collective-permute-start(bf16[672,256]{1,0:T(8,128)(2,1)S(1)} %get-tuple-element.26), channel_id=1, source_target_pairs={{0,32},{1,65},{32,0},{33,97},{64,96},{65,1},{96,64},{97,33},{2,34}... | collective-permute-start | bytes 1032200 | tf_op jit(solution)/shard_map/ppermute | solution.py:259
  122.0 10.1 %collective-permute-start.6 = (bf16[672,128]{1,0:T(8,128)(2,1)S(1)}, bf16[672,128]{1,0:T(8,128)(2,1)S(1)}, u32[]{:S(2)}, u32[]{:S(2)}) collective-permute-start(bf16[672,128]{1,0:T(8,128)(2,1)S(1)} %get-tuple-element.27), channel_id=1, source_target_pairs={{0,96},{32,64},{64,32},{96,0},{1,97},{33,65},{65,33},{97,1},{2,98}... | collective-permute-start | bytes 516104 | tf_op jit(solution)/shard_map/ppermute | solution.py:260
  133.6 12.9 %collective-permute-start.7 = (bf16[672,384]{1,0:T(8,128)(2,1)S(1)}, bf16[672,384]{1,0:T(8,128)(2,1)S(1)}, u32[]{:S(2)}, u32[]{:S(2)}) collective-permute-start(bf16[672,384]{1,0:T(8,128)(2,1)S(1)} %shard_map.130), channel_id=1, source_target_pairs={{0,1},{1,0},{2,3},{3,2},{4,5},{5,4},{6,7},{7,6},{8,9},{9,8},{10,11... | collective-permute-start | bytes 1548296 | tf_op jit(solution)/shard_map/ppermute | solution.py:322
  136.3 9.5 %all-to-all-start.4 = ((bf16[4,16,512]{2,1,0:T(8,128)(2,1)}), bf16[4,16,512]{2,1,0:T(8,128)(2,1)S(1)}, u32[]{:S(2)}, u32[]{:S(2)}) async-start(bf16[4,16,512]{2,1,0:T(8,128)(2,1)} %shard_map.125), calls=%async_computation.4 | async-start | bytes 131072 | tf_op jit(solution)/shard_map/all_to_all | solution.py:318

commit v6 on v5

--- a/solution.py
+++ b/solution.py
@@ -216,7 +216,6 @@
     up_out,
     down_out,
     pieces,
-    tall,
 ):
     own, rep = lax.axis_index("b"), lax.axis_index("rep")
     first, second, last = members(own)
@@ -226,25 +225,21 @@
     blocks = gate_keep.shape[1]
     span = gate_out.shape[1] // blocks
 
-    pieces[own] = stay[...]
-    pieces[first] = whole[...]
-    pieces[second] = theirs[:, :model]
-    pieces[last, :, half_of(rep, size)] = part[...]
-    pieces[last, :, half_of(1 - rep, size)] = theirs[:, model:]
     for place, keep, out in ((0, gate_keep, gate_out), (1, up_keep, up_out), (2, down_keep, down_out)):
-        for member in range(pieces.shape[0]):
-            tall[member * units : (member + 1) * units, :] = pieces[
-                member, place * units : (place + 1) * units, :
-            ]
-        turned = tall[...].T if place < 2 else None
+        cut = slice(place * units, (place + 1) * units)
+        pieces[place, own] = stay[cut, :]
+        pieces[place, first] = whole[cut, :]
+        pieces[place, second] = theirs[cut, :model]
+        pieces[place, last, :, half_of(rep, size)] = part[cut, :]
+        pieces[place, last, :, half_of(1 - rep, size)] = theirs[cut, model:]
+        value = pieces[place].reshape(pieces.shape[1] * units, model)
+        if place < 2:
+            value = value.T
         for h in range(HALVES):
             for b in range(blocks):
-                if place < 2:
-                    at = (slice(h * size, (h + 1) * size), slice(b * span, (b + 1) * span))
-                    out[at] = pick(keep[h, b], turned[at])
-                else:
-                    at = (slice(b * span, (b + 1) * span), slice(h * size, (h + 1) * size))
-                    out[at] = pick(keep[h, b], tall[at])
+                at = (slice(h * size, (h + 1) * size), slice(b * span, (b + 1) * span))
+                at = at if place < 2 else at[::-1]
+                out[at] = pick(keep[h, b], value[at])
 
 
 def spread(value, axis):
@@ -325,7 +320,7 @@
         unpack_body,
         [VMEM] * 5 + [SMEM] * 3,
         [shape(model, width), shape(model, width), shape(width, model)],
-        [pltpu.VMEM((group, 3 * units, model), BF16), pltpu.VMEM((width, model), BF16)],
+        [pltpu.VMEM((3, group, units, model), BF16)],
     )(
         third_mark,
         distant(stay),

time: 150 us -> 150 us (level)
  no operation moved by 1% of the time
where the time goes in v6:
time: 150 us; the launch traced here: 149 us
  starting transfers between devices  65.7 us (44%)
  waiting for transfers between devices  40 us (27%)
  blocking collectives  28.1 us (19%)
  Pallas kernels  12.4 us (8%)
    all_gather x1, blocking collectives, per_device(): mid = lax.all_gather(own.reshape(3 * piece, held), 'a', axis=0, tiled=True)  17.3 us
    ppermute x2, waiting for transfers between devices, exchange(): part = lax.ppermute(part, 'b', [(b, b ^ 3) for b in range(group)])  16.9 us
    ppermute x1, starting transfers between devices, per_device(): other_mid = lax.ppermute(mid, 'rep', SWAP)  13 us
    all_to_all x1, waiting for transfers between devices, per_device(): parts = lax.all_to_all(partial, 'a', 0, 0)  12.7 us
    all_to_all x1, starting transfers between devices, per_device(): parts = lax.all_to_all(partial, 'a', 0, 0)  12.1 us
    ppermute x2, starting transfers between devices, exchange(): whole = lax.ppermute(whole, ('b', 'rep'), whole_moves)  11.2 us
    all_to_all x1, blocking collectives, spread(): lax.all_to_all(jnp.broadcast_to(value[None], (count,) + value.shape), axi...  10.8 us
    all_to_all x1, starting transfers between devices, spread(): lax.all_to_all(jnp.broadcast_to(value[None], (count,) + value.shape), axi...  6.75 us
  transfers between devices with their start and end apart: 12, of which 7 were waited for; matrix products, arithmetic and copies ran while one was open for 0% of the time, Pallas kernels for 6%

profile of v6, /device:TPU:1, one launch (start us, length us, event | category | flops | bytes accessed | tf_op | source)
XLA Modules:
  0.0 148.8 jit_solution(12803796110092938221)
XLA Ops:
  0.6 0.7 pad_maximum_fusion
  1.4 10.8 %all_to_all.25 = bf16[4,16,512]{2,1,0:T(8,128)(2,1)S(1)} all-to-all(bf16[4,16,512]{2,1,0:T(8,128)(2,1)S(1)} %broadcast_in_dim.4), channel_id=1, replica_groups=mesh['a'=4,'b'=4,'col'=16,'rep'=2] {'b'}, dimensions={0} | all-to-all | bytes 131072 | tf_op jit(solution)/shard_map/all_to_all | solution.py:247
  12.2 1.1 broadcast_in_dim.5
  13.3 6.8 %all-to-all-start.1 = ((bf16[16,4,16,512]{3,2,1,0:T(8,128)(2,1)}), bf16[16,4,16,512]{3,2,1,0:T(8,128)(2,1)S(1)}, u32[]{:S(2)}, u32[]{:S(2)}) async-start(bf16[16,4,16,512]{3,2,1,0:T(8,128)(2,1)} %broadcast_in_dim.5), calls=%async_computation.1 | async-start | bytes 2097152 | tf_op jit(solution)/shard_map/all_to_all | solution.py:247
  20.1 1.9 %shard_map.120 = (bf16[672,256]{1,0:T(8,128)(2,1)S(1)}, bf16[672,256]{1,0:T(8,128)(2,1)S(1)}, bf16[672,128]{1,0:T(8,128)(2,1)S(1)}) custom-call(bf16[256,896]{1,0:T(8,128)(2,1)} %gate.1, bf16[256,896]{1,0:T(8,128)(2,1)} %up.1, bf16[896,256]{1,0:T(8,128)(2,1)} %down.1, s32[2,7]{1,0:T(2,128)} %gate_keep.3, s32[2,7]{1,0:T(2,128)} %up_keep.3, s32[2,7]{1,0:T(2,128)} %bitcast.7), custom_call_target="tpu_custom_call" | custom-call | tf_op jit(solution)/shard_map/pallas_call | solution.py:271
  22.0 2.7 %collective-permute-start = (bf16[672,256]{1,0:T(8,128)(2,1)S(1)}, bf16[672,256]{1,0:T(8,128)(2,1)S(1)}, u32[]{:S(2)}, u32[]{:S(2)}) collective-permute-start(bf16[672,256]{1,0:T(8,128)(2,1)S(1)} %get-tuple-element.19), channel_id=1, source_target_pairs={{0,32},{1,65},{32,0},{33,97},{64,96},{65,1},{96,64},{97,33},{2,34}... | collective-permute-start | bytes 1032200 | tf_op jit(solution)/shard_map/ppermute | solution.py:254
  24.6 3.9 %collective-permute-start.1 = (bf16[672,128]{1,0:T(8,128)(2,1)S(1)}, bf16[672,128]{1,0:T(8,128)(2,1)S(1)}, u32[]{:S(2)}, u32[]{:S(2)}) collective-permute-start(bf16[672,128]{1,0:T(8,128)(2,1)S(1)} %get-tuple-element.20), channel_id=1, source_target_pairs={{0,96},{32,64},{64,32},{96,0},{1,97},{33,65},{65,33},{97,1},{2,98}... | collective-permute-start | bytes 516104 | tf_op jit(solution)/shard_map/ppermute | solution.py:255
  28.5 8.7 %collective-permute-done.1.part.part_in = bf16[672,128]{1,0:T(8,128)(2,1)S(1)} collective-permute-done((bf16[672,128]{1,0:T(8,128)(2,1)S(1)}, bf16[672,128]{1,0:T(8,128)(2,1)S(1)}, u32[]{:S(2)}, u32[]{:S(2)}) %collective-permute-start.1) | collective-permute-done | bytes 172064 | tf_op jit(solution)/shard_map/ppermute | solution.py:255
  37.2 2.7 %collective-permute-done.whole = bf16[672,256]{1,0:T(8,128)(2,1)S(1)} collective-permute-done((bf16[672,256]{1,0:T(8,128)(2,1)S(1)}, bf16[672,256]{1,0:T(8,128)(2,1)S(1)}, u32[]{:S(2)}, u32[]{:S(2)}) %collective-permute-start) | collective-permute-done | bytes 344096 | tf_op jit(solution)/shard_map/ppermute | solution.py:254
  40.0 2.2 %collective-permute-start.2 = (bf16[672,384]{1,0:T(8,128)(2,1)S(1)}, bf16[672,384]{1,0:T(8,128)(2,1)S(1)}, u32[]{:S(2)}, u32[]{:S(2)}) collective-permute-start(bf16[672,384]{1,0:T(8,128)(2,1)S(1)} %shard_map.121), channel_id=1, source_target_pairs={{0,1},{1,0},{2,3},{3,2},{4,5},{5,4},{6,7},{7,6},{8,9},{9,8},{10,11... | collective-permute-start | bytes 1548296 | tf_op jit(solution)/shard_map/ppermute | solution.py:286
  42.2 1.6 %collective-permute-done.2.theirs = bf16[672,384]{1,0:T(8,128)(2,1)S(1)} collective-permute-done((bf16[672,384]{1,0:T(8,128)(2,1)S(1)}, bf16[672,384]{1,0:T(8,128)(2,1)S(1)}, u32[]{:S(2)}, u32[]{:S(2)}) %collective-permute-start.2) | collective-permute-done | bytes 516128 | tf_op jit(solution)/shard_map/ppermute | solution.py:286
  43.8 1.6 %shard_map.122 = (bf16[4,672,256]{2,1,0:T(8,128)(2,1)}, bf16[4,3,56,256]{3,2,1,0:T(8,128)(2,1)}) custom-call(bf16[16,128]{1,0:T(8,128)(2,1)S(1)} %shard_map.119.marked.before, bf16[16,4,16,512]{3,2,1,0:T(8,128)(2,1)S(1)} %all-to-all-done.1.panel, bf16[672,256]{1,0:T(8,128)(2,1)S(1)} %get-tuple-element.18.stay, ...), custom_call_target="tpu_custom_call" | custom-call | tf_op jit(solution)/shard_map/pallas_call | solution.py:288
  45.4 12.1 %all-to-all-start.2 = ((bf16[4,3,56,256]{3,2,1,0:T(8,128)(2,1)}), bf16[4,3,56,256]{3,2,1,0:T(8,128)(2,1)S(1)}, u32[]{:S(2)}, u32[]{:S(2)}) async-start(bf16[4,3,56,256]{3,2,1,0:T(8,128)(2,1)} %get-tuple-element.21), calls=%async_computation.2 | async-start | bytes 688128 | tf_op jit(solution)/shard_map/all_to_all | solution.py:293
  57.5 2.5 %collective-permute-start.3 = (bf16[16,4,16,512]{3,2,1,0:T(8,128)(2,1)S(1)}, bf16[16,4,16,512]{3,2,1,0:T(8,128)(2,1)S(1)}, u32[]{:S(2)}, u32[]{:S(2)}) collective-permute-start(bf16[16,4,16,512]{3,2,1,0:T(8,128)(2,1)S(1)} %all-to-all-done.1.panel), channel_id=1, source_target_pairs={{0,1},{1,0},{2,3},{3,2},{4,5},{5,4},{6,7},{7,6},{8,9},{9,8},{10,11... | collective-permute-start | bytes 3145736 | tf_op jit(solution)/shard_map/ppermute | solution.py:294
  60.0 12.7 %all-to-all-done.2.parts = bf16[4,3,56,256]{3,2,1,0:T(8,128)(2,1)S(1)} async-done(((bf16[4,3,56,256]{3,2,1,0:T(8,128)(2,1)}), bf16[4,3,56,256]{3,2,1,0:T(8,128)(2,1)S(1)}, u32[]{:S(2)}, u32[]{:S(2)}) %all-to-all-start.2) | async-done | bytes 344096 | tf_op jit(solution)/shard_map/all_to_all | solution.py:293
  72.6 0.1 shard_map.123
  72.7 17.3 %all_gather.3 = bf16[672,256]{1,0:T(8,128)(2,1)S(1)} all-gather(bf16[168,256]{1,0:T(8,128)(2,1)S(1)} %bitcast.6), channel_id=1, replica_groups=mesh['a'=4,'b'=4,'col'=16,'rep'=2] {'a'}, dimensions={0}, use_global_device_ids=true | all-gather | bytes 430080 | tf_op jit(solution)/shard_map/all_gather | solution.py:297
  89.9 13.0 %collective-permute-start.4 = (bf16[4,3,56,256]{3,2,1,0:T(8,128)(2,1)S(1)}, bf16[4,3,56,256]{3,2,1,0:T(8,128)(2,1)}, u32[]{:S(2)}, u32[]{:S(2)}) collective-permute-start(bf16[4,3,56,256]{3,2,1,0:T(8,128)(2,1)S(1)} %bitcast.3), channel_id=1, source_target_pairs={{0,1},{1,0},{2,3},{3,2},{4,5},{5,4},{6,7},{7,6},{8,9},{9,8},{10,11... | collective-permute-start | bytes 1032200 | tf_op jit(solution)/shard_map/ppermute | solution.py:303
  102.9 2.9 %shard_map.124 = bf16[16,4,16,512]{3,2,1,0:T(8,128)(2,1)} custom-call(bf16[4,3,56,256]{3,2,1,0:T(8,128)(2,1)S(1)} %bitcast.4, bf16[4,672,256]{2,1,0:T(8,128)(2,1)} %get-tuple-element.22.weights), custom_call_target="tpu_custom_call" | custom-call | tf_op jit(solution)/shard_map/pallas_call | solution.py:299
  105.8 5.5 %all-to-all-start.3 = ((bf16[16,4,16,512]{3,2,1,0:T(8,128)(2,1)}), bf16[16,4,16,512]{3,2,1,0:T(8,128)(2,1)S(1)}, u32[]{:S(2)}, u32[]{:S(2)}) async-start(bf16[16,4,16,512]{3,2,1,0:T(8,128)(2,1)} %shard_map.124), calls=%async_computation.3 | async-start | bytes 2097152 | tf_op jit(solution)/shard_map/all_to_all | solution.py:302
  111.4 2.1 %shard_map.129 = (bf16[672,256]{1,0:T(8,128)(2,1)}, bf16[672,256]{1,0:T(8,128)(2,1)S(1)}, bf16[672,128]{1,0:T(8,128)(2,1)S(1)}) custom-call(bf16[16,128]{1,0:T(8,128)(2,1)S(1)} %shard_map.127.before.marked, bf16[16,4,16,512]{3,2,1,0:T(8,128)(2,1)S(1)} %all-to-all-done.1.panel, bf16[16,4,16,512]{3,2,1,0:T(8,128)(2,1)S(1)} %collective-permute-done.3.other_panel, ...), custom_call_target="tpu_custom_call" | custom-call | tf_op jit(solution)/shard_map/pallas_call | solution.py:304
  113.4 8.5 %collective-permute-start.5 = (bf16[672,256]{1,0:T(8,128)(2,1)S(1)}, bf16[672,256]{1,0:T(8,128)(2,1)S(1)}, u32[]{:S(2)}, u32[]{:S(2)}) collective-permute-start(bf16[672,256]{1,0:T(8,128)(2,1)S(1)} %get-tuple-element.26), channel_id=1, source_target_pairs={{0,32},{1,65},{32,0},{33,97},{64,96},{65,1},{96,64},{97,33},{2,34}... | collective-permute-start | bytes 1032200 | tf_op jit(solution)/shard_map/ppermute | solution.py:254
  122.0 1.9 %collective-permute-start.6 = (bf16[672,128]{1,0:T(8,128)(2,1)S(1)}, bf16[672,128]{1,0:T(8,128)(2,1)S(1)}, u32[]{:S(2)}, u32[]{:S(2)}) collective-permute-start(bf16[672,128]{1,0:T(8,128)(2,1)S(1)} %get-tuple-element.27), channel_id=1, source_target_pairs={{0,96},{32,64},{64,32},{96,0},{1,97},{33,65},{65,33},{97,1},{2,98}... | collective-permute-start | bytes 516104 | tf_op jit(solution)/shard_map/ppermute | solution.py:255
  123.9 8.2 %collective-permute-done.6.part = bf16[672,128]{1,0:T(8,128)(2,1)S(1)} collective-permute-done((bf16[672,128]{1,0:T(8,128)(2,1)S(1)}, bf16[672,128]{1,0:T(8,128)(2,1)S(1)}, u32[]{:S(2)}, u32[]{:S(2)}) %collective-permute-start.6) | collective-permute-done | bytes 172064 | tf_op jit(solution)/shard_map/ppermute | solution.py:255
  132.1 1.5 collective-permute-done.5.whole
  133.6 0.1 shard_map.130
  133.6 1.9 %collective-permute-start.7 = (bf16[672,384]{1,0:T(8,128)(2,1)S(1)}, bf16[672,384]{1,0:T(8,128)(2,1)S(1)}, u32[]{:S(2)}, u32[]{:S(2)}) collective-permute-start(bf16[672,384]{1,0:T(8,128)(2,1)S(1)} %shard_map.130), channel_id=1, source_target_pairs={{0,1},{1,0},{2,3},{3,2},{4,5},{5,4},{6,7},{7,6},{8,9},{9,8},{10,11... | collective-permute-start | bytes 1548296 | tf_op jit(solution)/shard_map/ppermute | solution.py:317
  135.5 0.8 shard_map.125
  136.3 4.8 %all-to-all-start.4 = ((bf16[4,16,512]{2,1,0:T(8,128)(2,1)}), bf16[4,16,512]{2,1,0:T(8,128)(2,1)S(1)}, u32[]{:S(2)}, u32[]{:S(2)}) async-start(bf16[4,16,512]{2,1,0:T(8,128)(2,1)} %shard_map.125), calls=%async_computation.4 | async-start | bytes 131072 | tf_op jit(solution)/shard_map/all_to_all | solution.py:313
  141.2 4.7 %all-to-all-done.4.pieces = bf16[4,16,512]{2,1,0:T(8,128)(2,1)S(1)} async-done(((bf16[4,16,512]{2,1,0:T(8,128)(2,1)}), bf16[4,16,512]{2,1,0:T(8,128)(2,1)S(1)}, u32[]{:S(2)}, u32[]{:S(2)}) %all-to-all-start.4) | async-done | bytes 65568 | tf_op jit(solution)/shard_map/all_to_all | solution.py:313
  145.8 0.6 shard_map.126
  146.5 2.3 %shard_map.131 = (bf16[256,896]{1,0:T(8,128)(2,1)}, bf16[256,896]{1,0:T(8,128)(2,1)}, bf16[896,256]{1,0:T(8,128)(2,1)}) custom-call(bf16[16,128]{1,0:T(8,128)(2,1)S(1)} %shard_map.128.marked, bf16[672,256]{1,0:T(8,128)(2,1)} %get-tuple-element.25.stay, bf16[672,256]{1,0:T(8,128)(2,1)S(1)} %collective-permute-done.5.whole, ...), custom_call_target="tpu_custom_call" | custom-call | tf_op jit(solution)/shard_map/pallas_call | solution.py:319
  (10 shorter events, 0.1 us)
Async XLA Ops:
  13.3 30.5 %all-to-all-start.1 = ((bf16[16,4,16,512]{3,2,1,0:T(8,128)(2,1)}), bf16[16,4,16,512]{3,2,1,0:T(8,128)(2,1)S(1)}, u32[]{:S(2)}, u32[]{:S(2)}) async-start(bf16[16,4,16,512]{3,2,1,0:T(8,128)(2,1)} %broadcast_in_dim.5), calls=%async_computation.1 | async-start | bytes 2097152 | tf_op jit(solution)/shard_map/all_to_all | solution.py:247
  22.0 18.0 %collective-permute-start = (bf16[672,256]{1,0:T(8,128)(2,1)S(1)}, bf16[672,256]{1,0:T(8,128)(2,1)S(1)}, u32[]{:S(2)}, u32[]{:S(2)}) collective-permute-start(bf16[672,256]{1,0:T(8,128)(2,1)S(1)} %get-tuple-element.19), channel_id=1, source_target_pairs={{0,32},{1,65},{32,0},{33,97},{64,96},{65,1},{96,64},{97,33},{2,34}... | collective-permute-start | bytes 1032200 | tf_op jit(solution)/shard_map/ppermute | solution.py:254
  24.6 12.6 %collective-permute-start.1 = (bf16[672,128]{1,0:T(8,128)(2,1)S(1)}, bf16[672,128]{1,0:T(8,128)(2,1)S(1)}, u32[]{:S(2)}, u32[]{:S(2)}) collective-permute-start(bf16[672,128]{1,0:T(8,128)(2,1)S(1)} %get-tuple-element.20), channel_id=1, source_target_pairs={{0,96},{32,64},{64,32},{96,0},{1,97},{33,65},{65,33},{97,1},{2,98}... | collective-permute-start | bytes 516104 | tf_op jit(solution)/shard_map/ppermute | solution.py:255
  40.0 3.8 %collective-permute-start.2 = (bf16[672,384]{1,0:T(8,128)(2,1)S(1)}, bf16[672,384]{1,0:T(8,128)(2,1)S(1)}, u32[]{:S(2)}, u32[]{:S(2)}) collective-permute-start(bf16[672,384]{1,0:T(8,128)(2,1)S(1)} %shard_map.121), channel_id=1, source_target_pairs={{0,1},{1,0},{2,3},{3,2},{4,5},{5,4},{6,7},{7,6},{8,9},{9,8},{10,11... | collective-permute-start | bytes 1548296 | tf_op jit(solution)/shard_map/ppermute | solution.py:286
  45.4 27.2 %all-to-all-start.2 = ((bf16[4,3,56,256]{3,2,1,0:T(8,128)(2,1)}), bf16[4,3,56,256]{3,2,1,0:T(8,128)(2,1)S(1)}, u32[]{:S(2)}, u32[]{:S(2)}) async-start(bf16[4,3,56,256]{3,2,1,0:T(8,128)(2,1)} %get-tuple-element.21), calls=%async_computation.2 | async-start | bytes 688128 | tf_op jit(solution)/shard_map/all_to_all | solution.py:293
  57.5 53.9 %collective-permute-start.3 = (bf16[16,4,16,512]{3,2,1,0:T(8,128)(2,1)S(1)}, bf16[16,4,16,512]{3,2,1,0:T(8,128)(2,1)S(1)}, u32[]{:S(2)}, u32[]{:S(2)}) collective-permute-start(bf16[16,4,16,512]{3,2,1,0:T(8,128)(2,1)S(1)} %all-to-all-done.1.panel), channel_id=1, source_target_pairs={{0,1},{1,0},{2,3},{3,2},{4,5},{5,4},{6,7},{7,6},{8,9},{9,8},{10,11... | collective-permute-start | bytes 3145736 | tf_op jit(solution)/shard_map/ppermute | solution.py:294
  89.9 21.4 %collective-permute-start.4 = (bf16[4,3,56,256]{3,2,1,0:T(8,128)(2,1)S(1)}, bf16[4,3,56,256]{3,2,1,0:T(8,128)(2,1)}, u32[]{:S(2)}, u32[]{:S(2)}) collective-permute-start(bf16[4,3,56,256]{3,2,1,0:T(8,128)(2,1)S(1)} %bitcast.3), channel_id=1, source_target_pairs={{0,1},{1,0},{2,3},{3,2},{4,5},{5,4},{6,7},{7,6},{8,9},{9,8},{10,11... | collective-permute-start | bytes 1032200 | tf_op jit(solution)/shard_map/ppermute | solution.py:303
  105.8 29.7 %all-to-all-start.3 = ((bf16[16,4,16,512]{3,2,1,0:T(8,128)(2,1)}), bf16[16,4,16,512]{3,2,1,0:T(8,128)(2,1)S(1)}, u32[]{:S(2)}, u32[]{:S(2)}) async-start(bf16[16,4,16,512]{3,2,1,0:T(8,128)(2,1)} %shard_map.124), calls=%async_computation.3 | async-start | bytes 2097152 | tf_op jit(solution)/shard_map/all_to_all | solution.py:302
  113.4 20.1 %collective-permute-start.5 = (bf16[672,256]{1,0:T(8,128)(2,1)S(1)}, bf16[672,256]{1,0:T(8,128)(2,1)S(1)}, u32[]{:S(2)}, u32[]{:S(2)}) collective-permute-start(bf16[672,256]{1,0:T(8,128)(2,1)S(1)} %get-tuple-element.26), channel_id=1, source_target_pairs={{0,32},{1,65},{32,0},{33,97},{64,96},{65,1},{96,64},{97,33},{2,34}... | collective-permute-start | bytes 1032200 | tf_op jit(solution)/shard_map/ppermute | solution.py:254
  122.0 10.1 %collective-permute-start.6 = (bf16[672,128]{1,0:T(8,128)(2,1)S(1)}, bf16[672,128]{1,0:T(8,128)(2,1)S(1)}, u32[]{:S(2)}, u32[]{:S(2)}) collective-permute-start(bf16[672,128]{1,0:T(8,128)(2,1)S(1)} %get-tuple-element.27), channel_id=1, source_target_pairs={{0,96},{32,64},{64,32},{96,0},{1,97},{33,65},{65,33},{97,1},{2,98}... | collective-permute-start | bytes 516104 | tf_op jit(solution)/shard_map/ppermute | solution.py:255
  133.6 12.9 %collective-permute-start.7 = (bf16[672,384]{1,0:T(8,128)(2,1)S(1)}, bf16[672,384]{1,0:T(8,128)(2,1)S(1)}, u32[]{:S(2)}, u32[]{:S(2)}) collective-permute-start(bf16[672,384]{1,0:T(8,128)(2,1)S(1)} %shard_map.130), channel_id=1, source_target_pairs={{0,1},{1,0},{2,3},{3,2},{4,5},{5,4},{6,7},{7,6},{8,9},{9,8},{10,11... | collective-permute-start | bytes 1548296 | tf_op jit(solution)/shard_map/ppermute | solution.py:317
  136.3 9.5 %all-to-all-start.4 = ((bf16[4,16,512]{2,1,0:T(8,128)(2,1)}), bf16[4,16,512]{2,1,0:T(8,128)(2,1)S(1)}, u32[]{:S(2)}, u32[]{:S(2)}) async-start(bf16[4,16,512]{2,1,0:T(8,128)(2,1)} %shard_map.125), calls=%async_computation.4 | async-start | bytes 131072 | tf_op jit(solution)/shard_map/all_to_all | solution.py:313

commit v7 on v6

--- a/solution.py
+++ b/solution.py
@@ -288,7 +288,7 @@
     weights, partial = call(
         partial_body,
         [VMEM] * 6,
-        [outside(group, 3 * units, model), local(far, 3, piece, held)],
+        [local(group, 3 * units, model), local(far, 3, piece, held)],
     )(first_mark, panel, stay, near(whole), near(part), near(theirs))
     parts = lax.all_to_all(partial, "a", 0, 0)
     other_panel = lax.ppermute(panel, "rep", SWAP)
@@ -296,9 +296,7 @@
     (own,) = call(pointwise_body, [VMEM], [local(3, piece, held)])(near(parts))
     mid = lax.all_gather(own.reshape(3 * piece, held), "a", axis=0, tiled=True)
     mid = near(mid.reshape(far, 3, piece, held))
-    (out,) = call(outputs_body, [VMEM] * 2, [local(cols, group, block, 2 * model)])(
-        mid, distant(weights)
-    )
+    (out,) = call(outputs_body, [VMEM] * 2, [local(cols, group, block, 2 * model)])(mid, weights)
     pieces = lax.all_to_all(out, "col", 0, 0)
     other_mid = lax.ppermute(mid, "rep", SWAP)
     stay, whole, part = call(

time: 150 us -> 151 us (level)
  local copies, waits for them, and re-layouts: 1.13 us -> 3.6 us
    unnamed x0 -> x4, local copies, waits for them, and re-layouts: none -> 2.47 us
  transfers between devices with their start and end apart: 12 -> 12, of which waited for: 7 -> 7; matrix products, arithmetic and copies ran while one was open for 0% -> 0% of each run, Pallas kernels for 6% -> 5%
where the time goes in v7:
time: 151 us; the launch traced here: 150 us
  starting transfers between devices  65.7 us (44%)
  waiting for transfers between devices  39.9 us (26%)
  blocking collectives  28.1 us (19%)
  Pallas kernels  10.9 us (7%)
  local copies, waits for them, and re-layouts  3.6 us (2%)
    all_gather x1, blocking collectives, per_device(): mid = lax.all_gather(own.reshape(3 * piece, held), 'a', axis=0, tiled=True)  17.3 us
    ppermute x2, waiting for transfers between devices, exchange(): part = lax.ppermute(part, 'b', [(b, b ^ 3) for b in range(group)])  16.9 us
    ppermute x1, starting transfers between devices, per_device(): other_mid = lax.ppermute(mid, 'rep', SWAP)  13 us
    all_to_all x1, waiting for transfers between devices, per_device(): parts = lax.all_to_all(partial, 'a', 0, 0)  12.7 us
    all_to_all x1, starting transfers between devices, per_device(): parts = lax.all_to_all(partial, 'a', 0, 0)  12.1 us
    ppermute x2, starting transfers between devices, exchange(): whole = lax.ppermute(whole, ('b', 'rep'), whole_moves)  11.2 us
    all_to_all x1, blocking collectives, spread(): lax.all_to_all(jnp.broadcast_to(value[None], (count,) + value.shape), axi...  10.8 us
    all_to_all x1, starting transfers between devices, spread(): lax.all_to_all(jnp.broadcast_to(value[None], (count,) + value.shape), axi...  6.75 us
  transfers between devices with their start and end apart: 12, of which 7 were waited for; matrix products, arithmetic and copies ran while one was open for 0% of the time, Pallas kernels for 5%

profile of v7, /device:TPU:1, one launch (start us, length us, event | category | flops | bytes accessed | tf_op | source)
XLA Modules:
  0.0 149.7 jit_solution(11647514761776491506)
XLA Ops:
  0.6 0.7 pad_maximum_fusion
  1.4 10.8 %all_to_all.25 = bf16[4,16,512]{2,1,0:T(8,128)(2,1)S(1)} all-to-all(bf16[4,16,512]{2,1,0:T(8,128)(2,1)S(1)} %broadcast_in_dim.4), channel_id=1, replica_groups=mesh['a'=4,'b'=4,'col'=16,'rep'=2] {'b'}, dimensions={0} | all-to-all | bytes 131072 | tf_op jit(solution)/shard_map/all_to_all | solution.py:247
  12.2 1.1 broadcast_in_dim.5
  13.3 6.8 %all-to-all-start.1 = ((bf16[16,4,16,512]{3,2,1,0:T(8,128)(2,1)}), bf16[16,4,16,512]{3,2,1,0:T(8,128)(2,1)S(1)}, u32[]{:S(2)}, u32[]{:S(2)}) async-start(bf16[16,4,16,512]{3,2,1,0:T(8,128)(2,1)} %broadcast_in_dim.5), calls=%async_computation.1 | async-start | bytes 2097152 | tf_op jit(solution)/shard_map/all_to_all | solution.py:247
  20.1 1.9 %shard_map.120 = (bf16[672,256]{1,0:T(8,128)(2,1)S(1)}, bf16[672,256]{1,0:T(8,128)(2,1)S(1)}, bf16[672,128]{1,0:T(8,128)(2,1)S(1)}) custom-call(bf16[256,896]{1,0:T(8,128)(2,1)} %gate.1, bf16[256,896]{1,0:T(8,128)(2,1)} %up.1, bf16[896,256]{1,0:T(8,128)(2,1)} %down.1, s32[2,7]{1,0:T(2,128)} %gate_keep.3, s32[2,7]{1,0:T(2,128)} %up_keep.3, s32[2,7]{1,0:T(2,128)} %bitcast.7), custom_call_target="tpu_custom_call" | custom-call | tf_op jit(solution)/shard_map/pallas_call | solution.py:271
  22.0 2.7 %collective-permute-start = (bf16[672,256]{1,0:T(8,128)(2,1)S(1)}, bf16[672,256]{1,0:T(8,128)(2,1)S(1)}, u32[]{:S(2)}, u32[]{:S(2)}) collective-permute-start(bf16[672,256]{1,0:T(8,128)(2,1)S(1)} %get-tuple-element.19), channel_id=1, source_target_pairs={{0,32},{1,65},{32,0},{33,97},{64,96},{65,1},{96,64},{97,33},{2,34}... | collective-permute-start | bytes 1032200 | tf_op jit(solution)/shard_map/ppermute | solution.py:254
  24.7 3.9 %collective-permute-start.1 = (bf16[672,128]{1,0:T(8,128)(2,1)S(1)}, bf16[672,128]{1,0:T(8,128)(2,1)S(1)}, u32[]{:S(2)}, u32[]{:S(2)}) collective-permute-start(bf16[672,128]{1,0:T(8,128)(2,1)S(1)} %get-tuple-element.20), channel_id=1, source_target_pairs={{0,96},{32,64},{64,32},{96,0},{1,97},{33,65},{65,33},{97,1},{2,98}... | collective-permute-start | bytes 516104 | tf_op jit(solution)/shard_map/ppermute | solution.py:255
  28.5 8.7 %collective-permute-done.1.part.part_in = bf16[672,128]{1,0:T(8,128)(2,1)S(1)} collective-permute-done((bf16[672,128]{1,0:T(8,128)(2,1)S(1)}, bf16[672,128]{1,0:T(8,128)(2,1)S(1)}, u32[]{:S(2)}, u32[]{:S(2)}) %collective-permute-start.1) | collective-permute-done | bytes 172064 | tf_op jit(solution)/shard_map/ppermute | solution.py:255
  37.2 2.7 %collective-permute-done.whole = bf16[672,256]{1,0:T(8,128)(2,1)S(1)} collective-permute-done((bf16[672,256]{1,0:T(8,128)(2,1)S(1)}, bf16[672,256]{1,0:T(8,128)(2,1)S(1)}, u32[]{:S(2)}, u32[]{:S(2)}) %collective-permute-start) | collective-permute-done | bytes 344096 | tf_op jit(solution)/shard_map/ppermute | solution.py:254
  40.0 2.2 %collective-permute-start.2 = (bf16[672,384]{1,0:T(8,128)(2,1)S(1)}, bf16[672,384]{1,0:T(8,128)(2,1)S(1)}, u32[]{:S(2)}, u32[]{:S(2)}) collective-permute-start(bf16[672,384]{1,0:T(8,128)(2,1)S(1)} %shard_map.121), channel_id=1, source_target_pairs={{0,1},{1,0},{2,3},{3,2},{4,5},{5,4},{6,7},{7,6},{8,9},{9,8},{10,11... | collective-permute-start | bytes 1548296 | tf_op jit(solution)/shard_map/ppermute | solution.py:286
  42.2 1.6 %collective-permute-done.2.theirs = bf16[672,384]{1,0:T(8,128)(2,1)S(1)} collective-permute-done((bf16[672,384]{1,0:T(8,128)(2,1)S(1)}, bf16[672,384]{1,0:T(8,128)(2,1)S(1)}, u32[]{:S(2)}, u32[]{:S(2)}) %collective-permute-start.2) | collective-permute-done | bytes 516128 | tf_op jit(solution)/shard_map/ppermute | solution.py:286
  43.8 1.4 shard_map.122
  45.2 1.1 copy-done
  46.3 12.1 %all-to-all-start.2 = ((bf16[4,3,56,256]{3,2,1,0:T(8,128)(2,1)}), bf16[4,3,56,256]{3,2,1,0:T(8,128)(2,1)S(1)}, u32[]{:S(2)}, u32[]{:S(2)}) async-start(bf16[4,3,56,256]{3,2,1,0:T(8,128)(2,1)} %get-tuple-element.21), calls=%async_computation.2 | async-start | bytes 688128 | tf_op jit(solution)/shard_map/all_to_all | solution.py:293
  58.4 2.5 %collective-permute-start.3 = (bf16[16,4,16,512]{3,2,1,0:T(8,128)(2,1)S(1)}, bf16[16,4,16,512]{3,2,1,0:T(8,128)(2,1)S(1)}, u32[]{:S(2)}, u32[]{:S(2)}) collective-permute-start(bf16[16,4,16,512]{3,2,1,0:T(8,128)(2,1)S(1)} %all-to-all-done.1.panel), channel_id=1, source_target_pairs={{0,1},{1,0},{2,3},{3,2},{4,5},{5,4},{6,7},{7,6},{8,9},{9,8},{10,11... | collective-permute-start | bytes 3145736 | tf_op jit(solution)/shard_map/ppermute | solution.py:294
  60.9 12.7 %all-to-all-done.2.parts = bf16[4,3,56,256]{3,2,1,0:T(8,128)(2,1)S(1)} async-done(((bf16[4,3,56,256]{3,2,1,0:T(8,128)(2,1)}), bf16[4,3,56,256]{3,2,1,0:T(8,128)(2,1)S(1)}, u32[]{:S(2)}, u32[]{:S(2)}) %all-to-all-start.2) | async-done | bytes 344096 | tf_op jit(solution)/shard_map/all_to_all | solution.py:293
  73.6 17.3 %all_gather.3 = bf16[672,256]{1,0:T(8,128)(2,1)S(1)} all-gather(bf16[168,256]{1,0:T(8,128)(2,1)S(1)} %bitcast.6), channel_id=1, replica_groups=mesh['a'=4,'b'=4,'col'=16,'rep'=2] {'a'}, dimensions={0}, use_global_device_ids=true | all-gather | bytes 430080 | tf_op jit(solution)/shard_map/all_gather | solution.py:297
  90.9 13.0 %collective-permute-start.4 = (bf16[4,3,56,256]{3,2,1,0:T(8,128)(2,1)S(1)}, bf16[4,3,56,256]{3,2,1,0:T(8,128)(2,1)}, u32[]{:S(2)}, u32[]{:S(2)}) collective-permute-start(bf16[4,3,56,256]{3,2,1,0:T(8,128)(2,1)S(1)} %bitcast.3), channel_id=1, source_target_pairs={{0,1},{1,0},{2,3},{3,2},{4,5},{5,4},{6,7},{7,6},{8,9},{9,8},{10,11... | collective-permute-start | bytes 1032200 | tf_op jit(solution)/shard_map/ppermute | solution.py:301
  103.8 1.3 copy-done.1
  105.2 1.6 %shard_map.124 = bf16[16,4,16,512]{3,2,1,0:T(8,128)(2,1)} custom-call(bf16[4,3,56,256]{3,2,1,0:T(8,128)(2,1)S(1)} %bitcast.4, bf16[4,672,256]{2,1,0:T(8,128)(2,1)S(1)} %copy-done.1), custom_call_target="tpu_custom_call" | custom-call | tf_op jit(solution)/shard_map/pallas_call | solution.py:299
  106.8 5.4 %all-to-all-start.3 = ((bf16[16,4,16,512]{3,2,1,0:T(8,128)(2,1)}), bf16[16,4,16,512]{3,2,1,0:T(8,128)(2,1)S(1)}, u32[]{:S(2)}, u32[]{:S(2)}) async-start(bf16[16,4,16,512]{3,2,1,0:T(8,128)(2,1)} %shard_map.124), calls=%async_computation.3 | async-start | bytes 2097152 | tf_op jit(solution)/shard_map/all_to_all | solution.py:300
  112.3 2.1 %shard_map.129 = (bf16[672,256]{1,0:T(8,128)(2,1)}, bf16[672,256]{1,0:T(8,128)(2,1)S(1)}, bf16[672,128]{1,0:T(8,128)(2,1)S(1)}) custom-call(bf16[16,128]{1,0:T(8,128)(2,1)S(1)} %shard_map.127.before.marked, bf16[16,4,16,512]{3,2,1,0:T(8,128)(2,1)S(1)} %all-to-all-done.1.panel, bf16[16,4,16,512]{3,2,1,0:T(8,128)(2,1)S(1)} %collective-permute-done.3.other_panel, ...), custom_call_target="tpu_custom_call" | custom-call | tf_op jit(solution)/shard_map/pallas_call | solution.py:302
  114.3 8.6 %collective-permute-start.5 = (bf16[672,256]{1,0:T(8,128)(2,1)S(1)}, bf16[672,256]{1,0:T(8,128)(2,1)S(1)}, u32[]{:S(2)}, u32[]{:S(2)}) collective-permute-start(bf16[672,256]{1,0:T(8,128)(2,1)S(1)} %get-tuple-element.26), channel_id=1, source_target_pairs={{0,32},{1,65},{32,0},{33,97},{64,96},{65,1},{96,64},{97,33},{2,34}... | collective-permute-start | bytes 1032200 | tf_op jit(solution)/shard_map/ppermute | solution.py:254
  122.9 1.9 %collective-permute-start.6 = (bf16[672,128]{1,0:T(8,128)(2,1)S(1)}, bf16[672,128]{1,0:T(8,128)(2,1)S(1)}, u32[]{:S(2)}, u32[]{:S(2)}) collective-permute-start(bf16[672,128]{1,0:T(8,128)(2,1)S(1)} %get-tuple-element.27), channel_id=1, source_target_pairs={{0,96},{32,64},{64,32},{96,0},{1,97},{33,65},{65,33},{97,1},{2,98}... | collective-permute-start | bytes 516104 | tf_op jit(solution)/shard_map/ppermute | solution.py:255
  124.8 8.2 %collective-permute-done.6.part = bf16[672,128]{1,0:T(8,128)(2,1)S(1)} collective-permute-done((bf16[672,128]{1,0:T(8,128)(2,1)S(1)}, bf16[672,128]{1,0:T(8,128)(2,1)S(1)}, u32[]{:S(2)}, u32[]{:S(2)}) %collective-permute-start.6) | collective-permute-done | bytes 172064 | tf_op jit(solution)/shard_map/ppermute | solution.py:255
  133.0 1.4 collective-permute-done.5.whole
  134.5 1.9 %collective-permute-start.7 = (bf16[672,384]{1,0:T(8,128)(2,1)S(1)}, bf16[672,384]{1,0:T(8,128)(2,1)S(1)}, u32[]{:S(2)}, u32[]{:S(2)}) collective-permute-start(bf16[672,384]{1,0:T(8,128)(2,1)S(1)} %shard_map.130), channel_id=1, source_target_pairs={{0,1},{1,0},{2,3},{3,2},{4,5},{5,4},{6,7},{7,6},{8,9},{9,8},{10,11... | collective-permute-start | bytes 1548296 | tf_op jit(solution)/shard_map/ppermute | solution.py:315
  136.4 0.8 shard_map.125
  137.2 4.8 %all-to-all-start.4 = ((bf16[4,16,512]{2,1,0:T(8,128)(2,1)}), bf16[4,16,512]{2,1,0:T(8,128)(2,1)S(1)}, u32[]{:S(2)}, u32[]{:S(2)}) async-start(bf16[4,16,512]{2,1,0:T(8,128)(2,1)} %shard_map.125), calls=%async_computation.4 | async-start | bytes 131072 | tf_op jit(solution)/shard_map/all_to_all | solution.py:311
  142.0 4.7 %all-to-all-done.4.pieces = bf16[4,16,512]{2,1,0:T(8,128)(2,1)S(1)} async-done(((bf16[4,16,512]{2,1,0:T(8,128)(2,1)}), bf16[4,16,512]{2,1,0:T(8,128)(2,1)S(1)}, u32[]{:S(2)}, u32[]{:S(2)}) %all-to-all-start.4) | async-done | bytes 65568 | tf_op jit(solution)/shard_map/all_to_all | solution.py:311
  146.7 0.6 shard_map.126
  147.3 2.3 %shard_map.131 = (bf16[256,896]{1,0:T(8,128)(2,1)}, bf16[256,896]{1,0:T(8,128)(2,1)}, bf16[896,256]{1,0:T(8,128)(2,1)}) custom-call(bf16[16,128]{1,0:T(8,128)(2,1)S(1)} %shard_map.128.marked, bf16[672,256]{1,0:T(8,128)(2,1)} %get-tuple-element.25.stay, bf16[672,256]{1,0:T(8,128)(2,1)S(1)} %collective-permute-done.5.whole, ...), custom_call_target="tpu_custom_call" | custom-call | tf_op jit(solution)/shard_map/pallas_call | solution.py:317
  (14 shorter events, 0.2 us)
Async XLA Ops:
  13.3 30.5 %all-to-all-start.1 = ((bf16[16,4,16,512]{3,2,1,0:T(8,128)(2,1)}), bf16[16,4,16,512]{3,2,1,0:T(8,128)(2,1)S(1)}, u32[]{:S(2)}, u32[]{:S(2)}) async-start(bf16[16,4,16,512]{3,2,1,0:T(8,128)(2,1)} %broadcast_in_dim.5), calls=%async_computation.1 | async-start | bytes 2097152 | tf_op jit(solution)/shard_map/all_to_all | solution.py:247
  22.0 18.0 %collective-permute-start = (bf16[672,256]{1,0:T(8,128)(2,1)S(1)}, bf16[672,256]{1,0:T(8,128)(2,1)S(1)}, u32[]{:S(2)}, u32[]{:S(2)}) collective-permute-start(bf16[672,256]{1,0:T(8,128)(2,1)S(1)} %get-tuple-element.19), channel_id=1, source_target_pairs={{0,32},{1,65},{32,0},{33,97},{64,96},{65,1},{96,64},{97,33},{2,34}... | collective-permute-start | bytes 1032200 | tf_op jit(solution)/shard_map/ppermute | solution.py:254
  24.7 12.6 %collective-permute-start.1 = (bf16[672,128]{1,0:T(8,128)(2,1)S(1)}, bf16[672,128]{1,0:T(8,128)(2,1)S(1)}, u32[]{:S(2)}, u32[]{:S(2)}) collective-permute-start(bf16[672,128]{1,0:T(8,128)(2,1)S(1)} %get-tuple-element.20), channel_id=1, source_target_pairs={{0,96},{32,64},{64,32},{96,0},{1,97},{33,65},{65,33},{97,1},{2,98}... | collective-permute-start | bytes 516104 | tf_op jit(solution)/shard_map/ppermute | solution.py:255
  40.0 3.8 %collective-permute-start.2 = (bf16[672,384]{1,0:T(8,128)(2,1)S(1)}, bf16[672,384]{1,0:T(8,128)(2,1)S(1)}, u32[]{:S(2)}, u32[]{:S(2)}) collective-permute-start(bf16[672,384]{1,0:T(8,128)(2,1)S(1)} %shard_map.121), channel_id=1, source_target_pairs={{0,1},{1,0},{2,3},{3,2},{4,5},{5,4},{6,7},{7,6},{8,9},{9,8},{10,11... | collective-permute-start | bytes 1548296 | tf_op jit(solution)/shard_map/ppermute | solution.py:286
  45.2 1.1 copy-start
  46.3 27.2 %all-to-all-start.2 = ((bf16[4,3,56,256]{3,2,1,0:T(8,128)(2,1)}), bf16[4,3,56,256]{3,2,1,0:T(8,128)(2,1)S(1)}, u32[]{:S(2)}, u32[]{:S(2)}) async-start(bf16[4,3,56,256]{3,2,1,0:T(8,128)(2,1)} %get-tuple-element.21), calls=%async_computation.2 | async-start | bytes 688128 | tf_op jit(solution)/shard_map/all_to_all | solution.py:293
  58.4 53.8 %collective-permute-start.3 = (bf16[16,4,16,512]{3,2,1,0:T(8,128)(2,1)S(1)}, bf16[16,4,16,512]{3,2,1,0:T(8,128)(2,1)S(1)}, u32[]{:S(2)}, u32[]{:S(2)}) collective-permute-start(bf16[16,4,16,512]{3,2,1,0:T(8,128)(2,1)S(1)} %all-to-all-done.1.panel), channel_id=1, source_target_pairs={{0,1},{1,0},{2,3},{3,2},{4,5},{5,4},{6,7},{7,6},{8,9},{9,8},{10,11... | collective-permute-start | bytes 3145736 | tf_op jit(solution)/shard_map/ppermute | solution.py:294
  90.9 21.4 %collective-permute-start.4 = (bf16[4,3,56,256]{3,2,1,0:T(8,128)(2,1)S(1)}, bf16[4,3,56,256]{3,2,1,0:T(8,128)(2,1)}, u32[]{:S(2)}, u32[]{:S(2)}) collective-permute-start(bf16[4,3,56,256]{3,2,1,0:T(8,128)(2,1)S(1)} %bitcast.3), channel_id=1, source_target_pairs={{0,1},{1,0},{2,3},{3,2},{4,5},{5,4},{6,7},{7,6},{8,9},{9,8},{10,11... | collective-permute-start | bytes 1032200 | tf_op jit(solution)/shard_map/ppermute | solution.py:301
  103.8 1.3 copy-start.1
  106.8 29.6 %all-to-all-start.3 = ((bf16[16,4,16,512]{3,2,1,0:T(8,128)(2,1)}), bf16[16,4,16,512]{3,2,1,0:T(8,128)(2,1)S(1)}, u32[]{:S(2)}, u32[]{:S(2)}) async-start(bf16[16,4,16,512]{3,2,1,0:T(8,128)(2,1)} %shard_map.124), calls=%async_computation.3 | async-start | bytes 2097152 | tf_op jit(solution)/shard_map/all_to_all | solution.py:300
  114.3 20.1 %collective-permute-start.5 = (bf16[672,256]{1,0:T(8,128)(2,1)S(1)}, bf16[672,256]{1,0:T(8,128)(2,1)S(1)}, u32[]{:S(2)}, u32[]{:S(2)}) collective-permute-start(bf16[672,256]{1,0:T(8,128)(2,1)S(1)} %get-tuple-element.26), channel_id=1, source_target_pairs={{0,32},{1,65},{32,0},{33,97},{64,96},{65,1},{96,64},{97,33},{2,34}... | collective-permute-start | bytes 1032200 | tf_op jit(solution)/shard_map/ppermute | solution.py:254
  122.9 10.1 %collective-permute-start.6 = (bf16[672,128]{1,0:T(8,128)(2,1)S(1)}, bf16[672,128]{1,0:T(8,128)(2,1)S(1)}, u32[]{:S(2)}, u32[]{:S(2)}) collective-permute-start(bf16[672,128]{1,0:T(8,128)(2,1)S(1)} %get-tuple-element.27), channel_id=1, source_target_pairs={{0,96},{32,64},{64,32},{96,0},{1,97},{33,65},{65,33},{97,1},{2,98}... | collective-permute-start | bytes 516104 | tf_op jit(solution)/shard_map/ppermute | solution.py:255
  134.5 12.8 %collective-permute-start.7 = (bf16[672,384]{1,0:T(8,128)(2,1)S(1)}, bf16[672,384]{1,0:T(8,128)(2,1)S(1)}, u32[]{:S(2)}, u32[]{:S(2)}) collective-permute-start(bf16[672,384]{1,0:T(8,128)(2,1)S(1)} %shard_map.130), channel_id=1, source_target_pairs={{0,1},{1,0},{2,3},{3,2},{4,5},{5,4},{6,7},{7,6},{8,9},{9,8},{10,11... | collective-permute-start | bytes 1548296 | tf_op jit(solution)/shard_map/ppermute | solution.py:315
  137.2 9.5 %all-to-all-start.4 = ((bf16[4,16,512]{2,1,0:T(8,128)(2,1)}), bf16[4,16,512]{2,1,0:T(8,128)(2,1)S(1)}, u32[]{:S(2)}, u32[]{:S(2)}) async-start(bf16[4,16,512]{2,1,0:T(8,128)(2,1)} %shard_map.125), calls=%async_computation.4 | async-start | bytes 131072 | tf_op jit(solution)/shard_map/all_to_all | solution.py:311
